TPU v7x, 32 devices: a whole 2x2x4 slice. The times are simulated.
32 devices in a mesh: dp: 2 (over y), tile: 4 (over z), replica: 4 (over x, core).
Axes of the slice: x: 2, y: 2, z: 4, core: 2. Of those that a mesh axis runs over, the one named last changes fastest.
Arguments:
- tokens: bfloat16 [128, 8192], P(('tile', 'replica'), 'dp'), may hold values from -6 to 6
- out_grad: bfloat16 [128, 8192], P(('tile', 'replica'), 'dp'), may hold values from -3 to 3
- gate_blocks: bfloat16 [2, 4, 384, 128, 128], P('dp', 'tile'), may hold values from -0.125 to 0.125
- up_blocks: bfloat16 [2, 4, 384, 128, 128], P('dp', 'tile'), may hold values from -0.125 to 0.125
- down_blocks: bfloat16 [2, 4, 384, 128, 128], P('dp', 'tile'), may hold values from -0.09375 to 0.09375
- gate_ids: int32 [2, 4, 384], P('dp', 'tile'), may hold values from 0 to 896, as said below
- up_ids: int32 [2, 4, 384], P('dp', 'tile'), may hold values from 0 to 896, as said below
- down_ids: int32 [2, 4, 384], P('dp', 'tile'), may hold values from 0 to 896, as said below
Outputs:
- output: bfloat16 [128, 8192], P(('tile', 'replica'), 'dp')
- input_grad: bfloat16 [128, 8192], P(('tile', 'replica'), 'dp')
- gate_grad: bfloat16 [2, 4, 384, 128, 128], P('dp', 'tile')
- up_grad: bfloat16 [2, 4, 384, 128, 128], P('dp', 'tile')
- down_grad: bfloat16 [2, 4, 384, 128, 128], P('dp', 'tile')
Inputs may be any that keep to these rules, and one draw needn't show every extreme that they name: `gate_ids`: entry s for device (d, t) names a kept block of its 32 x 28 grid as row * 28 + column, each block at most once for a device; the value 896 marks an empty slot. Every device keeps 64 to 384 blocks; in every draw some device fills all 384 slots and another keeps 64 blocks. `up_ids`: as for gate_ids, drawn apart. `down_ids`: as for gate_ids, drawn apart; the row names a model-width block, the column a hidden-unit block.
All inputs are finite; a program needn't handle non-finite values.
Results may differ from a plain program's by a relative error of at most 0.017.
Values may be sent and summed in bfloat16 or wider, within the bound.
No kernel may reach another device: no remote copies, remote signals or barrier semaphores. Data moves between devices by JAX's collectives and lax.ppermute only.
A program may use at most 256 MiB of HBM per device.

v0:
```python
import jax
import jax.numpy as jnp
from jax import lax
from jax.sharding import PartitionSpec as P

FF = 14336


def block_slots(slot_ids, row_count, col_count):
    present = slot_ids < row_count * col_count
    row_index = jnp.where(present, slot_ids // col_count, row_count)
    col_index = jnp.where(present, slot_ids % col_count, col_count)
    return (row_index, col_index)


def select_blocks(matrix, index, block_count, block_size):
    blocked = matrix.reshape(matrix.shape[0], block_count, block_size)
    return jnp.take(blocked, index, axis=1, mode="fill", fill_value=0)


def place_blocks(product, index, block_count, block_size):
    placed = jnp.zeros((product.shape[0], block_count, block_size), jnp.float32)
    placed = placed.at[:, index, :].add(product, mode="drop")
    return placed.reshape(product.shape[0], block_count * block_size)


def on_device(tokens, out_grad, gate_blocks, up_blocks, down_blocks, gate_ids, up_ids, down_ids):
    gate_local = gate_blocks[0, 0]
    up_local = up_blocks[0, 0]
    down_local = down_blocks[0, 0]
    block_size = gate_local.shape[-1]
    token_rows, grad_rows = (
        lax.all_gather(tokens, "tile", axis=0, tiled=True),
        lax.all_gather(out_grad, "tile", axis=0, tiled=True),
    )
    row_count = token_rows.shape[1] // block_size
    hidden_width = FF // lax.axis_size("tile")
    col_count = hidden_width // block_size
    gate_rowslot, gate_colslot = block_slots(gate_ids[0, 0], row_count, col_count)
    up_rowslot, up_colslot = block_slots(up_ids[0, 0], row_count, col_count)
    down_rowslot, down_colslot = block_slots(down_ids[0, 0], row_count, col_count)
    gate_input = select_blocks(token_rows, gate_rowslot, row_count, block_size)
    up_input = select_blocks(token_rows, up_rowslot, row_count, block_size)
    gate_piece = gate_input
    up_piece = up_input
    gate_product = jnp.einsum(
        "tsk,skf->tsf", gate_piece, gate_local, preferred_element_type=jnp.float32
    )
    up_product = jnp.einsum("tsk,skf->tsf", up_piece, up_local, preferred_element_type=jnp.float32)
    gate_up = lax.psum_scatter(
        jnp.concatenate(
            [
                place_blocks(gate_product, gate_colslot, col_count, block_size),
                place_blocks(up_product, up_colslot, col_count, block_size),
            ],
            axis=1,
        ).astype(jnp.bfloat16),
        "dp",
        scatter_dimension=0,
        tiled=True,
    ).astype(jnp.float32)
    gate_sum = gate_up[:, :hidden_width]
    up_sum = gate_up[:, hidden_width:]
    sigmoid = jax.nn.sigmoid(gate_sum)
    silu_gate = gate_sum * sigmoid
    hidden = (silu_gate * up_sum).astype(jnp.bfloat16)
    hidden_rows = lax.all_gather(hidden, "dp", axis=0, tiled=True)
    hidden_picked = select_blocks(hidden_rows, down_colslot, col_count, block_size)
    grad_picked = select_blocks(grad_rows, down_rowslot, row_count, block_size)
    down_product = jnp.einsum(
        "tsf,sfk->tsk", hidden_picked, down_local, preferred_element_type=jnp.float32
    )
    output = lax.psum_scatter(
        place_blocks(down_product, down_rowslot, row_count, block_size).astype(jnp.bfloat16),
        "tile",
        scatter_dimension=0,
        tiled=True,
    )
    down_part = jnp.einsum(
        "tsf,tsk->sfk", hidden_picked, grad_picked, preferred_element_type=jnp.float32
    )
    back_product = jnp.einsum(
        "tsk,sfk->tsf", grad_picked, down_local, preferred_element_type=jnp.float32
    )
    hidden_grad = lax.psum_scatter(
        place_blocks(back_product, down_colslot, col_count, block_size).astype(jnp.bfloat16),
        "dp",
        scatter_dimension=0,
        tiled=True,
    ).astype(jnp.float32)
    gate_act_grad = (hidden_grad * up_sum * sigmoid * (1.0 + gate_sum * (1.0 - sigmoid))).astype(
        jnp.bfloat16
    )
    up_act_grad = (hidden_grad * silu_gate).astype(jnp.bfloat16)
    gate_grad_rows, up_grad_rows = (
        lax.all_gather(gate_act_grad, "dp", axis=0, tiled=True),
        lax.all_gather(up_act_grad, "dp", axis=0, tiled=True),
    )
    gate_grad_picked = select_blocks(gate_grad_rows, gate_colslot, col_count, block_size)
    up_grad_picked = select_blocks(up_grad_rows, up_colslot, col_count, block_size)
    gate_piece = gate_grad_picked
    up_piece = up_grad_picked
    gate_product = jnp.einsum(
        "tsf,skf->tsk", gate_piece, gate_local, preferred_element_type=jnp.float32
    )
    up_product = jnp.einsum("tsf,skf->tsk", up_piece, up_local, preferred_element_type=jnp.float32)
    input_grad = lax.psum_scatter(
        (
            place_blocks(gate_product, gate_rowslot, row_count, block_size)
            + place_blocks(up_product, up_rowslot, row_count, block_size)
        ).astype(jnp.bfloat16),
        "tile",
        scatter_dimension=0,
        tiled=True,
    )
    gate_part = jnp.einsum(
        "tsk,tsf->skf", gate_input, gate_grad_picked, preferred_element_type=jnp.float32
    )
    up_part = jnp.einsum(
        "tsk,tsf->skf", up_input, up_grad_picked, preferred_element_type=jnp.float32
    )
    gate_weight_grad, up_weight_grad, down_weight_grad = (
        lax.psum(gate_part.astype(jnp.bfloat16), "replica").astype(jnp.float32),
        lax.psum(up_part.astype(jnp.bfloat16), "replica").astype(jnp.float32),
        lax.psum(down_part.astype(jnp.bfloat16), "replica").astype(jnp.float32),
    )
    return (
        output,
        input_grad,
        gate_weight_grad.astype(jnp.bfloat16)[None, None],
        up_weight_grad.astype(jnp.bfloat16)[None, None],
        down_weight_grad.astype(jnp.bfloat16)[None, None],
    )


def solution(mesh):
    return jax.shard_map(
        on_device,
        mesh=mesh,
        in_specs=(
            P(("tile", "replica"), "dp"),
            P(("tile", "replica"), "dp"),
            P("dp", "tile", None, None, None),
            P("dp", "tile", None, None, None),
            P("dp", "tile", None, None, None),
            P("dp", "tile", None),
            P("dp", "tile", None),
            P("dp", "tile", None),
        ),
        out_specs=(
            P(("tile", "replica"), "dp"),
            P(("tile", "replica"), "dp"),
            P("dp", "tile", None, None, None),
            P("dp", "tile", None, None, None),
            P("dp", "tile", None, None, None),
        ),
        check_vma=False,
    )
```

profile of v0, /device:TPU:0, one launch (start us, length us, event | category | flops | bytes accessed | tf_op | source)
XLA Modules:
  0.0 1076.8 jit_solution(11249457878538878458)
XLA Ops:
  11.6 15.8 %all_gather.15 = bf16[32,4096]{1,0:T(8,128)(2,1)S(1)} all-gather(bf16[8,4096]{1,0:T(8,128)(2,1)} %param.12), channel_id=1, replica_groups=mesh['dp'=2,'tile'=4,'replica'=4] {'tile'}, dimensions={0}, use_global_device_ids=true | all-gather | bytes 327680 | tf_op jit(solution)/shard_map/all_gather | solution.py:33
  27.5 3.2 gather_fusion.1
  30.6 2.4 gather_fusion
  33.1 9.2 fusion.10
  42.4 34.6 %scatter_fusion = f32[32,28,128]{2,0,1:T(8,128)S(1)} fusion(f32[32,28,128]{2,0,1:T(8,128)S(1)} %broadcast.390.clone.2, s32[384]{0:T(512)S(1)} %get-tuple-element.14, f32[384,32,128]{2,1,0:T(8,128)} %fusion.10), kind=kCustom, calls=%fused_computation.6 | custom fusion | flops 1572864 | bytes 18875904 | tf_op jit(solution)/shard_map/scatter-add | solution.py:23
  77.0 11.7 %fusion.6 = f32[384,32,128]{2,1,0:T(8,128)} fusion(bf16[1,1,384,128,128]{4,3,2,1,0:T(8,128)(2,1)} %param.15, bf16[384,32,128]{2,1,0:T(8,128)(2,1)} %gather_fusion.1, pred[384]{0:T(512)(128)(4,1)S(1)} %get-tuple-element.43), kind=kOutput, calls=%fused_computation.18 | convolution fusion | flops 404226048 | bytes 22020480 | tf_op jit(solution)/shard_map/tsk,skf->tsf/dot_general | solution.py:49
  88.7 34.7 %scatter_fusion.1 = f32[32,28,128]{2,0,1:T(8,128)S(1)} fusion(f32[32,28,128]{2,0,1:T(8,128)S(1)} %broadcast.390.clone.1, s32[384]{0:T(512)S(1)} %get-tuple-element.8, f32[384,32,128]{2,1,0:T(8,128)} %fusion.6), kind=kCustom, calls=%fused_computation.7 | custom fusion | flops 1572864 | bytes 18875904 | tf_op jit(solution)/shard_map/scatter-add | solution.py:23
  124.4 14.5 %all_gather.17 = bf16[32,4096]{1,0:T(8,128)(2,1)S(1)} all-gather(bf16[8,4096]{1,0:T(8,128)(2,1)S(1)} %copy-done.6), channel_id=1, replica_groups=mesh['dp'=2,'tile'=4,'replica'=4] {'tile'}, dimensions={0}, use_global_device_ids=true | all-gather | bytes 327680 | tf_op jit(solution)/shard_map/all_gather | solution.py:34
  139.0 2.4 gather_fusion.3
  141.4 12.5 %fusion = f32[384,32,128]{2,1,0:T(8,128)} fusion(bf16[1,1,384,128,128]{4,3,2,1,0:T(8,128)(2,1)} %param.16, bf16[384,32,128]{2,1,0:T(8,128)(2,1)S(1)} %gather_fusion.3, pred[384]{0:T(512)(128)(4,1)S(1)} %get-tuple-element.26), kind=kOutput, calls=%fused_computation.12 | convolution fusion | flops 404226048 | bytes 22020480 | tf_op jit(solution)/shard_map/tsk,sfk->tsf/dot_general | solution.py:82
  154.0 34.4 %scatter_fusion.3 = f32[32,28,128]{2,0,1:T(8,128)S(1)} fusion(f32[32,28,128]{2,0,1:T(8,128)S(1)} %broadcast.390.clone, s32[384]{0:T(512)S(1)} %get-tuple-element.11, f32[384,32,128]{2,1,0:T(8,128)} %fusion), kind=kCustom, calls=%fused_computation.9 | custom fusion | flops 1572864 | bytes 18875904 | tf_op jit(solution)/shard_map/scatter-add | solution.py:23
  190.3 11.6 %reduce-scatter.9.cloned.1.call-done = bf16[16,3584]{1,0:T(8,128)(2,1)} async-done(((bf16[32,3584]{1,0:T(8,128)(2,1)}), bf16[16,3584]{1,0:T(8,128)(2,1)}) %reduce-scatter.9.cloned.1.call-update) | async-done | bytes 114704 | tf_op jit(solution)/shard_map/reduce_scatter | solution.py:85
  202.9 5.6 all_gather.19
  208.5 3.2 gather_fusion.5
  211.7 15.1 %fusion.4 = f32[384,32,128]{2,1,0:T(8,128)} fusion(bf16[1,1,384,128,128]{4,3,2,1,0:T(8,128)(2,1)} %param.15, bf16[384,32,128]{2,1,0:T(8,128)(2,1)} %gather_fusion.5, pred[384]{0:T(512)(128)(4,1)S(1)} %get-tuple-element.22), kind=kOutput, calls=%fused_computation.16 | convolution fusion | flops 404226048 | bytes 22020480 | tf_op jit(solution)/shard_map/tsf,skf->tsk/dot_general | solution.py:106
  226.8 9.8 convert_bitcast_fusion.1
  236.6 5.5 all_gather.18
  242.1 5.7 all_gather.16
  247.8 3.2 gather_fusion.4
  251.0 14.9 %fusion.8 = f32[384,32,128]{2,1,0:T(8,128)} fusion(bf16[1,1,384,128,128]{4,3,2,1,0:T(8,128)(2,1)} %param.14, bf16[384,32,128]{2,1,0:T(8,128)(2,1)} %gather_fusion.4, pred[384]{0:T(512)(128)(4,1)S(1)} %get-tuple-element.24), kind=kOutput, calls=%fused_computation.20 | convolution fusion | flops 404226048 | bytes 22020480 | tf_op jit(solution)/shard_map/tsf,skf->tsk/dot_general | solution.py:103
  266.0 34.7 %scatter_fusion.5 = f32[32,32,128]{2,0,1:T(8,128)S(1)} fusion(f32[32,32,128]{2,0,1:T(8,128)S(1)} %broadcast.388.clone.2, s32[384]{0:T(512)S(1)} %get-tuple-element.7, f32[384,32,128]{2,1,0:T(8,128)} %fusion.4), kind=kCustom, calls=%fused_computation.11 | custom fusion | flops 1572864 | bytes 18875904 | tf_op jit(solution)/shard_map/scatter-add | solution.py:23
  300.8 34.5 %scatter_fusion.4 = f32[32,32,128]{2,0,1:T(8,128)S(1)} fusion(f32[32,32,128]{2,0,1:T(8,128)S(1)} %broadcast.388.clone.1, s32[384]{0:T(512)S(1)} %get-tuple-element.13, f32[384,32,128]{2,1,0:T(8,128)} %fusion.8), kind=kCustom, calls=%fused_computation.10 | custom fusion | flops 1572864 | bytes 18875904 | tf_op jit(solution)/shard_map/scatter-add | solution.py:23
  336.4 2.4 gather_fusion.2
  338.8 9.3 fusion.2
  348.2 34.4 %scatter_fusion.2 = f32[32,32,128]{2,0,1:T(8,128)S(1)} fusion(f32[32,32,128]{2,0,1:T(8,128)S(1)} %broadcast.388.clone, s32[384]{0:T(512)S(1)} %get-tuple-element.12, f32[384,32,128]{2,1,0:T(8,128)} %fusion.2), kind=kCustom, calls=%fused_computation.8 | custom fusion | flops 1572864 | bytes 18875904 | tf_op jit(solution)/shard_map/scatter-add | solution.py:23
  383.3 10.4 convert_bitcast_fusion.2
  393.8 9.8 convert_bitcast_fusion
  403.7 10.1 reduce-scatter.7.cloned.1.call-done
  413.8 630.0 %all-reduce.3.cloned.1.call-done = (bf16[1,1,384,128,128]{4,3,2,1,0:T(8,128)(2,1)}, bf16[1,1,384,128,128]{4,3,2,1,0:T(8,128)(2,1)}, bf16[1,1,384,128,128]{4,3,2,1,0:T(8,128)(2,1)}) async-done(((bf16[1,1,384,128,128]{4,3,2,1,0:T(8,128)(2,1)}, bf16[1,1,384,128,128]{4,3,2,1,0:T(8,128)(2,1)}, bf16[1,1,384,128,128]{4,3,2,1,0:T(8,128)(2,1)}), (bf16[1,1,384,128,128]{4,3,2,1,0:T(8,128)(2,1)}, ...) | async-done | bytes 37748752 | tf_op jit(solution)/shard_map/psum | solution.py:123
  1043.8 12.6 %copy.61 = bf16[1,1,384,128,128]{4,3,2,1,0:T(8,128)(2,1)} copy(bf16[1,1,384,128,128]{4,3,2,1,0:T(8,128)(2,1)} %get-tuple-element.57) | data formatting | bytes 25165824
  1056.4 6.4 copy.62
  1065.0 4.8 copy.63
  (71 shorter events, 12.8 us)
Async XLA Ops:
  7.2 182.1 %reduce-scatter.5.cloned.1.call-start = ((), (), s32[]{:S(2)}) async-start(), calls=%async_computation.4 | async-start | bytes 688128 | tf_op jit(solution)/shard_map/reduce_scatter | solution.py:50
  33.1 9.2 copy-start
  88.7 35.6 %copy-start.7 = (s32[1,1,384]{2,1,0:T(1,128)S(1)}, s32[1,1,384]{2,1,0:T(1,128)}, u32[]{:S(2)}) copy-start(s32[1,1,384]{2,1,0:T(1,128)} %param.19) | copy-start | bytes 4612
  88.7 35.7 %copy-start.6 = (bf16[8,4096]{1,0:T(8,128)(2,1)S(1)}, bf16[8,4096]{1,0:T(8,128)(2,1)}, u32[]{:S(2)}) copy-start(bf16[8,4096]{1,0:T(8,128)(2,1)} %param.13) | copy-start | bytes 196612
  124.3 77.6 %reduce-scatter.9.cloned.1.call-start = ((), (), s32[]{:S(2)}) async-start(), calls=%async_computation.6 | async-start | bytes 344064 | tf_op jit(solution)/shard_map/reduce_scatter | solution.py:85
  141.4 12.5 %copy-start.4 = (bf16[384,32,128]{2,1,0:T(8,128)(2,1)}, bf16[384,32,128]{2,1,0:T(8,128)(2,1)S(1)}, u32[]{:S(2)}) copy-start(bf16[384,32,128]{2,1,0:T(8,128)(2,1)S(1)} %gather_fusion.3) | copy-start | bytes 9437188
  189.2 214.5 %reduce-scatter.11.cloned.1.call-start = ((), (), s32[]{:S(2)}) async-start(), calls=%async_computation.7 | async-start | bytes 327680 | tf_op jit(solution)/shard_map/reduce_scatter | solution.py:107
  211.7 15.1 %copy-start.1 = (bf16[384,32,128]{2,1,0:T(8,128)(2,1)S(1)}, bf16[384,32,128]{2,1,0:T(8,128)(2,1)}, u32[]{:S(2)}) copy-start(bf16[384,32,128]{2,1,0:T(8,128)(2,1)} %gather_fusion.1) | copy-start | bytes 9437188
  336.1 77.8 %reduce-scatter.7.cloned.1.call-start = ((), (), s32[]{:S(2)}) async-start(), calls=%async_computation.5 | async-start | bytes 327680 | tf_op jit(solution)/shard_map/reduce_scatter | solution.py:73
  338.8 9.3 copy-start.2
  383.3 10.5 copy-start.3
  393.8 650.0 %all-reduce.3.cloned.1.call-start = ((), (), s32[]{:S(2)}) async-start(), calls=%async_computation.8 | async-start | bytes 75497472 | tf_op jit(solution)/shard_map/psum | solution.py:123
  1043.8 12.6 %copy-start.5 = (bf16[1,1,384,128,128]{4,3,2,1,0:T(8,128)(2,1)S(1)}, bf16[1,1,384,128,128]{4,3,2,1,0:T(8,128)(2,1)}, u32[]{:S(2)}) copy-start(bf16[1,1,384,128,128]{4,3,2,1,0:T(8,128)(2,1)} %get-tuple-element.58) | copy-start | bytes 37748740
  1043.8 19.0 %slice-start = ((s8[12582912]{0:T(1024)(128)(4,1)}), s8[4194304]{0:T(1024)(128)(4,1)S(1)}, s32[]{:S(2)}) async-start(s8[12582912]{0:T(1024)(128)(4,1)} %bitcast.173), calls=%async_computation.9 | async-start | bytes 8388608
  1043.8 19.5 %slice-start.1 = ((s8[12582912]{0:T(1024)(128)(4,1)}), s8[4194304]{0:T(1024)(128)(4,1)S(1)}, s32[]{:S(2)}) async-start(s8[12582912]{0:T(1024)(128)(4,1)} %bitcast.173), calls=%async_computation.10 | async-start | bytes 8388608
  1056.4 8.6 slice-start.2
Sparse Core Ops, SparseCore 0:
  124.4 15.4 reduce-scatter.4
  189.3 12.5 reduce-scatter.8
  336.2 19.7 reduce-scatter.10
  393.9 19.8 reduce-scatter.6
  417.4 626.3 all-reduce.2
where the time goes:
time: 1090 us; the launch traced here: 1080 us
  waiting for transfers between devices  652 us (60%)
  other arithmetic  217 us (20%)
  matrix products  103 us (9%)
  blocking collectives  47 us (4%)
  local copies, waits for them, and re-layouts  43.4 us (4%)
  between operations  14.5 us (1%)
    psum x1, waiting for transfers between devices, on_device(): lax.psum(gate_part.astype(jnp.bfloat16), 'replica').astype(jnp.float32)  630 us
    scatter-add x6, other arithmetic, place_blocks(): placed = placed.at[:, index, :].add(product, mode='drop')  207 us
    unnamed x25, local copies, waits for them, and re-layouts  26 us
  transfers between devices with their start and end apart: 5, of which 3 were waited for; matrix products, arithmetic and copies ran while one was open for 11% of the time, Pallas kernels for 0%

commit v1 on v0

v1 whole, which is shorter than its diff:
```python
import functools

import jax
import jax.numpy as jnp
from jax import lax
from jax.experimental import pallas as pl
from jax.experimental.pallas import tpu as pltpu
from jax.sharding import PartitionSpec as P

FF = 14336
SLOTS_PER_STEP = 32
VMEM_LIMIT = 56 << 20


def divisor_up_to(count, limit):
    return max(step for step in range(1, limit + 1) if count % step == 0)


def row_of(slot_id, row_count, col_count):
    factor = -(-(1 << 16) // col_count)
    assert all((i * factor) >> 16 == i // col_count for i in range(row_count * col_count + 1))
    return (slot_id * factor) >> 16


def resident(shape):
    return pl.BlockSpec(shape, lambda step, *ids: (0,) * len(shape))


def stepped(slots, block):
    return pl.BlockSpec((1, 1, slots, block, block), lambda step, *ids: (0, 0, step, 0, 0))


def place(row_count, col_count, ids_ref, step, slots, slot):
    slot_id = ids_ref[step * slots + slot]
    row = row_of(slot_id, row_count, col_count)
    return row, slot_id - row * col_count


def to_hidden_kernel(count, pieces, row_count, col_count, slots, transposed, *refs):
    ids = refs[:count]
    parts = refs[count : count + pieces]
    blocks = refs[count + pieces : 2 * count + pieces]
    sums_out = refs[2 * count + pieces : 3 * count + pieces]
    rows_out = refs[3 * count + pieces]
    source = refs[3 * count + pieces + 1]
    sums = refs[3 * count + pieces + 2 :]
    step = pl.program_id(0)
    block = source.shape[-1]

    @pl.when(step == 0)
    def _():
        for row in range(row_count):
            columns = slice(row * block, (row + 1) * block)
            source[row] = jnp.concatenate([part[:, columns] for part in parts], axis=0)
        source[row_count] = jnp.zeros(source.shape[1:], source.dtype)
        rows_out[...] = source[:row_count]
        for total in sums:
            total[...] = jnp.zeros(total.shape, total.dtype)

    for slot in range(slots):
        for ids_ref, blocks_ref, total in zip(ids, blocks, sums):
            row, col = place(row_count, col_count, ids_ref, step, slots, slot)
            total[col] += lax.dot_general(
                source[row],
                blocks_ref[0, 0, slot],
                (((1,), (1 if transposed else 0,)), ((), ())),
                preferred_element_type=jnp.float32,
            )

    @pl.when(step == pl.num_programs(0) - 1)
    def _():
        for out, total in zip(sums_out, sums):
            out[...] = total[...].astype(out.dtype)


def to_hidden(parts, blocks, ids, row_count, col_count, transposed):
    count, pieces = len(ids), len(parts)
    slot_count, block = blocks[0].shape[2], blocks[0].shape[-1]
    slots = divisor_up_to(slot_count, SLOTS_PER_STEP)
    tokens = sum(part.shape[0] for part in parts)
    sums = jax.ShapeDtypeStruct((col_count, tokens, block), jnp.bfloat16)
    rows = jax.ShapeDtypeStruct((row_count, tokens, block), jnp.bfloat16)
    return pl.pallas_call(
        functools.partial(to_hidden_kernel, count, pieces, row_count, col_count, slots, transposed),
        out_shape=[sums] * count + [rows],
        grid_spec=pltpu.PrefetchScalarGridSpec(
            num_scalar_prefetch=count,
            grid=(slot_count // slots,),
            in_specs=[resident(part.shape) for part in parts] + [stepped(slots, block)] * count,
            out_specs=[resident(sums.shape)] * count + [resident(rows.shape)],
            scratch_shapes=[pltpu.VMEM((row_count + 1, tokens, block), jnp.bfloat16)]
            + [pltpu.VMEM(sums.shape, jnp.float32)] * count,
        ),
        compiler_params=pltpu.CompilerParams(
            dimension_semantics=("arbitrary",), vmem_limit_bytes=VMEM_LIMIT
        ),
        cost_estimate=pl.CostEstimate(
            flops=2 * count * slot_count * tokens * block * block,
            bytes_accessed=2 * count * slot_count * block * block,
            transcendentals=0,
        ),
    )(*ids, *parts, *blocks)


def to_model_kernel(count, pieces, row_count, col_count, slots, transposed, *refs):
    ids = refs[:count]
    sources = refs[count : 2 * count]
    blocks = refs[2 * count : 3 * count]
    outs = refs[3 * count : 3 * count + pieces]
    total = refs[3 * count + pieces]
    step = pl.program_id(0)
    block = total.shape[-1]

    @pl.when(step == 0)
    def _():
        total[...] = jnp.zeros(total.shape, total.dtype)

    for slot in range(slots):
        for ids_ref, source, blocks_ref in zip(ids, sources, blocks):
            row, col = place(row_count, col_count, ids_ref, step, slots, slot)
            total[row] += lax.dot_general(
                source[col],
                blocks_ref[0, 0, slot],
                (((1,), (1 if transposed else 0,)), ((), ())),
                preferred_element_type=jnp.float32,
            )

    @pl.when(step == pl.num_programs(0) - 1)
    def _():
        for piece, out in enumerate(outs):
            height = out.shape[0]
            for row in range(row_count):
                out[:, row * block : (row + 1) * block] = total[
                    row, piece * height : (piece + 1) * height
                ].astype(out.dtype)


def to_model(sources, blocks, ids, row_count, col_count, pieces, transposed):
    count = len(ids)
    slot_count, block = blocks[0].shape[2], blocks[0].shape[-1]
    slots = divisor_up_to(slot_count, SLOTS_PER_STEP)
    tokens = sources[0].shape[1]
    out = jax.ShapeDtypeStruct((tokens // pieces, row_count * block), jnp.bfloat16)
    return pl.pallas_call(
        functools.partial(to_model_kernel, count, pieces, row_count, col_count, slots, transposed),
        out_shape=[out] * pieces,
        grid_spec=pltpu.PrefetchScalarGridSpec(
            num_scalar_prefetch=count,
            grid=(slot_count // slots,),
            in_specs=[resident(source.shape) for source in sources]
            + [stepped(slots, block)] * count,
            out_specs=[resident(out.shape)] * pieces,
            scratch_shapes=[pltpu.VMEM((row_count + 1, tokens, block), jnp.float32)],
        ),
        compiler_params=pltpu.CompilerParams(
            dimension_semantics=("arbitrary",), vmem_limit_bytes=VMEM_LIMIT
        ),
        cost_estimate=pl.CostEstimate(
            flops=2 * count * slot_count * tokens * block * block,
            bytes_accessed=2 * count * slot_count * block * block,
            transcendentals=0,
        ),
    )(*ids, *sources, *blocks)


def block_grads_kernel(count, groups, row_count, col_count, slots, left_is_model, *refs):
    ids = refs[:count]
    model_parts = refs[count : count + groups]
    hidden_parts = [
        refs[count + groups * (1 + i) : count + groups * (2 + i)] for i in range(count)
    ]
    base = count + groups * (1 + count)
    outs = refs[base : base + count]
    model = refs[base + count]
    hiddens = refs[base + count + 1 :]
    step = pl.program_id(0)

    def gather(parts, index, transpose):
        stacked = jnp.concatenate([part[index] for part in parts], axis=0)
        return stacked.T if transpose else stacked

    @pl.when(step == 0)
    def _():
        for row in range(row_count):
            model[row] = gather(model_parts, row, left_is_model)
        model[row_count] = jnp.zeros(model.shape[1:], model.dtype)
        for hidden, parts in zip(hiddens, hidden_parts):
            for col in range(col_count):
                hidden[col] = gather(parts, col, not left_is_model)

    for slot in range(slots):
        for ids_ref, hidden, out in zip(ids, hiddens, outs):
            row, col = place(row_count, col_count, ids_ref, step, slots, slot)
            left, right = (model[row], hidden[col]) if left_is_model else (hidden[col], model[row])
            out[0, 0, slot] = jnp.dot(left, right, preferred_element_type=jnp.float32).astype(
                out.dtype
            )


def block_grads(model_parts, hidden_parts, ids, slot_count, left_is_model):
    count, groups = len(ids), len(model_parts)
    row_count, tokens, block = model_parts[0].shape
    col_count = hidden_parts[0][0].shape[0]
    slots = divisor_up_to(slot_count, SLOTS_PER_STEP)
    total = tokens * groups
    out = jax.ShapeDtypeStruct((1, 1, slot_count, block, block), jnp.bfloat16)

    def held(blocks_held, transposed):
        shape = (block, total) if transposed else (total, block)
        return pltpu.VMEM((blocks_held,) + shape, jnp.bfloat16)

    flat = list(model_parts) + [part for parts in hidden_parts for part in parts]
    return pl.pallas_call(
        functools.partial(
            block_grads_kernel, count, groups, row_count, col_count, slots, left_is_model
        ),
        out_shape=[out] * count,
        grid_spec=pltpu.PrefetchScalarGridSpec(
            num_scalar_prefetch=count,
            grid=(slot_count // slots,),
            in_specs=[resident(part.shape) for part in flat],
            out_specs=[stepped(slots, block)] * count,
            scratch_shapes=[held(row_count + 1, left_is_model)]
            + [held(col_count, not left_is_model)] * count,
        ),
        compiler_params=pltpu.CompilerParams(
            dimension_semantics=("arbitrary",), vmem_limit_bytes=VMEM_LIMIT
        ),
        cost_estimate=pl.CostEstimate(
            flops=2 * count * slot_count * total * block * block,
            bytes_accessed=2 * count * slot_count * block * block,
            transcendentals=0,
        ),
    )(*ids, *flat)


def sent(value, axis, target):
    size = lax.axis_size(axis)
    return lax.ppermute(value, axis, [(i, target(i, size)) for i in range(size)])


def gathered(value, axis):
    size = lax.axis_size(axis)
    return [value] + [
        sent(value, axis, lambda i, n, d=d: (i + d) % n) for d in range(1, size)
    ]


def gathered_by_halves(value, axis):
    size = lax.axis_size(axis)
    if size & (size - 1):
        return gathered(value, axis)
    pieces = [value]
    distance = size // 2
    while distance:
        pieces += [sent(piece, axis, lambda i, n, d=distance: i ^ d) for piece in pieces]
        distance //= 2
    return pieces


def scattered_sum(pieces, axis):
    total = pieces[0].astype(jnp.float32)
    for d in range(1, len(pieces)):
        total += sent(pieces[d], axis, lambda i, n, d=d: (i - d) % n).astype(jnp.float32)
    return total.astype(jnp.bfloat16)


def summed(value, axis):
    size = lax.axis_size(axis)
    return sum(piece.astype(jnp.float32) for piece in gathered(value, axis))


def on_device(tokens, out_grad, gate_blocks, up_blocks, down_blocks, gate_ids, up_ids, down_ids):
    slot_count, block = gate_blocks.shape[2], gate_blocks.shape[-1]
    tile = lax.axis_size("tile")
    row_count = tokens.shape[1] // block
    col_count = FF // tile // block
    grid = (row_count, col_count)
    gate_ids, up_ids, down_ids = (ids.reshape(slot_count) for ids in (gate_ids, up_ids, down_ids))

    token_parts = gathered(tokens, "tile")
    grad_parts = gathered(out_grad, "tile")
    gate_part, up_part, token_rows = to_hidden(
        token_parts, [gate_blocks, up_blocks], [gate_ids, up_ids], *grid, False
    )
    back_part, grad_rows = to_hidden(grad_parts, [down_blocks], [down_ids], *grid, True)
    gate_sum = summed(gate_part, "dp")
    up_sum = summed(up_part, "dp")
    sigmoid = jax.nn.sigmoid(gate_sum)
    silu_gate = gate_sum * sigmoid
    hidden = (silu_gate * up_sum).astype(jnp.bfloat16)
    output = to_model([hidden], [down_blocks], [down_ids], *grid, tile, False)
    hidden_grad = summed(back_part, "dp")
    gate_act_grad = (hidden_grad * up_sum * sigmoid * (1.0 + gate_sum * (1.0 - sigmoid))).astype(
        jnp.bfloat16
    )
    up_act_grad = (hidden_grad * silu_gate).astype(jnp.bfloat16)
    input_grad = to_model(
        [gate_act_grad, up_act_grad],
        [gate_blocks, up_blocks],
        [gate_ids, up_ids],
        *grid,
        tile,
        True,
    )
    all_tokens = gathered_by_halves(token_rows, "replica")
    all_grads = gathered_by_halves(grad_rows, "replica")
    all_hidden = gathered_by_halves(hidden, "replica")
    all_gate = gathered_by_halves(gate_act_grad, "replica")
    all_up = gathered_by_halves(up_act_grad, "replica")
    (down_grad,) = block_grads(all_grads, [all_hidden], [down_ids], slot_count, False)
    gate_grad, up_grad = block_grads(
        all_tokens, [all_gate, all_up], [gate_ids, up_ids], slot_count, True
    )
    return (
        scattered_sum(output, "tile"),
        scattered_sum(input_grad, "tile"),
        gate_grad,
        up_grad,
        down_grad,
    )


def solution(mesh):
    rows = P(("tile", "replica"), "dp")
    blocks = P("dp", "tile", None, None, None)
    ids = P("dp", "tile", None)
    return jax.shard_map(
        on_device,
        mesh=mesh,
        in_specs=(rows, rows, blocks, blocks, blocks, ids, ids, ids),
        out_specs=(rows, rows, blocks, blocks, blocks),
        check_vma=False,
    )
```

time: 1090 us -> 147 us (0.13); the launches traced: 1080 us -> 146 us
  waiting for transfers between devices: 652 us -> 13 us
  other arithmetic: 217 us -> 8.27 us
  matrix products: 103 us -> 0 us
  Pallas kernels: 0 us -> 89.9 us
  blocking collectives: 47 us -> 0 us
  local copies, waits for them, and re-layouts: 43.4 us -> 4.11 us
  starting transfers between devices: 0.46 us -> 29.7 us
  between operations: 14.5 us -> 0.86 us
    psum x1 -> x0, waiting for transfers between devices: 630 us -> none  [on_device(): lax.psum(gate_part.astype(jnp.bfloat16), 'replica').astype(jnp.float32)]
    scatter-add x6 -> x0, other arithmetic: 207 us -> none  [place_blocks(): placed = placed.at[:, index, :].add(product, mode='drop')]
    dot_general x9 -> x0, matrix products: 103 us -> none  [the longest x1 15.1 us: on_device(): jnp.einsum('tsf,skf->tsk', up_piece, up_local, preferred_element_type=jnp...]
    pallas_call x0 -> x6, Pallas kernels: none -> 89.9 us  [the longest x2 31.9 us: to_model(): pl.pallas_call(functools.partial(to_model_kernel, count, pieces, row_coun...]
    all_gather x5 -> x0, blocking collectives: 47 us -> none  [the longest x1 15.8 us: on_device(): lax.all_gather(tokens, 'tile', axis=0, tiled=True)]
    ppermute x0 -> x30, starting transfers between devices: none -> 29.7 us  [sent(): lax.ppermute(value, axis, [(i, target(i, size)) for i in range(size)])]
    unnamed x25 -> x54, local copies, waits for them, and re-layouts: 26 us -> 4.11 us
    reduce_scatter x4 -> x0, waiting for transfers between devices: 21.8 us -> none  [the longest x1 11.6 us: on_device(): lax.psum_scatter(place_blocks(back_product, down_colslot, col_count, bloc...]
  transfers between devices with their start and end apart: 5 -> 30, of which waited for: 3 -> 6; matrix products, arithmetic and copies ran while one was open for 11% -> 6% of each run, Pallas kernels for 0% -> 51%
where the time goes in v1:
time: 147 us; the launch traced here: 146 us
  Pallas kernels  89.9 us (61%)
  starting transfers between devices  29.7 us (20%)
  waiting for transfers between devices  13 us (9%)
  other arithmetic  8.27 us (6%)
  local copies, waits for them, and re-layouts  4.11 us (3%)
    pallas_call x2, Pallas kernels, to_model(): pl.pallas_call(functools.partial(to_model_kernel, count, pieces, row_coun...  31.9 us
    pallas_call x2, Pallas kernels, to_hidden(): pl.pallas_call(functools.partial(to_hidden_kernel, count, pieces, row_cou...  30.6 us
    ppermute x30, starting transfers between devices, sent(): lax.ppermute(value, axis, [(i, target(i, size)) for i in range(size)])  29.7 us
    pallas_call x2, Pallas kernels, block_grads(): pl.pallas_call(functools.partial(block_grads_kernel, count, groups, row_c...  27.3 us
    ppermute x30, waiting for transfers between devices, sent(): lax.ppermute(value, axis, [(i, target(i, size)) for i in range(size)])  13 us
    unnamed x54, local copies, waits for them, and re-layouts  4.11 us
    unnamed x3, other arithmetic  3.86 us
  transfers between devices with their start and end apart: 30, of which 6 were waited for; matrix products, arithmetic and copies ran while one was open for 6% of the time, Pallas kernels for 51%

profile of v1, /device:TPU:0, one launch (start us, length us, event | category | flops | bytes accessed | tf_op | source)
XLA Modules:
  0.0 145.8 jit_solution(3980725347287079367)
XLA Ops:
  0.6 3.1 %collective-permute-start.8 = (bf16[8,4096]{1,0:T(8,128)(2,1)}, bf16[8,4096]{1,0:T(8,128)(2,1)S(1)}, u32[]{:S(2)}, u32[]{:S(2)}) collective-permute-start(bf16[8,4096]{1,0:T(8,128)(2,1)} %refs_1_.1), channel_id=1, source_target_pairs={{0,4},{4,8},{8,12},{12,0},{1,5},{5,9},{9,13},{13,1},{2,6},{6,10},{... | collective-permute-start | bytes 196616 | tf_op jit(solution)/shard_map/ppermute | solution.py:239
  3.7 2.6 %collective-permute-start.9 = (bf16[8,4096]{1,0:T(8,128)(2,1)}, bf16[8,4096]{1,0:T(8,128)(2,1)S(1)}, u32[]{:S(2)}, u32[]{:S(2)}) collective-permute-start(bf16[8,4096]{1,0:T(8,128)(2,1)} %refs_1_.1), channel_id=1, source_target_pairs={{0,8},{4,12},{8,0},{12,4},{1,9},{5,13},{9,1},{13,5},{2,10},{6,14},... | collective-permute-start | bytes 196616 | tf_op jit(solution)/shard_map/ppermute | solution.py:239
  6.3 1.3 collective-permute-start.10
  7.6 0.7 collective-permute-start
  8.7 2.9 %collective-permute-start.2 = (bf16[8,4096]{1,0:T(8,128)(2,1)}, bf16[8,4096]{1,0:T(8,128)(2,1)S(1)}, u32[]{:S(2)}, u32[]{:S(2)}) collective-permute-start(bf16[8,4096]{1,0:T(8,128)(2,1)} %refs_2_.2), channel_id=1, source_target_pairs={{0,12},{4,0},{8,4},{12,8},{1,13},{5,1},{9,5},{13,9},{2,14},{6,2},{... | collective-permute-start | bytes 196616 | tf_op jit(solution)/shard_map/ppermute | solution.py:239
  11.5 1.3 reduce.refs_0_
  12.8 1.3 reduce.1.refs_0_
  14.1 1.3 reduce.2.refs_1_
  16.0 0.6 copy-done.15
  16.7 14.0 %shard_map.121 = (bf16[28,32,128]{2,1,0:T(8,128)(2,1)}, bf16[32,32,128]{2,1,0:T(8,128)(2,1)}) custom-call(s32[384]{0:T(512)} %reduce.refs_0_, bf16[8,4096]{1,0:T(8,128)(2,1)} %refs_1_.1, bf16[8,4096]{1,0:T(8,128)(2,1)} %copy-done.12, bf16[8,4096]{1,0:T(8,128)(2,1)} %copy-done.14, bf16[8,4096]{1,0:T(8,128)(2,1)} %copy-done.15, ...), custom_call_target="tpu_custom_call" | custom-call | flops 402653184 | bytes 12582912 | tf_op jit(solution)/shard_map/pallas_call | solution.py:83
  30.7 1.6 %collective-permute-start.11 = (bf16[28,32,128]{2,1,0:T(8,128)(2,1)}, bf16[28,32,128]{2,1,0:T(8,128)(2,1)S(1)}, u32[]{:S(2)}, u32[]{:S(2)}) collective-permute-start(bf16[28,32,128]{2,1,0:T(8,128)(2,1)} %get-tuple-element.26), channel_id=1, source_target_pairs={{0,16},{16,0},{1,17},{17,1},{2,18},{18,2},{3,19},{19,3},{4,20},{20... | collective-permute-start | bytes 688136 | tf_op jit(solution)/shard_map/ppermute | solution.py:239
  33.6 16.6 %shard_map.119 = (bf16[28,32,128]{2,1,0:T(8,128)(2,1)}, bf16[28,32,128]{2,1,0:T(8,128)(2,1)}, bf16[32,32,128]{2,1,0:T(8,128)(2,1)}) custom-call(s32[384]{0:T(512)} %reduce.1.refs_0_, s32[384]{0:T(512)} %reduce.2.refs_1_, bf16[8,4096]{1,0:T(8,128)(2,1)} %refs_2_.2, bf16[8,4096]{1,0:T(8,128)(2,1)} %copy-done.10, bf16[8,4096]{1,0:T(8,128)(2,1)} %copy-done.11, ...), custom_call_target="tpu_custom_call" | custom-call | flops 805306368 | bytes 25165824 | tf_op jit(solution)/shard_map/pallas_call | solution.py:83
  50.6 1.5 %collective-permute-start.4 = (bf16[28,32,128]{2,1,0:T(8,128)(2,1)}, bf16[28,32,128]{2,1,0:T(8,128)(2,1)S(1)}, u32[]{:S(2)}, u32[]{:S(2)}) collective-permute-start(bf16[28,32,128]{2,1,0:T(8,128)(2,1)} %get-tuple-element.21), channel_id=1, source_target_pairs={{0,16},{16,0},{1,17},{17,1},{2,18},{18,2},{3,19},{19,3},{4,20},{20... | collective-permute-start | bytes 688136 | tf_op jit(solution)/shard_map/ppermute | solution.py:239
  52.2 1.5 %collective-permute-start.15 = (bf16[32,32,128]{2,1,0:T(8,128)(2,1)}, bf16[32,32,128]{2,1,0:T(8,128)(2,1)S(1)}, u32[]{:S(2)}, u32[]{:S(2)}) collective-permute-start(bf16[32,32,128]{2,1,0:T(8,128)(2,1)} %get-tuple-element.31.refs_2_), channel_id=1, source_target_pairs={{0,2},{1,3},{2,0},{3,1},{4,6},{5,7},{6,4},{7,5},{8,10},{9,11},{10,... | collective-permute-start | bytes 786440 | tf_op jit(solution)/shard_map/ppermute | solution.py:239
  54.3 4.2 %collective-permute-done.3 = bf16[28,32,128]{2,1,0:T(8,128)(2,1)S(1)} collective-permute-done((bf16[28,32,128]{2,1,0:T(8,128)(2,1)}, bf16[28,32,128]{2,1,0:T(8,128)(2,1)S(1)}, u32[]{:S(2)}, u32[]{:S(2)}) %collective-permute-start.3) | collective-permute-done | bytes 229408 | tf_op jit(solution)/shard_map/ppermute | solution.py:239
  58.5 2.5 %collective-permute-done.4 = bf16[28,32,128]{2,1,0:T(8,128)(2,1)S(1)} collective-permute-done((bf16[28,32,128]{2,1,0:T(8,128)(2,1)}, bf16[28,32,128]{2,1,0:T(8,128)(2,1)S(1)}, u32[]{:S(2)}, u32[]{:S(2)}) %collective-permute-start.4) | collective-permute-done | bytes 229408 | tf_op jit(solution)/shard_map/ppermute | solution.py:239
  60.9 2.2 %multiply_convert_fusion = (bf16[28,32,128]{2,1,0:T(8,128)(2,1)}, bf16[28,32,128]{2,1,0:T(8,128)(2,1)}, bf16[28,32,128]{2,1,0:T(8,128)(2,1)}) fusion(bf16[28,32,128]{2,1,0:T(8,128)(2,1)S(1)} %collective-permute-done.11, bf16[28,32,128]{2,1,0:T(8,128)(2,1)S(1)} %copy-done.9, bf16[28,32,128]{2,1,0:T(8,128)(2,1)S(1)} %collective-permute-done.3, ...), kind=kLoop, calls=%fused_computation | loop fusion | flops 2752512 | bytes 2064384 | tf_op jit(solution)/shard_map/convert_element_type | solution.py:297
  63.2 1.5 %collective-permute-start.27 = (bf16[28,32,128]{2,1,0:T(8,128)(2,1)}, bf16[28,32,128]{2,1,0:T(8,128)(2,1)S(1)}, u32[]{:S(2)}, u32[]{:S(2)}) collective-permute-start(bf16[28,32,128]{2,1,0:T(8,128)(2,1)} %get-tuple-element.37.refs_1_.refs_5_), channel_id=1, source_target_pairs={{0,2},{1,3},{2,0},{3,1},{4,6},{5,7},{6,4},{7,5},{8,10},{9,11},{10,... | collective-permute-start | bytes 688136 | tf_op jit(solution)/shard_map/ppermute | solution.py:239
  64.7 12.1 %shard_map.120 = (bf16[8,4096]{1,0:T(8,128)(2,1)}, bf16[8,4096]{1,0:T(8,128)(2,1)}, bf16[8,4096]{1,0:T(8,128)(2,1)}, bf16[8,4096]{1,0:T(8,128)(2,1)}) custom-call(s32[384]{0:T(512)} %reduce.refs_0_, bf16[28,32,128]{2,1,0:T(8,128)(2,1)} %get-tuple-element.37.refs_1_.refs_5_, bf16[1,1,384,128,128]{4,3,2,1,0:T(8,128)(2,1)} %refs_5_.2), custom_call_target="tpu_custom_call" | custom-call | flops 402653184 | bytes 12582912 | tf_op jit(solution)/shard_map/pallas_call | solution.py:144
  77.4 1.2 collective-permute-start.6
  78.7 19.8 %shard_map.122 = (bf16[8,4096]{1,0:T(8,128)(2,1)}, bf16[8,4096]{1,0:T(8,128)(2,1)}, bf16[8,4096]{1,0:T(8,128)(2,1)}, bf16[8,4096]{1,0:T(8,128)(2,1)}) custom-call(s32[384]{0:T(512)} %reduce.1.refs_0_, s32[384]{0:T(512)} %reduce.2.refs_1_, bf16[28,32,128]{2,1,0:T(8,128)(2,1)} %get-tuple-element.36.refs_2_.refs_6_, ...), custom_call_target="tpu_custom_call" | custom-call | flops 805306368 | bytes 25165824 | tf_op jit(solution)/shard_map/pallas_call | solution.py:144
  98.5 2.9 %collective-permute-start.5 = (bf16[8,4096]{1,0:T(8,128)(2,1)S(1)}, bf16[8,4096]{1,0:T(8,128)(2,1)S(1)}, u32[]{:S(2)}, u32[]{:S(2)}) collective-permute-start(bf16[8,4096]{1,0:T(8,128)(2,1)S(1)} %copy-done.26), channel_id=1, source_target_pairs={{0,12},{4,0},{8,4},{12,8},{1,13},{5,1},{9,5},{13,9},{2,14},{6,2},{... | collective-permute-start | bytes 196616 | tf_op jit(solution)/shard_map/ppermute | solution.py:239
  101.4 1.4 collective-permute-start.13
  102.8 2.8 %collective-permute-start.12 = (bf16[8,4096]{1,0:T(8,128)(2,1)}, bf16[8,4096]{1,0:T(8,128)(2,1)S(1)}, u32[]{:S(2)}, u32[]{:S(2)}) collective-permute-start(bf16[8,4096]{1,0:T(8,128)(2,1)} %get-tuple-element.28), channel_id=1, source_target_pairs={{0,12},{4,0},{8,4},{12,8},{1,13},{5,1},{9,5},{13,9},{2,14},{6,2},{... | collective-permute-start | bytes 196616 | tf_op jit(solution)/shard_map/ppermute | solution.py:239
  106.2 1.5 %collective-permute-done.14 = bf16[8,4096]{1,0:T(8,128)(2,1)S(1)} collective-permute-done((bf16[8,4096]{1,0:T(8,128)(2,1)}, bf16[8,4096]{1,0:T(8,128)(2,1)S(1)}, u32[]{:S(2)}, u32[]{:S(2)}) %collective-permute-start.14) | collective-permute-done | bytes 65568 | tf_op jit(solution)/shard_map/ppermute | solution.py:239
  108.9 0.7 add_convert_fusion.1
  109.6 2.2 %collective-permute-done.18.refs_7_ = bf16[28,32,128]{2,1,0:T(8,128)(2,1)S(1)} collective-permute-done((bf16[28,32,128]{2,1,0:T(8,128)(2,1)S(1)}, bf16[28,32,128]{2,1,0:T(8,128)(2,1)S(1)}, u32[]{:S(2)}, u32[]{:S(2)}) %collective-permute-start.18) | collective-permute-done | bytes 229408 | tf_op jit(solution)/shard_map/ppermute | solution.py:239
  111.7 2.5 %collective-permute-done.21.refs_11_ = bf16[28,32,128]{2,1,0:T(8,128)(2,1)S(1)} collective-permute-done((bf16[28,32,128]{2,1,0:T(8,128)(2,1)S(1)}, bf16[28,32,128]{2,1,0:T(8,128)(2,1)S(1)}, u32[]{:S(2)}, u32[]{:S(2)}) %collective-permute-start.21) | collective-permute-done | bytes 229408 | tf_op jit(solution)/shard_map/ppermute | solution.py:239
  115.3 1.5 %add_convert_fusion = bf16[8,4096]{1,0:T(8,128)(2,1)} fusion(bf16[8,4096]{1,0:T(8,128)(2,1)S(1)} %collective-permute-done.14, bf16[8,4096]{1,0:T(8,128)(2,1)S(1)} %collective-permute-done.13, bf16[8,4096]{1,0:T(8,128)(2,1)S(1)} %collective-permute-done.12, bf16[8,4096]{1,0:T(8,128)(2,1)} %get-tuple-element.27), kind=kLoop, calls=%fused_computation.8 | loop fusion | flops 262144 | bytes 327680 | tf_op jit(solution)/shard_map/convert_element_type | solution.py:265
  116.8 11.5 %shard_map.124 = bf16[1,1,384,128,128]{4,3,2,1,0:T(8,128)(2,1)} custom-call(s32[384]{0:T(512)} %reduce.refs_0_, bf16[32,32,128]{2,1,0:T(8,128)(2,1)} %get-tuple-element.34.refs_1_, bf16[32,32,128]{2,1,0:T(8,128)(2,1)} %copy-done.3, bf16[32,32,128]{2,1,0:T(8,128)(2,1)} %copy-done.4, bf16[32,32,128]{2,1,0:T(8,128)(2,1)} %copy-done.5, ...), custom_call_target="tpu_custom_call" | custom-call | flops 1610612736 | bytes 12582912 | tf_op jit(solution)/shard_map/pallas_call | solution.py:213
  129.3 0.7 copy-done.25
  130.0 15.8 %shard_map.123 = (bf16[1,1,384,128,128]{4,3,2,1,0:T(8,128)(2,1)}, bf16[1,1,384,128,128]{4,3,2,1,0:T(8,128)(2,1)}) custom-call(s32[384]{0:T(512)} %reduce.1.refs_0_, s32[384]{0:T(512)} %reduce.2.refs_1_, bf16[32,32,128]{2,1,0:T(8,128)(2,1)} %get-tuple-element.31.refs_2_, bf16[32,32,128]{2,1,0:T(8,128)(2,1)} %copy-done.17, bf16[32,32,128]{2,1,0:T(8,128)(2,1)} %copy-done.18, ...), custom_call_target="tpu_custom_call" | custom-call | flops 3221225472 | bytes 25165824 | tf_op jit(solution)/shard_map/pallas_call | solution.py:213
  (94 shorter events, 7.7 us)
Async XLA Ops:
  0.6 8.0 %collective-permute-start.8 = (bf16[8,4096]{1,0:T(8,128)(2,1)}, bf16[8,4096]{1,0:T(8,128)(2,1)S(1)}, u32[]{:S(2)}, u32[]{:S(2)}) collective-permute-start(bf16[8,4096]{1,0:T(8,128)(2,1)} %refs_1_.1), channel_id=1, source_target_pairs={{0,4},{4,8},{8,12},{12,0},{1,5},{5,9},{9,13},{13,1},{2,6},{6,10},{... | collective-permute-start | bytes 196616 | tf_op jit(solution)/shard_map/ppermute | solution.py:239
  3.7 11.7 %collective-permute-start.9 = (bf16[8,4096]{1,0:T(8,128)(2,1)}, bf16[8,4096]{1,0:T(8,128)(2,1)S(1)}, u32[]{:S(2)}, u32[]{:S(2)}) collective-permute-start(bf16[8,4096]{1,0:T(8,128)(2,1)} %refs_1_.1), channel_id=1, source_target_pairs={{0,8},{4,12},{8,0},{12,4},{1,9},{5,13},{9,1},{13,5},{2,10},{6,14},... | collective-permute-start | bytes 196616 | tf_op jit(solution)/shard_map/ppermute | solution.py:239
  6.3 9.1 %collective-permute-start.10 = (bf16[8,4096]{1,0:T(8,128)(2,1)}, bf16[8,4096]{1,0:T(8,128)(2,1)S(1)}, u32[]{:S(2)}, u32[]{:S(2)}) collective-permute-start(bf16[8,4096]{1,0:T(8,128)(2,1)} %refs_1_.1), channel_id=1, source_target_pairs={{0,12},{4,0},{8,4},{12,8},{1,13},{5,1},{9,5},{13,9},{2,14},{6,2},{... | collective-permute-start | bytes 196616 | tf_op jit(solution)/shard_map/ppermute | solution.py:239
  7.6 24.6 %collective-permute-start = (bf16[8,4096]{1,0:T(8,128)(2,1)}, bf16[8,4096]{1,0:T(8,128)(2,1)S(1)}, u32[]{:S(2)}, u32[]{:S(2)}) collective-permute-start(bf16[8,4096]{1,0:T(8,128)(2,1)} %refs_2_.2), channel_id=1, source_target_pairs={{0,4},{4,8},{8,12},{12,0},{1,5},{5,9},{9,13},{13,1},{2,6},{6,10},{... | collective-permute-start | bytes 196616 | tf_op jit(solution)/shard_map/ppermute | solution.py:239
  8.3 24.0 %collective-permute-start.1 = (bf16[8,4096]{1,0:T(8,128)(2,1)}, bf16[8,4096]{1,0:T(8,128)(2,1)S(1)}, u32[]{:S(2)}, u32[]{:S(2)}) collective-permute-start(bf16[8,4096]{1,0:T(8,128)(2,1)} %refs_2_.2), channel_id=1, source_target_pairs={{0,8},{4,12},{8,0},{12,4},{1,9},{5,13},{9,1},{13,5},{2,10},{6,14},... | collective-permute-start | bytes 196616 | tf_op jit(solution)/shard_map/ppermute | solution.py:239
  8.7 23.6 %collective-permute-start.2 = (bf16[8,4096]{1,0:T(8,128)(2,1)}, bf16[8,4096]{1,0:T(8,128)(2,1)S(1)}, u32[]{:S(2)}, u32[]{:S(2)}) collective-permute-start(bf16[8,4096]{1,0:T(8,128)(2,1)} %refs_2_.2), channel_id=1, source_target_pairs={{0,12},{4,0},{8,4},{12,8},{1,13},{5,1},{9,5},{13,9},{2,14},{6,2},{... | collective-permute-start | bytes 196616 | tf_op jit(solution)/shard_map/ppermute | solution.py:239
  30.7 30.3 %copy-start.9 = (bf16[28,32,128]{2,1,0:T(8,128)(2,1)S(1)}, bf16[28,32,128]{2,1,0:T(8,128)(2,1)}, u32[]{:S(2)}) copy-start(bf16[28,32,128]{2,1,0:T(8,128)(2,1)} %get-tuple-element.26) | copy-start | bytes 688132
  30.7 23.0 %collective-permute-start.11 = (bf16[28,32,128]{2,1,0:T(8,128)(2,1)}, bf16[28,32,128]{2,1,0:T(8,128)(2,1)S(1)}, u32[]{:S(2)}, u32[]{:S(2)}) collective-permute-start(bf16[28,32,128]{2,1,0:T(8,128)(2,1)} %get-tuple-element.26), channel_id=1, source_target_pairs={{0,16},{16,0},{1,17},{17,1},{2,18},{18,2},{3,19},{19,3},{4,20},{20... | collective-permute-start | bytes 688136 | tf_op jit(solution)/shard_map/ppermute | solution.py:239
  50.2 8.3 %collective-permute-start.3 = (bf16[28,32,128]{2,1,0:T(8,128)(2,1)}, bf16[28,32,128]{2,1,0:T(8,128)(2,1)S(1)}, u32[]{:S(2)}, u32[]{:S(2)}) collective-permute-start(bf16[28,32,128]{2,1,0:T(8,128)(2,1)} %get-tuple-element.20), channel_id=1, source_target_pairs={{0,16},{16,0},{1,17},{17,1},{2,18},{18,2},{3,19},{19,3},{4,20},{20... | collective-permute-start | bytes 688136 | tf_op jit(solution)/shard_map/ppermute | solution.py:239
  50.6 10.3 %collective-permute-start.4 = (bf16[28,32,128]{2,1,0:T(8,128)(2,1)}, bf16[28,32,128]{2,1,0:T(8,128)(2,1)S(1)}, u32[]{:S(2)}, u32[]{:S(2)}) collective-permute-start(bf16[28,32,128]{2,1,0:T(8,128)(2,1)} %get-tuple-element.21), channel_id=1, source_target_pairs={{0,16},{16,0},{1,17},{17,1},{2,18},{18,2},{3,19},{19,3},{4,20},{20... | collective-permute-start | bytes 688136 | tf_op jit(solution)/shard_map/ppermute | solution.py:239
  52.2 24.7 %collective-permute-start.15 = (bf16[32,32,128]{2,1,0:T(8,128)(2,1)}, bf16[32,32,128]{2,1,0:T(8,128)(2,1)S(1)}, u32[]{:S(2)}, u32[]{:S(2)}) collective-permute-start(bf16[32,32,128]{2,1,0:T(8,128)(2,1)} %get-tuple-element.31.refs_2_), channel_id=1, source_target_pairs={{0,2},{1,3},{2,0},{3,1},{4,6},{5,7},{6,4},{7,5},{8,10},{9,11},{10,... | collective-permute-start | bytes 786440 | tf_op jit(solution)/shard_map/ppermute | solution.py:239
  53.7 23.7 %collective-permute-start.16 = (bf16[32,32,128]{2,1,0:T(8,128)(2,1)}, bf16[32,32,128]{2,1,0:T(8,128)(2,1)S(1)}, u32[]{:S(2)}, u32[]{:S(2)}) collective-permute-start(bf16[32,32,128]{2,1,0:T(8,128)(2,1)} %get-tuple-element.31.refs_2_), channel_id=1, source_target_pairs={{0,1},{1,0},{2,3},{3,2},{4,5},{5,4},{6,7},{7,6},{8,9},{9,8},{10,11... | collective-permute-start | bytes 786440 | tf_op jit(solution)/shard_map/ppermute | solution.py:239
  53.7 44.8 %collective-permute-start.24 = (bf16[32,32,128]{2,1,0:T(8,128)(2,1)S(1)}, bf16[32,32,128]{2,1,0:T(8,128)(2,1)S(1)}, u32[]{:S(2)}, u32[]{:S(2)}) collective-permute-start(bf16[32,32,128]{2,1,0:T(8,128)(2,1)S(1)} %copy-done.2), channel_id=1, source_target_pairs={{0,2},{1,3},{2,0},{3,1},{4,6},{5,7},{6,4},{7,5},{8,10},{9,11},{10,... | collective-permute-start | bytes 786440 | tf_op jit(solution)/shard_map/ppermute | solution.py:239
  58.5 42.9 %collective-permute-start.25 = (bf16[32,32,128]{2,1,0:T(8,128)(2,1)S(1)}, bf16[32,32,128]{2,1,0:T(8,128)(2,1)S(1)}, u32[]{:S(2)}, u32[]{:S(2)}) collective-permute-start(bf16[32,32,128]{2,1,0:T(8,128)(2,1)S(1)} %copy-done.2), channel_id=1, source_target_pairs={{0,1},{1,0},{2,3},{3,2},{4,5},{5,4},{6,7},{7,6},{8,9},{9,8},{10,11... | collective-permute-start | bytes 786440 | tf_op jit(solution)/shard_map/ppermute | solution.py:239
  63.2 45.5 %collective-permute-start.27 = (bf16[28,32,128]{2,1,0:T(8,128)(2,1)}, bf16[28,32,128]{2,1,0:T(8,128)(2,1)S(1)}, u32[]{:S(2)}, u32[]{:S(2)}) collective-permute-start(bf16[28,32,128]{2,1,0:T(8,128)(2,1)} %get-tuple-element.37.refs_1_.refs_5_), channel_id=1, source_target_pairs={{0,2},{1,3},{2,0},{3,1},{4,6},{5,7},{6,4},{7,5},{8,10},{9,11},{10,... | collective-permute-start | bytes 688136 | tf_op jit(solution)/shard_map/ppermute | solution.py:239
  76.8 37.4 %copy-start.17 = (bf16[32,32,128]{2,1,0:T(8,128)(2,1)}, bf16[32,32,128]{2,1,0:T(8,128)(2,1)S(1)}, u32[]{:S(2)}) copy-start(bf16[32,32,128]{2,1,0:T(8,128)(2,1)S(1)} %collective-permute-done.15.refs_3_) | copy-start | bytes 786436
  76.8 24.6 %collective-permute-start.7 = (bf16[8,4096]{1,0:T(8,128)(2,1)}, bf16[8,4096]{1,0:T(8,128)(2,1)S(1)}, u32[]{:S(2)}, u32[]{:S(2)}) collective-permute-start(bf16[8,4096]{1,0:T(8,128)(2,1)} %get-tuple-element.25), channel_id=1, source_target_pairs={{0,4},{4,8},{8,12},{12,0},{1,5},{5,9},{9,13},{13,1},{2,6},{6,10},{... | collective-permute-start | bytes 196616 | tf_op jit(solution)/shard_map/ppermute | solution.py:239
  77.4 25.4 %collective-permute-start.6 = (bf16[8,4096]{1,0:T(8,128)(2,1)}, bf16[8,4096]{1,0:T(8,128)(2,1)S(1)}, u32[]{:S(2)}, u32[]{:S(2)}) collective-permute-start(bf16[8,4096]{1,0:T(8,128)(2,1)} %get-tuple-element.24), channel_id=1, source_target_pairs={{0,8},{4,12},{8,0},{12,4},{1,9},{5,13},{9,1},{13,5},{2,10},{6,14},... | collective-permute-start | bytes 196616 | tf_op jit(solution)/shard_map/ppermute | solution.py:239
  98.5 7.2 %collective-permute-start.5 = (bf16[8,4096]{1,0:T(8,128)(2,1)S(1)}, bf16[8,4096]{1,0:T(8,128)(2,1)S(1)}, u32[]{:S(2)}, u32[]{:S(2)}) collective-permute-start(bf16[8,4096]{1,0:T(8,128)(2,1)S(1)} %copy-done.26), channel_id=1, source_target_pairs={{0,12},{4,0},{8,4},{12,8},{1,13},{5,1},{9,5},{13,9},{2,14},{6,2},{... | collective-permute-start | bytes 196616 | tf_op jit(solution)/shard_map/ppermute | solution.py:239
  101.4 6.3 %collective-permute-start.14 = (bf16[8,4096]{1,0:T(8,128)(2,1)}, bf16[8,4096]{1,0:T(8,128)(2,1)S(1)}, u32[]{:S(2)}, u32[]{:S(2)}) collective-permute-start(bf16[8,4096]{1,0:T(8,128)(2,1)} %get-tuple-element.30), channel_id=1, source_target_pairs={{0,4},{4,8},{8,12},{12,0},{1,5},{5,9},{9,13},{13,1},{2,6},{6,10},{... | collective-permute-start | bytes 196616 | tf_op jit(solution)/shard_map/ppermute | solution.py:239
  101.4 6.8 %collective-permute-start.13 = (bf16[8,4096]{1,0:T(8,128)(2,1)}, bf16[8,4096]{1,0:T(8,128)(2,1)S(1)}, u32[]{:S(2)}, u32[]{:S(2)}) collective-permute-start(bf16[8,4096]{1,0:T(8,128)(2,1)} %get-tuple-element.29), channel_id=1, source_target_pairs={{0,8},{4,12},{8,0},{12,4},{1,9},{5,13},{9,1},{13,5},{2,10},{6,14},... | collective-permute-start | bytes 196616 | tf_op jit(solution)/shard_map/ppermute | solution.py:239
  102.8 5.6 %collective-permute-start.12 = (bf16[8,4096]{1,0:T(8,128)(2,1)}, bf16[8,4096]{1,0:T(8,128)(2,1)S(1)}, u32[]{:S(2)}, u32[]{:S(2)}) collective-permute-start(bf16[8,4096]{1,0:T(8,128)(2,1)} %get-tuple-element.28), channel_id=1, source_target_pairs={{0,12},{4,0},{8,4},{12,8},{1,13},{5,1},{9,5},{13,9},{2,14},{6,2},{... | collective-permute-start | bytes 196616 | tf_op jit(solution)/shard_map/ppermute | solution.py:239
  105.7 6.1 %collective-permute-start.18 = (bf16[28,32,128]{2,1,0:T(8,128)(2,1)S(1)}, bf16[28,32,128]{2,1,0:T(8,128)(2,1)S(1)}, u32[]{:S(2)}, u32[]{:S(2)}) collective-permute-start(bf16[28,32,128]{2,1,0:T(8,128)(2,1)S(1)} %copy-done.1), channel_id=1, source_target_pairs={{0,2},{1,3},{2,0},{3,1},{4,6},{5,7},{6,4},{7,5},{8,10},{9,11},{10,... | collective-permute-start | bytes 688136 | tf_op jit(solution)/shard_map/ppermute | solution.py:239
  107.7 6.5 %collective-permute-start.21 = (bf16[28,32,128]{2,1,0:T(8,128)(2,1)S(1)}, bf16[28,32,128]{2,1,0:T(8,128)(2,1)S(1)}, u32[]{:S(2)}, u32[]{:S(2)}) collective-permute-start(bf16[28,32,128]{2,1,0:T(8,128)(2,1)S(1)} %copy-done), channel_id=1, source_target_pairs={{0,2},{1,3},{2,0},{3,1},{4,6},{5,7},{6,4},{7,5},{8,10},{9,11},{10,... | collective-permute-start | bytes 688136 | tf_op jit(solution)/shard_map/ppermute | solution.py:239
  108.2 6.0 %collective-permute-start.28 = (bf16[28,32,128]{2,1,0:T(8,128)(2,1)}, bf16[28,32,128]{2,1,0:T(8,128)(2,1)S(1)}, u32[]{:S(2)}, u32[]{:S(2)}) collective-permute-start(bf16[28,32,128]{2,1,0:T(8,128)(2,1)} %get-tuple-element.37.refs_1_.refs_5_), channel_id=1, source_target_pairs={{0,1},{1,0},{2,3},{3,2},{4,5},{5,4},{6,7},{7,6},{8,9},{9,8},{10,11... | collective-permute-start | bytes 688136 | tf_op jit(solution)/shard_map/ppermute | solution.py:239
  108.4 6.4 %collective-permute-start.26 = (bf16[32,32,128]{2,1,0:T(8,128)(2,1)S(1)}, bf16[32,32,128]{2,1,0:T(8,128)(2,1)S(1)}, u32[]{:S(2)}, u32[]{:S(2)}) collective-permute-start(bf16[32,32,128]{2,1,0:T(8,128)(2,1)S(1)} %collective-permute-done.24.refs_2_), channel_id=1, source_target_pairs={{0,1},{1,0},{2,3},{3,2},{4,5},{5,4},{6,7},{7,6},{8,9},{9,8},{10,11... | collective-permute-start | bytes 786440 | tf_op jit(solution)/shard_map/ppermute | solution.py:239
  108.7 6.1 %collective-permute-start.29 = (bf16[28,32,128]{2,1,0:T(8,128)(2,1)S(1)}, bf16[28,32,128]{2,1,0:T(8,128)(2,1)S(1)}, u32[]{:S(2)}, u32[]{:S(2)}) collective-permute-start(bf16[28,32,128]{2,1,0:T(8,128)(2,1)S(1)} %collective-permute-done.27.refs_6_), channel_id=1, source_target_pairs={{0,1},{1,0},{2,3},{3,2},{4,5},{5,4},{6,7},{7,6},{8,9},{9,8},{10,11... | collective-permute-start | bytes 688136 | tf_op jit(solution)/shard_map/ppermute | solution.py:239
  111.7 16.6 %collective-permute-start.19 = (bf16[28,32,128]{2,1,0:T(8,128)(2,1)S(1)}, bf16[28,32,128]{2,1,0:T(8,128)(2,1)S(1)}, u32[]{:S(2)}, u32[]{:S(2)}) collective-permute-start(bf16[28,32,128]{2,1,0:T(8,128)(2,1)S(1)} %copy-done.1), channel_id=1, source_target_pairs={{0,1},{1,0},{2,3},{3,2},{4,5},{5,4},{6,7},{7,6},{8,9},{9,8},{10,11... | collective-permute-start | bytes 688136 | tf_op jit(solution)/shard_map/ppermute | solution.py:239
  114.2 14.1 %collective-permute-start.22 = (bf16[28,32,128]{2,1,0:T(8,128)(2,1)S(1)}, bf16[28,32,128]{2,1,0:T(8,128)(2,1)S(1)}, u32[]{:S(2)}, u32[]{:S(2)}) collective-permute-start(bf16[28,32,128]{2,1,0:T(8,128)(2,1)S(1)} %copy-done), channel_id=1, source_target_pairs={{0,1},{1,0},{2,3},{3,2},{4,5},{5,4},{6,7},{7,6},{8,9},{9,8},{10,11... | collective-permute-start | bytes 688136 | tf_op jit(solution)/shard_map/ppermute | solution.py:239
  114.2 14.1 %collective-permute-start.17 = (bf16[32,32,128]{2,1,0:T(8,128)(2,1)S(1)}, bf16[32,32,128]{2,1,0:T(8,128)(2,1)S(1)}, u32[]{:S(2)}, u32[]{:S(2)}) collective-permute-start(bf16[32,32,128]{2,1,0:T(8,128)(2,1)S(1)} %collective-permute-done.15.refs_3_), channel_id=1, source_target_pairs={{0,1},{1,0},{2,3},{3,2},{4,5},{5,4},{6,7},{7,6},{8,9},{9,8},{10,11... | collective-permute-start | bytes 786440 | tf_op jit(solution)/shard_map/ppermute | solution.py:239
  114.8 13.6 %collective-permute-start.20 = (bf16[28,32,128]{2,1,0:T(8,128)(2,1)S(1)}, bf16[28,32,128]{2,1,0:T(8,128)(2,1)S(1)}, u32[]{:S(2)}, u32[]{:S(2)}) collective-permute-start(bf16[28,32,128]{2,1,0:T(8,128)(2,1)S(1)} %collective-permute-done.18.refs_7_), channel_id=1, source_target_pairs={{0,1},{1,0},{2,3},{3,2},{4,5},{5,4},{6,7},{7,6},{8,9},{9,8},{10,11... | collective-permute-start | bytes 688136 | tf_op jit(solution)/shard_map/ppermute | solution.py:239
  114.9 13.5 %collective-permute-start.23 = (bf16[28,32,128]{2,1,0:T(8,128)(2,1)S(1)}, bf16[28,32,128]{2,1,0:T(8,128)(2,1)S(1)}, u32[]{:S(2)}, u32[]{:S(2)}) collective-permute-start(bf16[28,32,128]{2,1,0:T(8,128)(2,1)S(1)} %collective-permute-done.21.refs_11_), channel_id=1, source_target_pairs={{0,1},{1,0},{2,3},{3,2},{4,5},{5,4},{6,7},{7,6},{8,9},{9,8},{10,11... | collective-permute-start | bytes 688136 | tf_op jit(solution)/shard_map/ppermute | solution.py:239
  (25 other events, 243.1 us)

commit v2 on v0

v2 whole, which is shorter than its diff:
```python
import functools

import jax
import jax.numpy as jnp
from jax import lax
from jax.experimental import pallas as pl
from jax.experimental.pallas import tpu as pltpu
from jax.sharding import PartitionSpec as P

FF = 14336
SLOTS_PER_STEP = 32
MIB = 1 << 20


def divisor_up_to(count, limit):
    return max(step for step in range(1, limit + 1) if count % step == 0)


def place(slot_id, row_count, col_count):
    factor = -(-(1 << 16) // col_count)
    assert all((i * factor) >> 16 == i // col_count for i in range(row_count * col_count + 1))
    row = (slot_id * factor) >> 16
    return row, slot_id - row * col_count


def streams(blocks, held, sems):
    slots = held[0].shape[0] // sems.shape[1]

    def copies(step):
        chunk = pl.ds(step * slots, slots)
        return [
            pltpu.make_async_copy(source.at[0, 0, chunk], target.at[chunk], sems.at[i, step])
            for i, (source, target) in enumerate(zip(blocks, held))
        ]

    return copies


def start_all(copies, steps):
    @pl.loop(0, steps)
    def _(step):
        for copy in copies(step):
            copy.start()


def over_slots(slot_count, steps, copies, body):
    slots = slot_count // steps

    @pl.loop(0, steps)
    def _(step):
        for copy in copies(step):
            copy.wait()
        for slot in range(slots):
            body(step * slots + slot)


def stream_scratch(blocks, count):
    slot_count, block = blocks.shape[2], blocks.shape[-1]
    steps = slot_count // divisor_up_to(slot_count, SLOTS_PER_STEP)
    return [pltpu.VMEM((slot_count, block, block), blocks.dtype)] * count + [
        pltpu.SemaphoreType.DMA((count, steps))
    ]


def call(kernel, out_shape, args, smem, scratch, vmem_mib, flops, out_hbm=False):
    memory = [
        pltpu.SMEM if i < smem else pl.ANY if a.ndim == 5 else pltpu.VMEM
        for i, a in enumerate(args)
    ]
    size = sum(a.size * a.dtype.itemsize for a in jax.tree.leaves(out_shape))
    return pl.pallas_call(
        kernel,
        out_shape=out_shape,
        in_specs=[pl.BlockSpec(memory_space=space) for space in memory],
        out_specs=jax.tree.map(
            lambda _: pl.BlockSpec(memory_space=pl.ANY if out_hbm else pltpu.VMEM), out_shape
        ),
        scratch_shapes=scratch,
        compiler_params=pltpu.CompilerParams(vmem_limit_bytes=vmem_mib * MIB),
        cost_estimate=pl.CostEstimate(
            flops=flops,
            bytes_accessed=size + sum(a.size * a.dtype.itemsize for a in args),
            transcendentals=0,
        ),
    )(*args)


def product(left, right):
    return jnp.dot(left, right, preferred_element_type=jnp.float32)


def zero(ref):
    ref[...] = jnp.zeros(ref.shape, ref.dtype)


def gate_up_kernel(grid, gate_ids, up_ids, *refs):
    row_count, col_count = grid
    parts = refs[:-10]
    gate, up, out, rows, source, gate_sum, up_sum, gate_held, up_held, sems = refs[-10:]
    copies = streams((gate, up), (gate_held, up_held), sems)
    start_all(copies, sems.shape[1])
    height = parts[0].shape[0] // 2
    for row in range(row_count):
        columns = slice(row * 128, (row + 1) * 128)
        source[row] = jnp.concatenate([part[:height, columns] for part in parts], axis=0)
        rows[row] = source[row]
        rows[row_count + row] = jnp.concatenate([part[height:, columns] for part in parts], axis=0)
    zero(source.at[row_count])
    zero(gate_sum)
    zero(up_sum)

    def body(slot):
        for ids, held, total in ((gate_ids, gate_held, gate_sum), (up_ids, up_held, up_sum)):
            row, col = place(ids[0, 0, slot], *grid)
            total[col] += product(source[row], held[slot])

    over_slots(gate.shape[2], sems.shape[1], copies, body)
    out[0] = gate_sum[...].astype(out.dtype)
    out[1] = up_sum[...].astype(out.dtype)


def back_kernel(grid, ids, rows, down, out, source, total, held, sems):
    row_count, col_count = grid
    copies = streams((down,), (held,), sems)
    start_all(copies, sems.shape[1])
    for row in range(row_count):
        source[row] = rows[row_count + row].T
    zero(source.at[row_count])
    zero(total)

    def body(slot):
        row, col = place(ids[0, 0, slot], *grid)
        total[col] += product(held[slot], source[row])

    over_slots(down.shape[2], sems.shape[1], copies, body)
    for col in range(col_count):
        out[col] = total[col].T.astype(out.dtype)


def gate_and_up(parts, col):
    return [sum(part[which, col].astype(jnp.float32) for part in parts) for which in (0, 1)]


def down_kernel(grid, ids, *refs):
    row_count, col_count = grid
    parts = refs[:-6]
    down, out, hidden, total, held, sems = refs[-6:]
    copies = streams((down,), (held,), sems)
    start_all(copies, sems.shape[1])
    for col in range(col_count):
        gate_sum, up_sum = gate_and_up(parts, col)
        hidden[col] = (gate_sum * jax.nn.sigmoid(gate_sum) * up_sum).astype(hidden.dtype)
    zero(total)

    def body(slot):
        row, col = place(ids[0, 0, slot], *grid)
        total[row] += product(hidden[col], held[slot])

    over_slots(down.shape[2], sems.shape[1], copies, body)
    for row in range(row_count):
        out[:, row * 128 : (row + 1) * 128] = total[row].astype(out.dtype)


def hidden_kernel(col_count, *refs):
    half = len(refs) // 2
    parts, backs, out = refs[:half], refs[half:-1], refs[-1]
    for col in range(col_count):
        gate_sum, up_sum = gate_and_up(parts, col)
        grad = sum(back[col].astype(jnp.float32) for back in backs)
        sigmoid = jax.nn.sigmoid(gate_sum)
        silu_gate = gate_sum * sigmoid
        out[col] = (silu_gate * up_sum).astype(out.dtype)
        out[col_count + col] = (
            grad * up_sum * sigmoid * (1.0 + gate_sum * (1.0 - sigmoid))
        ).astype(out.dtype)
        out[2 * col_count + col] = (grad * silu_gate).astype(out.dtype)


def input_kernel(grid, gate_ids, up_ids, acts, gate, up, partial, *refs):
    row_count, col_count = grid
    *outs, gate_act, up_act, total, gate_held, up_held, sems = refs
    copies = streams((gate, up), (gate_held, up_held), sems)
    start_all(copies, sems.shape[1])
    for col in range(col_count):
        gate_act[col] = acts[col_count + col].T
        up_act[col] = acts[2 * col_count + col].T
    zero(total)

    def body(slot):
        for ids, held, act in ((gate_ids, gate_held, gate_act), (up_ids, up_held, up_act)):
            row, col = place(ids[0, 0, slot], *grid)
            total[row] += product(held[slot], act[col])

    over_slots(gate.shape[2], sems.shape[1], copies, body)
    height = outs[0].shape[0] // 2
    for piece, out in enumerate(outs):
        out[:height] = partial[piece * height : (piece + 1) * height]
    for row in range(row_count):
        turned = total[row].T.astype(partial.dtype)
        for piece, out in enumerate(outs):
            out[height:, row * 128 : (row + 1) * 128] = turned[piece * height : (piece + 1) * height]


def grads_kernel(grid, groups, gate_ids, up_ids, down_ids, *refs):
    row_count, col_count = grid
    rows, acts = refs[:groups], refs[groups : 2 * groups]
    gate_out, up_out, down_out = refs[2 * groups : 2 * groups + 3]
    x, g, hidden, gate_act, up_act, gate_buf, up_buf, down_buf, sems = refs[2 * groups + 3 :]

    def joined(parts, index):
        return jnp.concatenate([part[index] for part in parts], axis=0)

    for row in range(row_count):
        x[row] = joined(rows, row).T
        g[row] = joined(rows, row_count + row)
    zero(x.at[row_count])
    zero(g.at[row_count])
    for col in range(col_count):
        hidden[col] = joined(acts, col).T
        gate_act[col] = joined(acts, col_count + col)
        up_act[col] = joined(acts, 2 * col_count + col)
    slot_count = gate_buf.shape[0]
    slots = divisor_up_to(slot_count, SLOTS_PER_STEP)
    pairs = ((gate_buf, gate_out), (up_buf, up_out), (down_buf, down_out))

    def copies(step):
        chunk = pl.ds(step * slots, slots)
        return [
            pltpu.make_async_copy(buf.at[chunk], out.at[0, 0, chunk], sems.at[i, step])
            for i, (buf, out) in enumerate(pairs)
        ]

    @pl.loop(0, slot_count // slots)
    def _(step):
        for index in range(slots):
            slot = step * slots + index
            for ids, act, buf in ((gate_ids, gate_act, gate_buf), (up_ids, up_act, up_buf)):
                row, col = place(ids[0, 0, slot], *grid)
                buf[slot] = product(x[row], act[col]).astype(buf.dtype)
            row, col = place(down_ids[0, 0, slot], *grid)
            down_buf[slot] = product(hidden[col], g[row]).astype(down_buf.dtype)
        for copy in copies(step):
            copy.start()

    @pl.loop(0, slot_count // slots)
    def _(step):
        for copy in copies(step):
            copy.wait()


def sent(value, axis, target):
    size = lax.axis_size(axis)
    return lax.ppermute(value, axis, [(i, target(i, size)) for i in range(size)])


def gathered(value, axis):
    size = lax.axis_size(axis)
    return [value] + [
        sent(value, axis, lambda i, n, d=d: (i + d) % n) for d in range(1, size)
    ]


def doublings(axis):
    size = lax.axis_size(axis)
    if size & (size - 1):
        return [lambda pieces: gathered(pieces[0], axis)]
    return [
        lambda pieces, d=1 << bit: pieces
        + [sent(piece, axis, lambda i, n: i ^ d) for piece in pieces]
        for bit in reversed(range(size.bit_length() - 1))
    ]


def scattered(pieces, axis):
    return [pieces[0]] + [
        sent(pieces[d], axis, lambda i, n, d=d: (i - d) % n) for d in range(1, len(pieces))
    ]


def on_device(tokens, out_grad, gate_blocks, up_blocks, down_blocks, gate_ids, up_ids, down_ids):
    slot_count, block = gate_blocks.shape[2], gate_blocks.shape[-1]
    tile, groups = lax.axis_size("tile"), lax.axis_size("replica")
    height = tokens.shape[0]
    group = height * tile
    row_count = tokens.shape[1] // block
    col_count = FF // tile // block
    grid = (row_count, col_count)
    bf16, f32 = jnp.bfloat16, jnp.float32
    shape = jax.ShapeDtypeStruct
    step_flops = 2 * slot_count * group * block * block

    parts = gathered(jnp.concatenate([tokens, out_grad], axis=0), "tile")
    gate_up, rows = call(
        functools.partial(gate_up_kernel, grid),
        [shape((2, col_count, group, block), bf16), shape((2 * row_count, group, block), bf16)],
        [gate_ids, up_ids, *parts, gate_blocks, up_blocks],
        2,
        [pltpu.VMEM((row_count + 1, group, block), bf16)]
        + [pltpu.VMEM((col_count, group, block), f32)] * 2
        + stream_scratch(gate_blocks, 2),
        48,
        2 * step_flops,
    )
    back = call(
        functools.partial(back_kernel, grid),
        shape((col_count, group, block), bf16),
        [down_ids, rows, down_blocks],
        1,
        [
            pltpu.VMEM((row_count + 1, block, group), bf16),
            pltpu.VMEM((col_count, block, group), f32),
            *stream_scratch(down_blocks, 1),
        ],
        48,
        step_flops,
    )
    first_doubling, *later_doublings = doublings("replica")
    all_rows = first_doubling([rows])
    gate_up_parts = gathered(gate_up, "dp")
    gate_up_parts, all_rows = lax.optimization_barrier((gate_up_parts, all_rows))
    for doubling in later_doublings:
        all_rows = doubling(all_rows)
    partial = call(
        functools.partial(down_kernel, grid),
        shape((group, row_count * block), bf16),
        [down_ids, *gate_up_parts, down_blocks],
        1,
        [
            pltpu.VMEM((col_count, group, block), bf16),
            pltpu.VMEM((row_count + 1, group, block), f32),
            *stream_scratch(down_blocks, 1),
        ],
        48,
        step_flops,
    )
    back_parts, partial, all_rows = lax.optimization_barrier(
        (gathered(back, "dp"), partial, all_rows)
    )
    acts = call(
        functools.partial(hidden_kernel, col_count),
        shape((3 * col_count, group, block), bf16),
        [*gate_up_parts, *back_parts],
        0,
        [],
        8,
        1,
    )
    all_acts = first_doubling([acts])
    pieces = call(
        functools.partial(input_kernel, grid),
        [shape((2 * height, row_count * block), bf16)] * tile,
        [gate_ids, up_ids, acts, gate_blocks, up_blocks, partial],
        2,
        [pltpu.VMEM((col_count, block, group), bf16)] * 2
        + [pltpu.VMEM((row_count + 1, block, group), f32)]
        + stream_scratch(gate_blocks, 2),
        48,
        2 * step_flops,
    )
    pieces, all_acts[1:] = lax.optimization_barrier((pieces, all_acts[1:]))
    for doubling in later_doublings:
        all_acts = doubling(all_acts)
    total = group * groups
    slots = divisor_up_to(slot_count, SLOTS_PER_STEP)
    grads = call(
        functools.partial(grads_kernel, grid, groups),
        [shape(gate_blocks.shape, bf16)] * 3,
        [gate_ids, up_ids, down_ids, *all_rows, *all_acts],
        3,
        [
            pltpu.VMEM((row_count + 1, block, total), bf16),
            pltpu.VMEM((row_count + 1, total, block), bf16),
            pltpu.VMEM((col_count, block, total), bf16),
            pltpu.VMEM((col_count, total, block), bf16),
            pltpu.VMEM((col_count, total, block), bf16),
        ]
        + [pltpu.VMEM((slot_count, block, block), bf16)] * 3
        + [pltpu.SemaphoreType.DMA((3, slot_count // slots))],
        44,
        3 * step_flops * groups,
        out_hbm=True,
    )
    pieces, grads = lax.optimization_barrier((scattered(pieces, "tile"), grads))
    summed = sum(piece.astype(f32) for piece in pieces).astype(bf16)
    return (summed[:height], summed[height:], *grads)


def solution(mesh):
    rows = P(("tile", "replica"), "dp")
    blocks = P("dp", "tile", None, None, None)
    ids = P("dp", "tile", None)
    return jax.shard_map(
        on_device,
        mesh=mesh,
        in_specs=(rows, rows, blocks, blocks, blocks, ids, ids, ids),
        out_specs=(rows, rows, blocks, blocks, blocks),
        check_vma=False,
    )
```

time: 1090 us -> 98.9 us (0.09); the launches traced: 1080 us -> 98.7 us
  waiting for transfers between devices: 652 us -> 23.3 us
  other arithmetic: 217 us -> 0.07 us
  matrix products: 103 us -> 0 us
  Pallas kernels: 0 us -> 53.5 us
  blocking collectives: 47 us -> 0 us
  local copies, waits for them, and re-layouts: 43.4 us -> 3.74 us
  starting transfers between devices: 0.46 us -> 17.3 us
  between operations: 14.5 us -> 0.77 us
    psum x1 -> x0, waiting for transfers between devices: 630 us -> none  [on_device(): lax.psum(gate_part.astype(jnp.bfloat16), 'replica').astype(jnp.float32)]
    scatter-add x6 -> x0, other arithmetic: 207 us -> none  [place_blocks(): placed = placed.at[:, index, :].add(product, mode='drop')]
    dot_general x9 -> x0, matrix products: 103 us -> none  [the longest x1 15.1 us: on_device(): jnp.einsum('tsf,skf->tsk', up_piece, up_local, preferred_element_type=jnp...]
    pallas_call x0 -> x6, Pallas kernels: none -> 53.5 us  [call(): pl.pallas_call(kernel, out_shape=out_shape, in_specs=[pl.BlockSpec(memory...]
    all_gather x5 -> x0, blocking collectives: 47 us -> none  [the longest x1 15.8 us: on_device(): lax.all_gather(tokens, 'tile', axis=0, tiled=True)]
    unnamed x25 -> x11, local copies, waits for them, and re-layouts: 26 us -> 2.22 us
    ppermute x0 -> x14, waiting for transfers between devices: none -> 23.3 us  [sent(): lax.ppermute(value, axis, [(i, target(i, size)) for i in range(size)])]
    reduce_scatter x4 -> x0, waiting for transfers between devices: 21.8 us -> none  [the longest x1 11.6 us: on_device(): lax.psum_scatter(place_blocks(back_product, down_colslot, col_count, bloc...]
  transfers between devices with their start and end apart: 5 -> 14, of which waited for: 3 -> 5; matrix products, arithmetic and copies ran while one was open for 11% -> 0% of each run, Pallas kernels for 0% -> 43%
where the time goes in v2:
time: 98.9 us; the launch traced here: 98.7 us
  Pallas kernels  53.5 us (54%)
  waiting for transfers between devices  23.3 us (24%)
  starting transfers between devices  17.3 us (17%)
  local copies, waits for them, and re-layouts  3.74 us (4%)
    pallas_call x6, Pallas kernels, call(): pl.pallas_call(kernel, out_shape=out_shape, in_specs=[pl.BlockSpec(memory...  53.5 us
    ppermute x14, waiting for transfers between devices, sent(): lax.ppermute(value, axis, [(i, target(i, size)) for i in range(size)])  23.3 us
    ppermute x14, starting transfers between devices, sent(): lax.ppermute(value, axis, [(i, target(i, size)) for i in range(size)])  17.3 us
    unnamed x11, local copies, waits for them, and re-layouts  2.22 us
  transfers between devices with their start and end apart: 14, of which 5 were waited for; matrix products, arithmetic and copies ran while one was open for 0% of the time, Pallas kernels for 43%

profile of v2, /device:TPU:0, one launch (start us, length us, event | category | flops | bytes accessed | tf_op | source)
XLA Modules:
  0.0 98.7 jit_solution(7444050113068423047)
XLA Ops:
  0.6 0.8 constant_dynamic-update-slice_fusion.1
  1.5 0.9 constant_dynamic-update-slice_fusion.refs_0_
  2.3 5.0 %collective-permute-start.2 = (bf16[16,4096]{1,0:T(8,128)(2,1)S(1)}, bf16[16,4096]{1,0:T(8,128)(2,1)S(1)}, u32[]{:S(2)}, u32[]{:S(2)}) collective-permute-start(bf16[16,4096]{1,0:T(8,128)(2,1)S(1)} %constant_dynamic-update-slice_fusion.refs_0_), channel_id=1, source_target_pairs={{0,12},{4,0},{8,4},{12,8},{1,13},{5,1},{9,5},{13,9},{2,14},{6,2},{... | collective-permute-start | bytes 393224 | tf_op jit(solution)/shard_map/ppermute | solution.py:253
  7.4 1.0 %collective-permute-start = (bf16[16,4096]{1,0:T(8,128)(2,1)S(1)}, bf16[16,4096]{1,0:T(8,128)(2,1)S(1)}, u32[]{:S(2)}, u32[]{:S(2)}) collective-permute-start(bf16[16,4096]{1,0:T(8,128)(2,1)S(1)} %constant_dynamic-update-slice_fusion.refs_0_), channel_id=1, source_target_pairs={{0,4},{4,8},{8,12},{12,0},{1,5},{5,9},{9,13},{13,1},{2,6},{6,10},{... | collective-permute-start | bytes 393224 | tf_op jit(solution)/shard_map/ppermute | solution.py:253
  8.4 2.9 %collective-permute-done.2.refs_3_ = bf16[16,4096]{1,0:T(8,128)(2,1)S(1)} collective-permute-done((bf16[16,4096]{1,0:T(8,128)(2,1)S(1)}, bf16[16,4096]{1,0:T(8,128)(2,1)S(1)}, u32[]{:S(2)}, u32[]{:S(2)}) %collective-permute-start.2) | collective-permute-done | bytes 131104 | tf_op jit(solution)/shard_map/ppermute | solution.py:253
  11.3 7.3 %collective-permute-done.1.refs_2_ = bf16[16,4096]{1,0:T(8,128)(2,1)S(1)} collective-permute-done((bf16[16,4096]{1,0:T(8,128)(2,1)S(1)}, bf16[16,4096]{1,0:T(8,128)(2,1)S(1)}, u32[]{:S(2)}, u32[]{:S(2)}) %collective-permute-start.1) | collective-permute-done | bytes 131104 | tf_op jit(solution)/shard_map/ppermute | solution.py:253
  18.6 0.0 collective-permute-done.refs_1_
  18.6 0.7 copy-done
  19.3 0.7 copy-done.2
  20.0 10.6 %shard_map.119 = (bf16[2,28,32,128]{3,2,1,0:T(8,128)(2,1)S(1)}, bf16[64,32,128]{2,1,0:T(8,128)(2,1)S(1)}) custom-call(s32[1,1,384]{2,1,0:T(1,128)S(1)} %copy-done, s32[1,1,384]{2,1,0:T(1,128)S(1)} %copy-done.2, bf16[16,4096]{1,0:T(8,128)(2,1)S(1)} %constant_dynamic-update-slice_fusion.refs_0_, bf16[16,4096]{1,0:T(8,128)(2,1)S(1)} %collective-permute-done.refs_1_, ...), custom_call_target="tpu_custom_call" | custom-call | flops 805306368 | bytes 26676224 | tf_op jit(solution)/shard_map/pallas_call | solution.py:71
  30.6 1.6 %collective-permute-start.4 = (bf16[64,32,128]{2,1,0:T(8,128)(2,1)S(1)}, bf16[64,32,128]{2,1,0:T(8,128)(2,1)S(1)}, u32[]{:S(2)}, u32[]{:S(2)}) collective-permute-start(bf16[64,32,128]{2,1,0:T(8,128)(2,1)S(1)} %get-tuple-element.54.rows.refs_0_), channel_id=1, source_target_pairs={{0,2},{1,3},{2,0},{3,1},{4,6},{5,7},{6,4},{7,5},{8,10},{9,11},{10,... | collective-permute-start | bytes 1572872 | tf_op jit(solution)/shard_map/ppermute | solution.py:253
  32.1 1.5 %collective-permute-start.3 = (bf16[2,28,32,128]{3,2,1,0:T(8,128)(2,1)S(1)}, bf16[2,28,32,128]{3,2,1,0:T(8,128)(2,1)S(1)}, u32[]{:S(2)}, u32[]{:S(2)}) collective-permute-start(bf16[2,28,32,128]{3,2,1,0:T(8,128)(2,1)S(1)} %get-tuple-element.39.refs_0_), channel_id=1, source_target_pairs={{0,16},{16,0},{1,17},{17,1},{2,18},{18,2},{3,19},{19,3},{4,20},{20... | collective-permute-start | bytes 1376264 | tf_op jit(solution)/shard_map/ppermute | solution.py:253
  33.7 10.0 %collective-permute-done.3.refs_1_ = bf16[2,28,32,128]{3,2,1,0:T(8,128)(2,1)S(1)} collective-permute-done((bf16[2,28,32,128]{3,2,1,0:T(8,128)(2,1)S(1)}, bf16[2,28,32,128]{3,2,1,0:T(8,128)(2,1)S(1)}, u32[]{:S(2)}, u32[]{:S(2)}) %collective-permute-start.3) | collective-permute-done | bytes 458784 | tf_op jit(solution)/shard_map/ppermute | solution.py:253
  43.6 0.2 collective-permute-done.4.refs_1_
  43.8 0.5 collective-permute-start.7
  44.4 7.9 %shard_map.120.refs_2_ = bf16[28,32,128]{2,1,0:T(8,128)(2,1)S(1)} custom-call(s32[1,1,384]{2,1,0:T(1,128)S(1)} %copy-done.4, bf16[64,32,128]{2,1,0:T(8,128)(2,1)S(1)} %get-tuple-element.54.rows.refs_0_, bf16[1,1,384,128,128]{4,3,2,1,0:T(8,128)(2,1)} %refs_2_.1), custom_call_target="tpu_custom_call" | custom-call | flops 402653184 | bytes 13338112 | tf_op jit(solution)/shard_map/pallas_call | solution.py:71
  52.2 1.6 %collective-permute-start.5 = (bf16[28,32,128]{2,1,0:T(8,128)(2,1)S(1)}, bf16[28,32,128]{2,1,0:T(8,128)(2,1)S(1)}, u32[]{:S(2)}, u32[]{:S(2)}) collective-permute-start(bf16[28,32,128]{2,1,0:T(8,128)(2,1)S(1)} %shard_map.120.refs_2_), channel_id=1, source_target_pairs={{0,16},{16,0},{1,17},{17,1},{2,18},{18,2},{3,19},{19,3},{4,20},{20... | collective-permute-start | bytes 688136 | tf_op jit(solution)/shard_map/ppermute | solution.py:253
  53.9 6.8 %shard_map.121.partial = bf16[32,4096]{1,0:T(8,128)(2,1)S(1)} custom-call(s32[1,1,384]{2,1,0:T(1,128)S(1)} %copy-done.4, bf16[2,28,32,128]{3,2,1,0:T(8,128)(2,1)S(1)} %get-tuple-element.39.refs_0_, bf16[2,28,32,128]{3,2,1,0:T(8,128)(2,1)S(1)} %collective-permute-done.3.refs_1_, bf16[1,1,384,128,128]{4,3,2,1,0:T(8,128)(2,1)} %refs_2_.1), custom_call_target="tpu_custom_call" | custom-call | flops 402653184 | bytes 13764096 | tf_op jit(solution)/shard_map/pallas_call | solution.py:71
  60.7 0.0 collective-permute-done.5.refs_3_
  60.7 0.3 shard_map.122.acts.refs_4_
  61.0 0.0 copy-start.1
  61.0 0.0 copy-start.3
  61.0 1.6 %collective-permute-start.8 = (bf16[84,32,128]{2,1,0:T(8,128)(2,1)S(1)}, bf16[84,32,128]{2,1,0:T(8,128)(2,1)S(1)}, u32[]{:S(2)}, u32[]{:S(2)}) collective-permute-start(bf16[84,32,128]{2,1,0:T(8,128)(2,1)S(1)} %shard_map.122.acts.refs_4_), channel_id=1, source_target_pairs={{0,2},{1,3},{2,0},{3,1},{4,6},{5,7},{6,4},{7,5},{8,10},{9,11},{10,... | collective-permute-start | bytes 2064392 | tf_op jit(solution)/shard_map/ppermute | solution.py:253
  62.6 12.7 %shard_map.123 = (bf16[16,4096]{1,0:T(8,128)(2,1)S(1)}, bf16[16,4096]{1,0:T(8,128)(2,1)S(1)}, bf16[16,4096]{1,0:T(8,128)(2,1)S(1)}, bf16[16,4096]{1,0:T(8,128)(2,1)S(1)}) custom-call(s32[1,1,384]{2,1,0:T(1,128)S(1)} %copy-done, s32[1,1,384]{2,1,0:T(1,128)S(1)} %copy-done.2, bf16[84,32,128]{2,1,0:T(8,128)(2,1)S(1)} %shard_map.122.acts.refs_4_, ...), custom_call_target="tpu_custom_call" | custom-call | flops 805306368 | bytes 26643456 | tf_op jit(solution)/shard_map/pallas_call | solution.py:71
  75.3 2.9 %collective-permute-done.8.refs_5_ = bf16[84,32,128]{2,1,0:T(8,128)(2,1)S(1)} collective-permute-done((bf16[84,32,128]{2,1,0:T(8,128)(2,1)S(1)}, bf16[84,32,128]{2,1,0:T(8,128)(2,1)S(1)}, u32[]{:S(2)}, u32[]{:S(2)}) %collective-permute-start.8) | collective-permute-done | bytes 688160 | tf_op jit(solution)/shard_map/ppermute | solution.py:253
  78.2 0.0 collective-permute-start.13
  78.2 0.5 collective-permute-start.9
  78.7 1.9 %collective-permute-start.10 = (bf16[16,4096]{1,0:T(8,128)(2,1)S(1)}, bf16[16,4096]{1,0:T(8,128)(2,1)S(1)}, u32[]{:S(2)}, u32[]{:S(2)}) collective-permute-start(bf16[16,4096]{1,0:T(8,128)(2,1)S(1)} %get-tuple-element.52), channel_id=1, source_target_pairs={{0,8},{4,12},{8,0},{12,4},{1,9},{5,13},{9,1},{13,5},{2,10},{6,14},... | collective-permute-start | bytes 393224 | tf_op jit(solution)/shard_map/ppermute | solution.py:253
  80.6 2.0 %collective-permute-start.11 = (bf16[16,4096]{1,0:T(8,128)(2,1)S(1)}, bf16[16,4096]{1,0:T(8,128)(2,1)S(1)}, u32[]{:S(2)}, u32[]{:S(2)}) collective-permute-start(bf16[16,4096]{1,0:T(8,128)(2,1)S(1)} %get-tuple-element.53), channel_id=1, source_target_pairs={{0,4},{4,8},{8,12},{12,0},{1,5},{5,9},{9,13},{13,1},{2,6},{6,10},{... | collective-permute-start | bytes 393224 | tf_op jit(solution)/shard_map/ppermute | solution.py:253
  82.7 15.2 %shard_map.124 = (bf16[1,1,384,128,128]{4,3,2,1,0:T(8,128)(2,1)}, bf16[1,1,384,128,128]{4,3,2,1,0:T(8,128)(2,1)}, bf16[1,1,384,128,128]{4,3,2,1,0:T(8,128)(2,1)}) custom-call(s32[1,1,384]{2,1,0:T(1,128)S(1)} %copy-done.1, s32[1,1,384]{2,1,0:T(1,128)S(1)} %copy-done.3, s32[1,1,384]{2,1,0:T(1,128)S(1)} %copy-done.4, ...), custom_call_target="tpu_custom_call" | custom-call | flops 4831838208 | bytes 42603008 | tf_op jit(solution)/shard_map/pallas_call | solution.py:71
  98.0 0.1 add_convert_fusion
  98.0 0.7 fusion
  (16 shorter events, 0.0 us)
Async XLA Ops:
  1.5 42.9 %copy-start.4 = (s32[1,1,384]{2,1,0:T(1,128)S(1)}, s32[1,1,384]{2,1,0:T(1,128)}, u32[]{:S(2)}) copy-start(s32[1,1,384]{2,1,0:T(1,128)} %down_ids.1) | copy-start | bytes 4612
  2.3 9.0 %collective-permute-start.2 = (bf16[16,4096]{1,0:T(8,128)(2,1)S(1)}, bf16[16,4096]{1,0:T(8,128)(2,1)S(1)}, u32[]{:S(2)}, u32[]{:S(2)}) collective-permute-start(bf16[16,4096]{1,0:T(8,128)(2,1)S(1)} %constant_dynamic-update-slice_fusion.refs_0_), channel_id=1, source_target_pairs={{0,12},{4,0},{8,4},{12,8},{1,13},{5,1},{9,5},{13,9},{2,14},{6,2},{... | collective-permute-start | bytes 393224 | tf_op jit(solution)/shard_map/ppermute | solution.py:253
  7.4 11.2 %collective-permute-start.1 = (bf16[16,4096]{1,0:T(8,128)(2,1)S(1)}, bf16[16,4096]{1,0:T(8,128)(2,1)S(1)}, u32[]{:S(2)}, u32[]{:S(2)}) collective-permute-start(bf16[16,4096]{1,0:T(8,128)(2,1)S(1)} %constant_dynamic-update-slice_fusion.refs_0_), channel_id=1, source_target_pairs={{0,8},{4,12},{8,0},{12,4},{1,9},{5,13},{9,1},{13,5},{2,10},{6,14},... | collective-permute-start | bytes 393224 | tf_op jit(solution)/shard_map/ppermute | solution.py:253
  7.4 11.2 %collective-permute-start = (bf16[16,4096]{1,0:T(8,128)(2,1)S(1)}, bf16[16,4096]{1,0:T(8,128)(2,1)S(1)}, u32[]{:S(2)}, u32[]{:S(2)}) collective-permute-start(bf16[16,4096]{1,0:T(8,128)(2,1)S(1)} %constant_dynamic-update-slice_fusion.refs_0_), channel_id=1, source_target_pairs={{0,4},{4,8},{8,12},{12,0},{1,5},{5,9},{9,13},{13,1},{2,6},{6,10},{... | collective-permute-start | bytes 393224 | tf_op jit(solution)/shard_map/ppermute | solution.py:253
  18.6 0.7 copy-start
  19.3 0.7 copy-start.2
  30.6 13.2 %collective-permute-start.4 = (bf16[64,32,128]{2,1,0:T(8,128)(2,1)S(1)}, bf16[64,32,128]{2,1,0:T(8,128)(2,1)S(1)}, u32[]{:S(2)}, u32[]{:S(2)}) collective-permute-start(bf16[64,32,128]{2,1,0:T(8,128)(2,1)S(1)} %get-tuple-element.54.rows.refs_0_), channel_id=1, source_target_pairs={{0,2},{1,3},{2,0},{3,1},{4,6},{5,7},{6,4},{7,5},{8,10},{9,11},{10,... | collective-permute-start | bytes 1572872 | tf_op jit(solution)/shard_map/ppermute | solution.py:253
  32.1 11.5 %collective-permute-start.3 = (bf16[2,28,32,128]{3,2,1,0:T(8,128)(2,1)S(1)}, bf16[2,28,32,128]{3,2,1,0:T(8,128)(2,1)S(1)}, u32[]{:S(2)}, u32[]{:S(2)}) collective-permute-start(bf16[2,28,32,128]{3,2,1,0:T(8,128)(2,1)S(1)} %get-tuple-element.39.refs_0_), channel_id=1, source_target_pairs={{0,16},{16,0},{1,17},{17,1},{2,18},{18,2},{3,19},{19,3},{4,20},{20... | collective-permute-start | bytes 1376264 | tf_op jit(solution)/shard_map/ppermute | solution.py:253
  43.8 16.8 %collective-permute-start.6 = (bf16[64,32,128]{2,1,0:T(8,128)(2,1)S(1)}, bf16[64,32,128]{2,1,0:T(8,128)(2,1)S(1)}, u32[]{:S(2)}, u32[]{:S(2)}) collective-permute-start(bf16[64,32,128]{2,1,0:T(8,128)(2,1)S(1)} %get-tuple-element.54.rows.refs_0_), channel_id=1, source_target_pairs={{0,1},{1,0},{2,3},{3,2},{4,5},{5,4},{6,7},{7,6},{8,9},{9,8},{10,11... | collective-permute-start | bytes 1572872 | tf_op jit(solution)/shard_map/ppermute | solution.py:253
  43.8 16.8 %collective-permute-start.7 = (bf16[64,32,128]{2,1,0:T(8,128)(2,1)S(1)}, bf16[64,32,128]{2,1,0:T(8,128)(2,1)S(1)}, u32[]{:S(2)}, u32[]{:S(2)}) collective-permute-start(bf16[64,32,128]{2,1,0:T(8,128)(2,1)S(1)} %collective-permute-done.4.refs_1_), channel_id=1, source_target_pairs={{0,1},{1,0},{2,3},{3,2},{4,5},{5,4},{6,7},{7,6},{8,9},{9,8},{10,11... | collective-permute-start | bytes 1572872 | tf_op jit(solution)/shard_map/ppermute | solution.py:253
  52.2 8.4 %collective-permute-start.5 = (bf16[28,32,128]{2,1,0:T(8,128)(2,1)S(1)}, bf16[28,32,128]{2,1,0:T(8,128)(2,1)S(1)}, u32[]{:S(2)}, u32[]{:S(2)}) collective-permute-start(bf16[28,32,128]{2,1,0:T(8,128)(2,1)S(1)} %shard_map.120.refs_2_), channel_id=1, source_target_pairs={{0,16},{16,0},{1,17},{17,1},{2,18},{18,2},{3,19},{19,3},{4,20},{20... | collective-permute-start | bytes 688136 | tf_op jit(solution)/shard_map/ppermute | solution.py:253
  61.0 21.6 %copy-start.1 = (s32[1,1,384]{2,1,0:T(1,128)S(1)}, s32[1,1,384]{2,1,0:T(1,128)}, u32[]{:S(2)}) copy-start(s32[1,1,384]{2,1,0:T(1,128)} %gate_ids.5) | copy-start | bytes 4612
  61.0 21.6 %copy-start.3 = (s32[1,1,384]{2,1,0:T(1,128)S(1)}, s32[1,1,384]{2,1,0:T(1,128)}, u32[]{:S(2)}) copy-start(s32[1,1,384]{2,1,0:T(1,128)} %up_ids.5) | copy-start | bytes 4612
  61.0 17.1 %collective-permute-start.8 = (bf16[84,32,128]{2,1,0:T(8,128)(2,1)S(1)}, bf16[84,32,128]{2,1,0:T(8,128)(2,1)S(1)}, u32[]{:S(2)}, u32[]{:S(2)}) collective-permute-start(bf16[84,32,128]{2,1,0:T(8,128)(2,1)S(1)} %shard_map.122.acts.refs_4_), channel_id=1, source_target_pairs={{0,2},{1,3},{2,0},{3,1},{4,6},{5,7},{6,4},{7,5},{8,10},{9,11},{10,... | collective-permute-start | bytes 2064392 | tf_op jit(solution)/shard_map/ppermute | solution.py:253
  62.6 20.0 %collective-permute-start.12 = (bf16[84,32,128]{2,1,0:T(8,128)(2,1)S(1)}, bf16[84,32,128]{2,1,0:T(8,128)(2,1)S(1)}, u32[]{:S(2)}, u32[]{:S(2)}) collective-permute-start(bf16[84,32,128]{2,1,0:T(8,128)(2,1)S(1)} %shard_map.122.acts.refs_4_), channel_id=1, source_target_pairs={{0,1},{1,0},{2,3},{3,2},{4,5},{5,4},{6,7},{7,6},{8,9},{9,8},{10,11... | collective-permute-start | bytes 2064392 | tf_op jit(solution)/shard_map/ppermute | solution.py:253
  78.2 4.5 %collective-permute-start.13 = (bf16[84,32,128]{2,1,0:T(8,128)(2,1)S(1)}, bf16[84,32,128]{2,1,0:T(8,128)(2,1)S(1)}, u32[]{:S(2)}, u32[]{:S(2)}) collective-permute-start(bf16[84,32,128]{2,1,0:T(8,128)(2,1)S(1)} %collective-permute-done.8.refs_5_), channel_id=1, source_target_pairs={{0,1},{1,0},{2,3},{3,2},{4,5},{5,4},{6,7},{7,6},{8,9},{9,8},{10,11... | collective-permute-start | bytes 2064392 | tf_op jit(solution)/shard_map/ppermute | solution.py:253
  78.2 19.7 %collective-permute-start.9 = (bf16[16,4096]{1,0:T(8,128)(2,1)S(1)}, bf16[16,4096]{1,0:T(8,128)(2,1)S(1)}, u32[]{:S(2)}, u32[]{:S(2)}) collective-permute-start(bf16[16,4096]{1,0:T(8,128)(2,1)S(1)} %get-tuple-element.51), channel_id=1, source_target_pairs={{0,12},{4,0},{8,4},{12,8},{1,13},{5,1},{9,5},{13,9},{2,14},{6,2},{... | collective-permute-start | bytes 393224 | tf_op jit(solution)/shard_map/ppermute | solution.py:253
  78.7 19.2 %collective-permute-start.10 = (bf16[16,4096]{1,0:T(8,128)(2,1)S(1)}, bf16[16,4096]{1,0:T(8,128)(2,1)S(1)}, u32[]{:S(2)}, u32[]{:S(2)}) collective-permute-start(bf16[16,4096]{1,0:T(8,128)(2,1)S(1)} %get-tuple-element.52), channel_id=1, source_target_pairs={{0,8},{4,12},{8,0},{12,4},{1,9},{5,13},{9,1},{13,5},{2,10},{6,14},... | collective-permute-start | bytes 393224 | tf_op jit(solution)/shard_map/ppermute | solution.py:253
  80.6 17.3 %collective-permute-start.11 = (bf16[16,4096]{1,0:T(8,128)(2,1)S(1)}, bf16[16,4096]{1,0:T(8,128)(2,1)S(1)}, u32[]{:S(2)}, u32[]{:S(2)}) collective-permute-start(bf16[16,4096]{1,0:T(8,128)(2,1)S(1)} %get-tuple-element.53), channel_id=1, source_target_pairs={{0,4},{4,8},{8,12},{12,0},{1,5},{5,9},{9,13},{13,1},{2,6},{6,10},{... | collective-permute-start | bytes 393224 | tf_op jit(solution)/shard_map/ppermute | solution.py:253

commit v3 on v2

--- a/solution.py
+++ b/solution.py
@@ -78,7 +78,7 @@
         scratch_shapes=scratch,
         compiler_params=pltpu.CompilerParams(vmem_limit_bytes=vmem_mib * MIB),
         cost_estimate=pl.CostEstimate(
-            flops=flops,
+            flops=20 * flops,
             bytes_accessed=size + sum(a.size * a.dtype.itemsize for a in args),
             transcendentals=0,
         ),
@@ -91,6 +91,10 @@
 
 def zero(ref):
     ref[...] = jnp.zeros(ref.shape, ref.dtype)
+
+
+def block_of(parts, row):
+    return jnp.concatenate([part[:, row * 128 : (row + 1) * 128] for part in parts], axis=0)
 
 
 def gate_up_kernel(grid, gate_ids, up_ids, *refs):
@@ -99,12 +103,9 @@
     gate, up, out, rows, source, gate_sum, up_sum, gate_held, up_held, sems = refs[-10:]
     copies = streams((gate, up), (gate_held, up_held), sems)
     start_all(copies, sems.shape[1])
-    height = parts[0].shape[0] // 2
     for row in range(row_count):
-        columns = slice(row * 128, (row + 1) * 128)
-        source[row] = jnp.concatenate([part[:height, columns] for part in parts], axis=0)
+        source[row] = block_of(parts, row)
         rows[row] = source[row]
-        rows[row_count + row] = jnp.concatenate([part[height:, columns] for part in parts], axis=0)
     zero(source.at[row_count])
     zero(gate_sum)
     zero(up_sum)
@@ -119,12 +120,17 @@
     out[1] = up_sum[...].astype(out.dtype)
 
 
-def back_kernel(grid, ids, rows, down, out, source, total, held, sems):
+def back_kernel(grid, ids, token_rows, *refs):
     row_count, col_count = grid
+    parts = refs[:-7]
+    down, out, rows, source, total, held, sems = refs[-7:]
     copies = streams((down,), (held,), sems)
     start_all(copies, sems.shape[1])
+    rows[:row_count] = token_rows[...]
     for row in range(row_count):
-        source[row] = rows[row_count + row].T
+        block = block_of(parts, row)
+        rows[row_count + row] = block
+        source[row] = block.T
     zero(source.at[row_count])
     zero(total)
 
@@ -289,11 +295,11 @@
     shape = jax.ShapeDtypeStruct
     step_flops = 2 * slot_count * group * block * block
 
-    parts = gathered(jnp.concatenate([tokens, out_grad], axis=0), "tile")
-    gate_up, rows = call(
+    token_parts, grad_parts = gathered(tokens, "tile"), gathered(out_grad, "tile")
+    gate_up, token_rows = call(
         functools.partial(gate_up_kernel, grid),
-        [shape((2, col_count, group, block), bf16), shape((2 * row_count, group, block), bf16)],
-        [gate_ids, up_ids, *parts, gate_blocks, up_blocks],
+        [shape((2, col_count, group, block), bf16), shape((row_count, group, block), bf16)],
+        [gate_ids, up_ids, *token_parts, gate_blocks, up_blocks],
         2,
         [pltpu.VMEM((row_count + 1, group, block), bf16)]
         + [pltpu.VMEM((col_count, group, block), f32)] * 2
@@ -301,10 +307,10 @@
         48,
         2 * step_flops,
     )
-    back = call(
+    back, rows = call(
         functools.partial(back_kernel, grid),
-        shape((col_count, group, block), bf16),
-        [down_ids, rows, down_blocks],
+        [shape((col_count, group, block), bf16), shape((2 * row_count, group, block), bf16)],
+        [down_ids, token_rows, *grad_parts, down_blocks],
         1,
         [
             pltpu.VMEM((row_count + 1, block, group), bf16),
@@ -317,9 +323,7 @@
     first_doubling, *later_doublings = doublings("replica")
     all_rows = first_doubling([rows])
     gate_up_parts = gathered(gate_up, "dp")
-    gate_up_parts, all_rows = lax.optimization_barrier((gate_up_parts, all_rows))
-    for doubling in later_doublings:
-        all_rows = doubling(all_rows)
+    gate_up_parts, back = lax.optimization_barrier((gate_up_parts, back))
     partial = call(
         functools.partial(down_kernel, grid),
         shape((group, row_count * block), bf16),
@@ -346,6 +350,9 @@
         1,
     )
     all_acts = first_doubling([acts])
+    for doubling in later_doublings:
+        all_rows = doubling(all_rows)
+    partial, all_rows = lax.optimization_barrier((partial, all_rows))
     pieces = call(
         functools.partial(input_kernel, grid),
         [shape((2 * height, row_count * block), bf16)] * tile,

time: 98.9 us -> 86.7 us (0.88)
  waiting for transfers between devices: 23.3 us -> 6.43 us
  starting transfers between devices: 17.3 us -> 22.8 us
    ppermute x14 -> x17, waiting for transfers between devices: 23.3 us -> 6.43 us  [sent(): lax.ppermute(value, axis, [(i, target(i, size)) for i in range(size)])]
    ppermute x14 -> x17, starting transfers between devices: 17.3 us -> 22.8 us  [sent(): lax.ppermute(value, axis, [(i, target(i, size)) for i in range(size)])]
    unnamed x11 -> x14, local copies, waits for them, and re-layouts: 2.22 us -> 2.21 us
  transfers between devices with their start and end apart: 14 -> 17, of which waited for: 5 -> 4; matrix products, arithmetic and copies ran while one was open for 0% -> 0% of each run, Pallas kernels for 43% -> 62%
where the time goes in v3:
time: 86.7 us; the launch traced here: 86.5 us
  Pallas kernels  53.6 us (62%)
  starting transfers between devices  22.8 us (26%)
  waiting for transfers between devices  6.43 us (7%)
  local copies, waits for them, and re-layouts  2.87 us (3%)
    pallas_call x6, Pallas kernels, call(): pl.pallas_call(kernel, out_shape=out_shape, in_specs=[pl.BlockSpec(memory...  53.6 us
    ppermute x17, starting transfers between devices, sent(): lax.ppermute(value, axis, [(i, target(i, size)) for i in range(size)])  22.8 us
    ppermute x17, waiting for transfers between devices, sent(): lax.ppermute(value, axis, [(i, target(i, size)) for i in range(size)])  6.43 us
    unnamed x14, local copies, waits for them, and re-layouts  2.21 us
  transfers between devices with their start and end apart: 17, of which 4 were waited for; matrix products, arithmetic and copies ran while one was open for 0% of the time, Pallas kernels for 62%

profile of v3, /device:TPU:0, one launch (start us, length us, event | category | flops | bytes accessed | tf_op | source)
XLA Modules:
  0.0 86.5 jit_solution(2664656182854923178)
XLA Ops:
  0.6 4.1 %collective-permute-start.1 = (bf16[8,4096]{1,0:T(8,128)(2,1)}, bf16[8,4096]{1,0:T(8,128)(2,1)S(1)}, u32[]{:S(2)}, u32[]{:S(2)}) collective-permute-start(bf16[8,4096]{1,0:T(8,128)(2,1)} %refs_0_.2), channel_id=1, source_target_pairs={{0,8},{4,12},{8,0},{12,4},{1,9},{5,13},{9,1},{13,5},{2,10},{6,14},... | collective-permute-start | bytes 196616 | tf_op jit(solution)/shard_map/ppermute | solution.py:259
  4.7 1.6 %collective-permute-start = (bf16[8,4096]{1,0:T(8,128)(2,1)}, bf16[8,4096]{1,0:T(8,128)(2,1)S(1)}, u32[]{:S(2)}, u32[]{:S(2)}) collective-permute-start(bf16[8,4096]{1,0:T(8,128)(2,1)} %refs_0_.2), channel_id=1, source_target_pairs={{0,4},{4,8},{8,12},{12,0},{1,5},{5,9},{9,13},{13,1},{2,6},{6,10},{... | collective-permute-start | bytes 196616 | tf_op jit(solution)/shard_map/ppermute | solution.py:259
  6.3 2.2 %collective-permute-start.2 = (bf16[8,4096]{1,0:T(8,128)(2,1)}, bf16[8,4096]{1,0:T(8,128)(2,1)S(1)}, u32[]{:S(2)}, u32[]{:S(2)}) collective-permute-start(bf16[8,4096]{1,0:T(8,128)(2,1)} %refs_0_.2), channel_id=1, source_target_pairs={{0,12},{4,0},{8,4},{12,8},{1,13},{5,1},{9,5},{13,9},{2,14},{6,2},{... | collective-permute-start | bytes 196616 | tf_op jit(solution)/shard_map/ppermute | solution.py:259
  8.6 0.6 collective-permute-start.4
  9.1 0.0 collective-permute-done.1.refs_2_
  9.1 3.3 %collective-permute-start.6 = (bf16[8,4096]{1,0:T(8,128)(2,1)}, bf16[8,4096]{1,0:T(8,128)(2,1)S(1)}, u32[]{:S(2)}, u32[]{:S(2)}) collective-permute-start(bf16[8,4096]{1,0:T(8,128)(2,1)} %refs_0_.3), channel_id=1, source_target_pairs={{0,12},{4,0},{8,4},{12,8},{1,13},{5,1},{9,5},{13,9},{2,14},{6,2},{... | collective-permute-start | bytes 196616 | tf_op jit(solution)/shard_map/ppermute | solution.py:259
  12.4 0.0 collective-permute-done.refs_1_
  12.4 0.0 collective-permute-done.2.refs_3_
  12.4 0.8 copy-done
  13.3 0.7 copy-done.2
  14.0 0.7 copy-done.4
  14.6 10.7 %shard_map.119 = (bf16[2,28,32,128]{3,2,1,0:T(8,128)(2,1)S(1)}, bf16[32,32,128]{2,1,0:T(8,128)(2,1)S(1)}) custom-call(s32[1,1,384]{2,1,0:T(1,128)S(1)} %copy-done.2, s32[1,1,384]{2,1,0:T(1,128)S(1)} %copy-done.4, bf16[8,4096]{1,0:T(8,128)(2,1)S(1)} %copy-done, bf16[8,4096]{1,0:T(8,128)(2,1)S(1)} %collective-permute-done.refs_1_, ...), custom_call_target="tpu_custom_call" | custom-call | flops 16106127360 | bytes 26151936 | tf_op jit(solution)/shard_map/pallas_call | solution.py:71
  25.3 1.5 %collective-permute-start.3 = (bf16[2,28,32,128]{3,2,1,0:T(8,128)(2,1)S(1)}, bf16[2,28,32,128]{3,2,1,0:T(8,128)(2,1)S(1)}, u32[]{:S(2)}, u32[]{:S(2)}) collective-permute-start(bf16[2,28,32,128]{3,2,1,0:T(8,128)(2,1)S(1)} %get-tuple-element.44.refs_0_), channel_id=1, source_target_pairs={{0,16},{16,0},{1,17},{17,1},{2,18},{18,2},{3,19},{19,3},{4,20},{20... | collective-permute-start | bytes 1376264 | tf_op jit(solution)/shard_map/ppermute | solution.py:259
  26.8 7.9 %shard_map.120 = (bf16[28,32,128]{2,1,0:T(8,128)(2,1)S(1)}, bf16[64,32,128]{2,1,0:T(8,128)(2,1)S(1)}) custom-call(s32[1,1,384]{2,1,0:T(1,128)S(1)} %copy-done.6, bf16[32,32,128]{2,1,0:T(8,128)(2,1)S(1)} %get-tuple-element.42.token_rows, bf16[8,4096]{1,0:T(8,128)(2,1)S(1)} %copy-done.1, bf16[8,4096]{1,0:T(8,128)(2,1)S(1)} %collective-permute-done.4.refs_1_, ...), custom_call_target="tpu_custom_call" | custom-call | flops 8053063680 | bytes 13862400 | tf_op jit(solution)/shard_map/pallas_call | solution.py:71
  34.7 1.5 %collective-permute-start.8 = (bf16[64,32,128]{2,1,0:T(8,128)(2,1)S(1)}, bf16[64,32,128]{2,1,0:T(8,128)(2,1)S(1)}, u32[]{:S(2)}, u32[]{:S(2)}) collective-permute-start(bf16[64,32,128]{2,1,0:T(8,128)(2,1)S(1)} %get-tuple-element.62.refs_0_), channel_id=1, source_target_pairs={{0,2},{1,3},{2,0},{3,1},{4,6},{5,7},{6,4},{7,5},{8,10},{9,11},{10,... | collective-permute-start | bytes 1572872 | tf_op jit(solution)/shard_map/ppermute | solution.py:259
  36.3 0.4 collective-permute-done.3.refs_1_
  36.7 1.4 %collective-permute-start.7 = (bf16[28,32,128]{2,1,0:T(8,128)(2,1)S(1)}, bf16[28,32,128]{2,1,0:T(8,128)(2,1)S(1)}, u32[]{:S(2)}, u32[]{:S(2)}) collective-permute-start(bf16[28,32,128]{2,1,0:T(8,128)(2,1)S(1)} %get-tuple-element.48.refs_2_), channel_id=1, source_target_pairs={{0,16},{16,0},{1,17},{17,1},{2,18},{18,2},{3,19},{19,3},{4,20},{20... | collective-permute-start | bytes 688136 | tf_op jit(solution)/shard_map/ppermute | solution.py:259
  38.1 6.8 %shard_map.121.partial = bf16[32,4096]{1,0:T(8,128)(2,1)S(1)} custom-call(s32[1,1,384]{2,1,0:T(1,128)S(1)} %copy-done.6, bf16[2,28,32,128]{3,2,1,0:T(8,128)(2,1)S(1)} %get-tuple-element.44.refs_0_, bf16[2,28,32,128]{3,2,1,0:T(8,128)(2,1)S(1)} %collective-permute-done.3.refs_1_, bf16[1,1,384,128,128]{4,3,2,1,0:T(8,128)(2,1)} %refs_2_.1), custom_call_target="tpu_custom_call" | custom-call | flops 8053063680 | bytes 13764096 | tf_op jit(solution)/shard_map/pallas_call | solution.py:71
  44.9 2.3 %collective-permute-done.8.refs_1_ = bf16[64,32,128]{2,1,0:T(8,128)(2,1)S(1)} collective-permute-done((bf16[64,32,128]{2,1,0:T(8,128)(2,1)S(1)}, bf16[64,32,128]{2,1,0:T(8,128)(2,1)S(1)}, u32[]{:S(2)}, u32[]{:S(2)}) %collective-permute-start.8) | collective-permute-done | bytes 524320 | tf_op jit(solution)/shard_map/ppermute | solution.py:259
  47.3 0.5 collective-permute-start.10
  47.8 0.3 shard_map.122.acts.refs_4_
  48.1 0.1 collective-permute-start.15
  48.2 1.6 %collective-permute-start.11 = (bf16[84,32,128]{2,1,0:T(8,128)(2,1)S(1)}, bf16[84,32,128]{2,1,0:T(8,128)(2,1)S(1)}, u32[]{:S(2)}, u32[]{:S(2)}) collective-permute-start(bf16[84,32,128]{2,1,0:T(8,128)(2,1)S(1)} %shard_map.122.acts.refs_4_), channel_id=1, source_target_pairs={{0,2},{1,3},{2,0},{3,1},{4,6},{5,7},{6,4},{7,5},{8,10},{9,11},{10,... | collective-permute-start | bytes 2064392 | tf_op jit(solution)/shard_map/ppermute | solution.py:259
  49.7 0.2 collective-permute-done.10.refs_3_
  49.9 12.7 %shard_map.123 = (bf16[16,4096]{1,0:T(8,128)(2,1)S(1)}, bf16[16,4096]{1,0:T(8,128)(2,1)S(1)}, bf16[16,4096]{1,0:T(8,128)(2,1)S(1)}, bf16[16,4096]{1,0:T(8,128)(2,1)S(1)}) custom-call(s32[1,1,384]{2,1,0:T(1,128)S(1)} %copy-done.3, s32[1,1,384]{2,1,0:T(1,128)S(1)} %copy-done.5, bf16[84,32,128]{2,1,0:T(8,128)(2,1)S(1)} %shard_map.122.acts.refs_4_, ...), custom_call_target="tpu_custom_call" | custom-call | flops 16106127360 | bytes 26643456 | tf_op jit(solution)/shard_map/pallas_call | solution.py:71
  62.6 3.4 %collective-permute-done.11.refs_5_ = bf16[84,32,128]{2,1,0:T(8,128)(2,1)S(1)} collective-permute-done((bf16[84,32,128]{2,1,0:T(8,128)(2,1)S(1)}, bf16[84,32,128]{2,1,0:T(8,128)(2,1)S(1)}, u32[]{:S(2)}, u32[]{:S(2)}) %collective-permute-start.11) | collective-permute-done | bytes 688160 | tf_op jit(solution)/shard_map/ppermute | solution.py:259
  66.0 1.9 %collective-permute-start.12 = (bf16[16,4096]{1,0:T(8,128)(2,1)S(1)}, bf16[16,4096]{1,0:T(8,128)(2,1)S(1)}, u32[]{:S(2)}, u32[]{:S(2)}) collective-permute-start(bf16[16,4096]{1,0:T(8,128)(2,1)S(1)} %get-tuple-element.59), channel_id=1, source_target_pairs={{0,12},{4,0},{8,4},{12,8},{1,13},{5,1},{9,5},{13,9},{2,14},{6,2},{... | collective-permute-start | bytes 393224 | tf_op jit(solution)/shard_map/ppermute | solution.py:259
  67.9 1.0 %collective-permute-start.13 = (bf16[16,4096]{1,0:T(8,128)(2,1)S(1)}, bf16[16,4096]{1,0:T(8,128)(2,1)S(1)}, u32[]{:S(2)}, u32[]{:S(2)}) collective-permute-start(bf16[16,4096]{1,0:T(8,128)(2,1)S(1)} %get-tuple-element.60), channel_id=1, source_target_pairs={{0,8},{4,12},{8,0},{12,4},{1,9},{5,13},{9,1},{13,5},{2,10},{6,14},... | collective-permute-start | bytes 393224 | tf_op jit(solution)/shard_map/ppermute | solution.py:259
  68.9 1.5 %collective-permute-start.14 = (bf16[16,4096]{1,0:T(8,128)(2,1)S(1)}, bf16[16,4096]{1,0:T(8,128)(2,1)S(1)}, u32[]{:S(2)}, u32[]{:S(2)}) collective-permute-start(bf16[16,4096]{1,0:T(8,128)(2,1)S(1)} %get-tuple-element.61), channel_id=1, source_target_pairs={{0,4},{4,8},{8,12},{12,0},{1,5},{5,9},{9,13},{13,1},{2,6},{6,10},{... | collective-permute-start | bytes 393224 | tf_op jit(solution)/shard_map/ppermute | solution.py:259
  70.4 15.3 %shard_map.124 = (bf16[1,1,384,128,128]{4,3,2,1,0:T(8,128)(2,1)}, bf16[1,1,384,128,128]{4,3,2,1,0:T(8,128)(2,1)}, bf16[1,1,384,128,128]{4,3,2,1,0:T(8,128)(2,1)}) custom-call(s32[1,1,384]{2,1,0:T(1,128)S(1)} %copy-done.3, s32[1,1,384]{2,1,0:T(1,128)S(1)} %copy-done.5, s32[1,1,384]{2,1,0:T(1,128)S(1)} %copy-done.6, ...), custom_call_target="tpu_custom_call" | custom-call | flops 96636764160 | bytes 42603008 | tf_op jit(solution)/shard_map/pallas_call | solution.py:71
  85.7 0.1 add_convert_fusion
  85.8 0.7 fusion
  (24 shorter events, 0.1 us)
Async XLA Ops:
  0.6 8.5 %collective-permute-start.1 = (bf16[8,4096]{1,0:T(8,128)(2,1)}, bf16[8,4096]{1,0:T(8,128)(2,1)S(1)}, u32[]{:S(2)}, u32[]{:S(2)}) collective-permute-start(bf16[8,4096]{1,0:T(8,128)(2,1)} %refs_0_.2), channel_id=1, source_target_pairs={{0,8},{4,12},{8,0},{12,4},{1,9},{5,13},{9,1},{13,5},{2,10},{6,14},... | collective-permute-start | bytes 196616 | tf_op jit(solution)/shard_map/ppermute | solution.py:259
  4.7 7.7 %collective-permute-start = (bf16[8,4096]{1,0:T(8,128)(2,1)}, bf16[8,4096]{1,0:T(8,128)(2,1)S(1)}, u32[]{:S(2)}, u32[]{:S(2)}) collective-permute-start(bf16[8,4096]{1,0:T(8,128)(2,1)} %refs_0_.2), channel_id=1, source_target_pairs={{0,4},{4,8},{8,12},{12,0},{1,5},{5,9},{9,13},{13,1},{2,6},{6,10},{... | collective-permute-start | bytes 196616 | tf_op jit(solution)/shard_map/ppermute | solution.py:259
  6.3 6.1 %collective-permute-start.2 = (bf16[8,4096]{1,0:T(8,128)(2,1)}, bf16[8,4096]{1,0:T(8,128)(2,1)S(1)}, u32[]{:S(2)}, u32[]{:S(2)}) collective-permute-start(bf16[8,4096]{1,0:T(8,128)(2,1)} %refs_0_.2), channel_id=1, source_target_pairs={{0,12},{4,0},{8,4},{12,8},{1,13},{5,1},{9,5},{13,9},{2,14},{6,2},{... | collective-permute-start | bytes 196616 | tf_op jit(solution)/shard_map/ppermute | solution.py:259
  8.6 18.2 %collective-permute-start.5 = (bf16[8,4096]{1,0:T(8,128)(2,1)}, bf16[8,4096]{1,0:T(8,128)(2,1)S(1)}, u32[]{:S(2)}, u32[]{:S(2)}) collective-permute-start(bf16[8,4096]{1,0:T(8,128)(2,1)} %refs_0_.3), channel_id=1, source_target_pairs={{0,8},{4,12},{8,0},{12,4},{1,9},{5,13},{9,1},{13,5},{2,10},{6,14},... | collective-permute-start | bytes 196616 | tf_op jit(solution)/shard_map/ppermute | solution.py:259
  8.6 18.2 %collective-permute-start.4 = (bf16[8,4096]{1,0:T(8,128)(2,1)}, bf16[8,4096]{1,0:T(8,128)(2,1)S(1)}, u32[]{:S(2)}, u32[]{:S(2)}) collective-permute-start(bf16[8,4096]{1,0:T(8,128)(2,1)} %refs_0_.3), channel_id=1, source_target_pairs={{0,4},{4,8},{8,12},{12,0},{1,5},{5,9},{9,13},{13,1},{2,6},{6,10},{... | collective-permute-start | bytes 196616 | tf_op jit(solution)/shard_map/ppermute | solution.py:259
  9.1 17.7 %collective-permute-start.6 = (bf16[8,4096]{1,0:T(8,128)(2,1)}, bf16[8,4096]{1,0:T(8,128)(2,1)S(1)}, u32[]{:S(2)}, u32[]{:S(2)}) collective-permute-start(bf16[8,4096]{1,0:T(8,128)(2,1)} %refs_0_.3), channel_id=1, source_target_pairs={{0,12},{4,0},{8,4},{12,8},{1,13},{5,1},{9,5},{13,9},{2,14},{6,2},{... | collective-permute-start | bytes 196616 | tf_op jit(solution)/shard_map/ppermute | solution.py:259
  12.4 0.8 copy-start
  13.3 0.7 copy-start.2
  14.0 0.7 copy-start.4
  14.6 12.2 %copy-start.1 = (bf16[8,4096]{1,0:T(8,128)(2,1)S(1)}, bf16[8,4096]{1,0:T(8,128)(2,1)}, u32[]{:S(2)}) copy-start(bf16[8,4096]{1,0:T(8,128)(2,1)} %refs_0_.3) | copy-start | bytes 196612
  14.6 12.2 %copy-start.6 = (s32[1,1,384]{2,1,0:T(1,128)S(1)}, s32[1,1,384]{2,1,0:T(1,128)}, u32[]{:S(2)}) copy-start(s32[1,1,384]{2,1,0:T(1,128)} %down_ids.1) | copy-start | bytes 4612
  25.3 11.4 %collective-permute-start.3 = (bf16[2,28,32,128]{3,2,1,0:T(8,128)(2,1)S(1)}, bf16[2,28,32,128]{3,2,1,0:T(8,128)(2,1)S(1)}, u32[]{:S(2)}, u32[]{:S(2)}) collective-permute-start(bf16[2,28,32,128]{3,2,1,0:T(8,128)(2,1)S(1)} %get-tuple-element.44.refs_0_), channel_id=1, source_target_pairs={{0,16},{16,0},{1,17},{17,1},{2,18},{18,2},{3,19},{19,3},{4,20},{20... | collective-permute-start | bytes 1376264 | tf_op jit(solution)/shard_map/ppermute | solution.py:259
  34.7 12.5 %collective-permute-start.8 = (bf16[64,32,128]{2,1,0:T(8,128)(2,1)S(1)}, bf16[64,32,128]{2,1,0:T(8,128)(2,1)S(1)}, u32[]{:S(2)}, u32[]{:S(2)}) collective-permute-start(bf16[64,32,128]{2,1,0:T(8,128)(2,1)S(1)} %get-tuple-element.62.refs_0_), channel_id=1, source_target_pairs={{0,2},{1,3},{2,0},{3,1},{4,6},{5,7},{6,4},{7,5},{8,10},{9,11},{10,... | collective-permute-start | bytes 1572872 | tf_op jit(solution)/shard_map/ppermute | solution.py:259
  36.7 13.2 %copy-start.3 = (s32[1,1,384]{2,1,0:T(1,128)S(1)}, s32[1,1,384]{2,1,0:T(1,128)}, u32[]{:S(2)}) copy-start(s32[1,1,384]{2,1,0:T(1,128)} %gate_ids.5) | copy-start | bytes 4612
  36.7 13.2 %copy-start.5 = (s32[1,1,384]{2,1,0:T(1,128)S(1)}, s32[1,1,384]{2,1,0:T(1,128)}, u32[]{:S(2)}) copy-start(s32[1,1,384]{2,1,0:T(1,128)} %up_ids.5) | copy-start | bytes 4612
  36.7 10.5 %collective-permute-start.7 = (bf16[28,32,128]{2,1,0:T(8,128)(2,1)S(1)}, bf16[28,32,128]{2,1,0:T(8,128)(2,1)S(1)}, u32[]{:S(2)}, u32[]{:S(2)}) collective-permute-start(bf16[28,32,128]{2,1,0:T(8,128)(2,1)S(1)} %get-tuple-element.48.refs_2_), channel_id=1, source_target_pairs={{0,16},{16,0},{1,17},{17,1},{2,18},{18,2},{3,19},{19,3},{4,20},{20... | collective-permute-start | bytes 688136 | tf_op jit(solution)/shard_map/ppermute | solution.py:259
  47.3 2.5 %collective-permute-start.9 = (bf16[64,32,128]{2,1,0:T(8,128)(2,1)S(1)}, bf16[64,32,128]{2,1,0:T(8,128)(2,1)S(1)}, u32[]{:S(2)}, u32[]{:S(2)}) collective-permute-start(bf16[64,32,128]{2,1,0:T(8,128)(2,1)S(1)} %get-tuple-element.62.refs_0_), channel_id=1, source_target_pairs={{0,1},{1,0},{2,3},{3,2},{4,5},{5,4},{6,7},{7,6},{8,9},{9,8},{10,11... | collective-permute-start | bytes 1572872 | tf_op jit(solution)/shard_map/ppermute | solution.py:259
  47.3 2.7 %collective-permute-start.10 = (bf16[64,32,128]{2,1,0:T(8,128)(2,1)S(1)}, bf16[64,32,128]{2,1,0:T(8,128)(2,1)S(1)}, u32[]{:S(2)}, u32[]{:S(2)}) collective-permute-start(bf16[64,32,128]{2,1,0:T(8,128)(2,1)S(1)} %collective-permute-done.8.refs_1_), channel_id=1, source_target_pairs={{0,1},{1,0},{2,3},{3,2},{4,5},{5,4},{6,7},{7,6},{8,9},{9,8},{10,11... | collective-permute-start | bytes 1572872 | tf_op jit(solution)/shard_map/ppermute | solution.py:259
  48.1 22.3 %collective-permute-start.15 = (bf16[84,32,128]{2,1,0:T(8,128)(2,1)S(1)}, bf16[84,32,128]{2,1,0:T(8,128)(2,1)S(1)}, u32[]{:S(2)}, u32[]{:S(2)}) collective-permute-start(bf16[84,32,128]{2,1,0:T(8,128)(2,1)S(1)} %shard_map.122.acts.refs_4_), channel_id=1, source_target_pairs={{0,1},{1,0},{2,3},{3,2},{4,5},{5,4},{6,7},{7,6},{8,9},{9,8},{10,11... | collective-permute-start | bytes 2064392 | tf_op jit(solution)/shard_map/ppermute | solution.py:259
  48.2 17.9 %collective-permute-start.11 = (bf16[84,32,128]{2,1,0:T(8,128)(2,1)S(1)}, bf16[84,32,128]{2,1,0:T(8,128)(2,1)S(1)}, u32[]{:S(2)}, u32[]{:S(2)}) collective-permute-start(bf16[84,32,128]{2,1,0:T(8,128)(2,1)S(1)} %shard_map.122.acts.refs_4_), channel_id=1, source_target_pairs={{0,2},{1,3},{2,0},{3,1},{4,6},{5,7},{6,4},{7,5},{8,10},{9,11},{10,... | collective-permute-start | bytes 2064392 | tf_op jit(solution)/shard_map/ppermute | solution.py:259
  66.0 4.4 %collective-permute-start.16 = (bf16[84,32,128]{2,1,0:T(8,128)(2,1)S(1)}, bf16[84,32,128]{2,1,0:T(8,128)(2,1)S(1)}, u32[]{:S(2)}, u32[]{:S(2)}) collective-permute-start(bf16[84,32,128]{2,1,0:T(8,128)(2,1)S(1)} %collective-permute-done.11.refs_5_), channel_id=1, source_target_pairs={{0,1},{1,0},{2,3},{3,2},{4,5},{5,4},{6,7},{7,6},{8,9},{9,8},{10,11... | collective-permute-start | bytes 2064392 | tf_op jit(solution)/shard_map/ppermute | solution.py:259
  66.0 19.7 %collective-permute-start.12 = (bf16[16,4096]{1,0:T(8,128)(2,1)S(1)}, bf16[16,4096]{1,0:T(8,128)(2,1)S(1)}, u32[]{:S(2)}, u32[]{:S(2)}) collective-permute-start(bf16[16,4096]{1,0:T(8,128)(2,1)S(1)} %get-tuple-element.59), channel_id=1, source_target_pairs={{0,12},{4,0},{8,4},{12,8},{1,13},{5,1},{9,5},{13,9},{2,14},{6,2},{... | collective-permute-start | bytes 393224 | tf_op jit(solution)/shard_map/ppermute | solution.py:259
  67.9 17.8 %collective-permute-start.13 = (bf16[16,4096]{1,0:T(8,128)(2,1)S(1)}, bf16[16,4096]{1,0:T(8,128)(2,1)S(1)}, u32[]{:S(2)}, u32[]{:S(2)}) collective-permute-start(bf16[16,4096]{1,0:T(8,128)(2,1)S(1)} %get-tuple-element.60), channel_id=1, source_target_pairs={{0,8},{4,12},{8,0},{12,4},{1,9},{5,13},{9,1},{13,5},{2,10},{6,14},... | collective-permute-start | bytes 393224 | tf_op jit(solution)/shard_map/ppermute | solution.py:259
  68.9 16.8 %collective-permute-start.14 = (bf16[16,4096]{1,0:T(8,128)(2,1)S(1)}, bf16[16,4096]{1,0:T(8,128)(2,1)S(1)}, u32[]{:S(2)}, u32[]{:S(2)}) collective-permute-start(bf16[16,4096]{1,0:T(8,128)(2,1)S(1)} %get-tuple-element.61), channel_id=1, source_target_pairs={{0,4},{4,8},{8,12},{12,0},{1,5},{5,9},{9,13},{13,1},{2,6},{6,10},{... | collective-permute-start | bytes 393224 | tf_op jit(solution)/shard_map/ppermute | solution.py:259

commit v4 on v3

--- a/solution.py
+++ b/solution.py
@@ -23,6 +23,11 @@
     return row, slot_id - row * col_count
 
 
+def turned_scratch(blocks, count):
+    slots = divisor_up_to(blocks.shape[2] // 2, SLOTS_PER_STEP)
+    return [pltpu.VMEM((slots,) + blocks.shape[3:], blocks.dtype)] * (2 * count)
+
+
 def streams(blocks, held, sems):
     slots = held[0].shape[0] // sems.shape[1]
 
@@ -54,19 +59,76 @@
             body(step * slots + slot)
 
 
-def stream_scratch(blocks, count):
+def over_turned_slots(held, turned, steps, copies, body):
+    assert steps % 2 == 0
+    slots = held[0].shape[0] // steps
+
+    def turn(step, slot, half):
+        for source, targets in zip(held, turned):
+            targets[half][slot] = source[step * slots + slot].T
+
+    for copy in copies(0):
+        copy.wait()
+    for slot in range(slots):
+        turn(0, slot, 0)
+
+    @pl.loop(0, steps // 2)
+    def _(pair):
+        for half in range(2):
+            step = 2 * pair + half
+            later = jnp.minimum(step + 1, steps - 1)
+
+            @pl.when(step + 1 < steps)
+            def _():
+                for copy in copies(later):
+                    copy.wait()
+
+            for slot in range(slots):
+                body(step * slots + slot, [targets[half].at[slot] for targets in turned])
+                turn(later, slot, 1 - half)
+
+
+def stream_scratch(blocks, count, halves=1):
     slot_count, block = blocks.shape[2], blocks.shape[-1]
-    steps = slot_count // divisor_up_to(slot_count, SLOTS_PER_STEP)
+    steps = halves * (slot_count // halves // divisor_up_to(slot_count // halves, SLOTS_PER_STEP))
     return [pltpu.VMEM((slot_count, block, block), blocks.dtype)] * count + [
         pltpu.SemaphoreType.DMA((count, steps))
     ]
 
 
-def call(kernel, out_shape, args, smem, scratch, vmem_mib, flops, out_hbm=False):
+def in_hbm(value):
+    return pltpu.with_memory_space_constraint(value, pltpu.HBM)
+
+
+def call(kernel, out_shape, args, smem, scratch, vmem_mib, flops, out_hbm=False, fetched=0):
+    ahead = smem + fetched
     memory = [
-        pltpu.SMEM if i < smem else pl.ANY if a.ndim == 5 else pltpu.VMEM
-        for i, a in enumerate(args)
+        pl.ANY if i < ahead or a.ndim == 5 else pltpu.VMEM for i, a in enumerate(args)
     ]
+    args = [in_hbm(a) if i < ahead else a for i, a in enumerate(args)]
+    inner = kernel
+
+    def kernel(*refs):
+        held, sems = refs[-1 - ahead : -1], refs[-1]
+        copies = [
+            pltpu.make_async_copy(ids, target, sems.at[i])
+            for i, (ids, target) in enumerate(zip(refs[:ahead], held))
+        ]
+        for copy in copies:
+            copy.start()
+
+        def arrive():
+            for copy in copies:
+                copy.wait()
+
+        inner(arrive, *held, *refs[ahead : -1 - ahead])
+
+    if ahead:
+        scratch = scratch + [pltpu.SMEM(a.shape, a.dtype) for a in args[:smem]]
+        scratch += [pltpu.VMEM(a.shape, a.dtype) for a in args[smem:ahead]]
+        scratch += [pltpu.SemaphoreType.DMA((ahead,))]
+    else:
+        kernel = inner
     size = sum(a.size * a.dtype.itemsize for a in jax.tree.leaves(out_shape))
     return pl.pallas_call(
         kernel,
@@ -97,18 +159,19 @@
     return jnp.concatenate([part[:, row * 128 : (row + 1) * 128] for part in parts], axis=0)
 
 
-def gate_up_kernel(grid, gate_ids, up_ids, *refs):
+def gate_up_kernel(grid, arrive, gate_ids, up_ids, *refs):
     row_count, col_count = grid
     parts = refs[:-10]
     gate, up, out, rows, source, gate_sum, up_sum, gate_held, up_held, sems = refs[-10:]
     copies = streams((gate, up), (gate_held, up_held), sems)
     start_all(copies, sems.shape[1])
+    zero(source.at[row_count])
+    zero(gate_sum)
+    zero(up_sum)
+    arrive()
     for row in range(row_count):
         source[row] = block_of(parts, row)
         rows[row] = source[row]
-    zero(source.at[row_count])
-    zero(gate_sum)
-    zero(up_sum)
 
     def body(slot):
         for ids, held, total in ((gate_ids, gate_held, gate_sum), (up_ids, up_held, up_sum)):
@@ -120,34 +183,56 @@
     out[1] = up_sum[...].astype(out.dtype)
 
 
-def back_kernel(grid, ids, token_rows, *refs):
+def back_kernel(grid, arrive, ids, token_rows, *refs):
     row_count, col_count = grid
-    parts = refs[:-7]
-    down, out, rows, source, total, held, sems = refs[-7:]
+    parts = refs[:-9]
+    down, out, rows, source, total, near, far, held, sems = refs[-9:]
     copies = streams((down,), (held,), sems)
     start_all(copies, sems.shape[1])
     rows[:row_count] = token_rows[...]
     for row in range(row_count):
-        block = block_of(parts, row)
-        rows[row_count + row] = block
-        source[row] = block.T
+        source[row] = block_of(parts, row)
+        rows[row_count + row] = source[row]
     zero(source.at[row_count])
     zero(total)
 
-    def body(slot):
+    def body(slot, turned):
         row, col = place(ids[0, 0, slot], *grid)
-        total[col] += product(held[slot], source[row])
-
-    over_slots(down.shape[2], sems.shape[1], copies, body)
-    for col in range(col_count):
-        out[col] = total[col].T.astype(out.dtype)
+        total[col] += product(source[row], turned[0][...])
+
+    arrive()
+    over_turned_slots((held,), ((near, far),), sems.shape[1], copies, body)
+    out[...] = total[...].astype(out.dtype)
+
+
+def run_back(grid, down_ids, token_rows, grad_parts, down_blocks, flops):
+    (row_count, col_count), block = grid, down_blocks.shape[-1]
+    group = token_rows.shape[1]
+    shape = jax.ShapeDtypeStruct
+    return call(
+        functools.partial(back_kernel, grid),
+        [
+            shape((col_count, group, block), jnp.bfloat16),
+            shape((2 * row_count, group, block), jnp.bfloat16),
+        ],
+        [down_ids, token_rows, *grad_parts, down_blocks],
+        1,
+        [
+            pltpu.VMEM((row_count + 1, group, block), jnp.bfloat16),
+            pltpu.VMEM((col_count, group, block), jnp.float32),
+            *turned_scratch(down_blocks, 1),
+            *stream_scratch(down_blocks, 1, 2),
+        ],
+        48,
+        flops,
+    )
 
 
 def gate_and_up(parts, col):
     return [sum(part[which, col].astype(jnp.float32) for part in parts) for which in (0, 1)]
 
 
-def down_kernel(grid, ids, *refs):
+def down_kernel(grid, arrive, ids, *refs):
     row_count, col_count = grid
     parts = refs[:-6]
     down, out, hidden, total, held, sems = refs[-6:]
@@ -162,6 +247,7 @@
         row, col = place(ids[0, 0, slot], *grid)
         total[row] += product(hidden[col], held[slot])
 
+    arrive()
     over_slots(down.shape[2], sems.shape[1], copies, body)
     for row in range(row_count):
         out[:, row * 128 : (row + 1) * 128] = total[row].astype(out.dtype)
@@ -182,32 +268,48 @@
         out[2 * col_count + col] = (grad * silu_gate).astype(out.dtype)
 
 
-def input_kernel(grid, gate_ids, up_ids, acts, gate, up, partial, *refs):
+def input_kernel(grid, arrive, gate_ids, up_ids, acts, gate, up, partial, *refs):
     row_count, col_count = grid
-    *outs, gate_act, up_act, total, gate_held, up_held, sems = refs
+    *outs, total, gate_near, gate_far, up_near, up_far, gate_held, up_held, sems = refs
     copies = streams((gate, up), (gate_held, up_held), sems)
     start_all(copies, sems.shape[1])
-    for col in range(col_count):
-        gate_act[col] = acts[col_count + col].T
-        up_act[col] = acts[2 * col_count + col].T
     zero(total)
 
-    def body(slot):
-        for ids, held, act in ((gate_ids, gate_held, gate_act), (up_ids, up_held, up_act)):
+    def body(slot, turned):
+        for ids, blocks, which in ((gate_ids, turned[0], 1), (up_ids, turned[1], 2)):
             row, col = place(ids[0, 0, slot], *grid)
-            total[row] += product(held[slot], act[col])
-
-    over_slots(gate.shape[2], sems.shape[1], copies, body)
+            total[row] += product(acts[which * col_count + col], blocks[...])
+
+    halves = ((gate_near, gate_far), (up_near, up_far))
+    arrive()
+    over_turned_slots((gate_held, up_held), halves, sems.shape[1], copies, body)
     height = outs[0].shape[0] // 2
     for piece, out in enumerate(outs):
-        out[:height] = partial[piece * height : (piece + 1) * height]
-    for row in range(row_count):
-        turned = total[row].T.astype(partial.dtype)
-        for piece, out in enumerate(outs):
-            out[height:, row * 128 : (row + 1) * 128] = turned[piece * height : (piece + 1) * height]
-
-
-def grads_kernel(grid, groups, gate_ids, up_ids, down_ids, *refs):
+        tokens = slice(piece * height, (piece + 1) * height)
+        out[:height] = partial[tokens]
+        for row in range(row_count):
+            out[height:, row * 128 : (row + 1) * 128] = total[row, tokens].astype(out.dtype)
+
+
+def run_input(grid, gate_ids, up_ids, acts, gate_blocks, up_blocks, partial, tile, flops):
+    (row_count, _), block = grid, gate_blocks.shape[-1]
+    group = partial.shape[0]
+    return call(
+        functools.partial(input_kernel, grid),
+        [jax.ShapeDtypeStruct((2 * group // tile, row_count * block), jnp.bfloat16)] * tile,
+        [gate_ids, up_ids, acts, gate_blocks, up_blocks, partial],
+        2,
+        [
+            pltpu.VMEM((row_count + 1, group, block), jnp.float32),
+            *turned_scratch(gate_blocks, 2),
+            *stream_scratch(gate_blocks, 2, 2),
+        ],
+        48,
+        flops,
+    )
+
+
+def grads_kernel(grid, groups, arrive, gate_ids, up_ids, down_ids, *refs):
     row_count, col_count = grid
     rows, acts = refs[:groups], refs[groups : 2 * groups]
     gate_out, up_out, down_out = refs[2 * groups : 2 * groups + 3]
@@ -236,6 +338,8 @@
             for i, (buf, out) in enumerate(pairs)
         ]
 
+    arrive()
+
     @pl.loop(0, slot_count // slots)
     def _(step):
         for index in range(slots):
@@ -259,10 +363,14 @@
     return lax.ppermute(value, axis, [(i, target(i, size)) for i in range(size)])
 
 
+def beyond(device, distance, size):
+    return (device + distance) % size if size & (size - 1) else device ^ distance
+
+
 def gathered(value, axis):
     size = lax.axis_size(axis)
     return [value] + [
-        sent(value, axis, lambda i, n, d=d: (i + d) % n) for d in range(1, size)
+        sent(value, axis, lambda i, n, d=d: beyond(i, d, n)) for d in range(1, size)
     ]
 
 
@@ -278,8 +386,10 @@
 
 
 def scattered(pieces, axis):
+    size = lax.axis_size(axis)
+    sign = -1 if size & (size - 1) else 1
     return [pieces[0]] + [
-        sent(pieces[d], axis, lambda i, n, d=d: (i - d) % n) for d in range(1, len(pieces))
+        sent(pieces[d], axis, lambda i, n, d=d: beyond(i, sign * d, n)) for d in range(1, size)
     ]
 
 
@@ -306,20 +416,9 @@
         + stream_scratch(gate_blocks, 2),
         48,
         2 * step_flops,
-    )
-    back, rows = call(
-        functools.partial(back_kernel, grid),
-        [shape((col_count, group, block), bf16), shape((2 * row_count, group, block), bf16)],
-        [down_ids, token_rows, *grad_parts, down_blocks],
-        1,
-        [
-            pltpu.VMEM((row_count + 1, block, group), bf16),
-            pltpu.VMEM((col_count, block, group), f32),
-            *stream_scratch(down_blocks, 1),
-        ],
-        48,
-        step_flops,
-    )
+        fetched=1,
+    )
+    back, rows = run_back(grid, down_ids, token_rows, grad_parts, down_blocks, step_flops)
     first_doubling, *later_doublings = doublings("replica")
     all_rows = first_doubling([rows])
     gate_up_parts = gathered(gate_up, "dp")
@@ -337,9 +436,7 @@
         48,
         step_flops,
     )
-    back_parts, partial, all_rows = lax.optimization_barrier(
-        (gathered(back, "dp"), partial, all_rows)
-    )
+    back_parts, partial = lax.optimization_barrier((gathered(back, "dp"), partial))
     acts = call(
         functools.partial(hidden_kernel, col_count),
         shape((3 * col_count, group, block), bf16),
@@ -350,21 +447,13 @@
         1,
     )
     all_acts = first_doubling([acts])
+    partial, all_rows[1:] = lax.optimization_barrier((partial, all_rows[1:]))
     for doubling in later_doublings:
         all_rows = doubling(all_rows)
-    partial, all_rows = lax.optimization_barrier((partial, all_rows))
-    pieces = call(
-        functools.partial(input_kernel, grid),
-        [shape((2 * height, row_count * block), bf16)] * tile,
-        [gate_ids, up_ids, acts, gate_blocks, up_blocks, partial],
-        2,
-        [pltpu.VMEM((col_count, block, group), bf16)] * 2
-        + [pltpu.VMEM((row_count + 1, block, group), f32)]
-        + stream_scratch(gate_blocks, 2),
-        48,
-        2 * step_flops,
-    )
-    pieces, all_acts[1:] = lax.optimization_barrier((pieces, all_acts[1:]))
+    pieces = run_input(
+        grid, gate_ids, up_ids, acts, gate_blocks, up_blocks, partial, tile, 2 * step_flops
+    )
+    _, all_acts[1:] = lax.optimization_barrier((pieces, all_acts[1:]))
     for doubling in later_doublings:
         all_acts = doubling(all_acts)
     total = group * groups

time: 86.7 us -> 83.1 us (0.958)
  Pallas kernels: 53.6 us -> 49.1 us
  local copies, waits for them, and re-layouts: 2.87 us -> 0.66 us
  starting transfers between devices: 22.8 us -> 24.5 us
  waiting for transfers between devices: 6.43 us -> 7.57 us
    pallas_call x6, Pallas kernels: 53.6 us -> 49.1 us  [call(): pl.pallas_call(kernel, out_shape=out_shape, in_specs=[pl.BlockSpec(memory...]
    unnamed x14 -> x2, local copies, waits for them, and re-layouts: 2.21 us -> 0.01 us
    ppermute x17, starting transfers between devices: 22.8 us -> 24.5 us  [sent(): lax.ppermute(value, axis, [(i, target(i, size)) for i in range(size)])]
    ppermute x17, waiting for transfers between devices: 6.43 us -> 7.57 us  [sent(): lax.ppermute(value, axis, [(i, target(i, size)) for i in range(size)])]
  transfers between devices with their start and end apart: 17 -> 17, of which waited for: 4 -> 2; matrix products, arithmetic and copies ran while one was open for 0% -> 0% of each run, Pallas kernels for 62% -> 59%
where the time goes in v4:
time: 83.1 us; the launch traced here: 82.7 us
  Pallas kernels  49.1 us (59%)
  starting transfers between devices  24.5 us (29%)
  waiting for transfers between devices  7.57 us (9%)
    pallas_call x6, Pallas kernels, call(): pl.pallas_call(kernel, out_shape=out_shape, in_specs=[pl.BlockSpec(memory...  49.1 us
    ppermute x17, starting transfers between devices, sent(): lax.ppermute(value, axis, [(i, target(i, size)) for i in range(size)])  24.5 us
    ppermute x17, waiting for transfers between devices, sent(): lax.ppermute(value, axis, [(i, target(i, size)) for i in range(size)])  7.57 us
  transfers between devices with their start and end apart: 17, of which 2 were waited for; matrix products, arithmetic and copies ran while one was open for 0% of the time, Pallas kernels for 59%

profile of v4, /device:TPU:0, one launch (start us, length us, event | category | flops | bytes accessed | tf_op | source)
XLA Modules:
  0.0 82.7 jit_solution(3938716287251931175)
XLA Ops:
  0.6 4.1 %collective-permute-start.1 = (bf16[8,4096]{1,0:T(8,128)(2,1)}, bf16[8,4096]{1,0:T(8,128)(2,1)S(1)}, u32[]{:S(2)}, u32[]{:S(2)}) collective-permute-start(bf16[8,4096]{1,0:T(8,128)(2,1)} %refs_2_.3), channel_id=1, source_target_pairs={{0,8},{4,12},{8,0},{12,4},{1,9},{5,13},{9,1},{13,5},{2,10},{6,14},... | collective-permute-start | bytes 196616 | tf_op jit(solution)/shard_map/ppermute | solution.py:363
  4.7 1.6 %collective-permute-start = (bf16[8,4096]{1,0:T(8,128)(2,1)}, bf16[8,4096]{1,0:T(8,128)(2,1)S(1)}, u32[]{:S(2)}, u32[]{:S(2)}) collective-permute-start(bf16[8,4096]{1,0:T(8,128)(2,1)} %refs_2_.3), channel_id=1, source_target_pairs={{0,4},{4,0},{8,12},{12,8},{1,5},{5,1},{9,13},{13,9},{2,6},{6,2},{1... | collective-permute-start | bytes 196616 | tf_op jit(solution)/shard_map/ppermute | solution.py:363
  6.3 1.9 %collective-permute-start.5 = (bf16[8,4096]{1,0:T(8,128)(2,1)}, bf16[8,4096]{1,0:T(8,128)(2,1)S(1)}, u32[]{:S(2)}, u32[]{:S(2)}) collective-permute-start(bf16[8,4096]{1,0:T(8,128)(2,1)} %refs_2_.4), channel_id=1, source_target_pairs={{0,8},{4,12},{8,0},{12,4},{1,9},{5,13},{9,1},{13,5},{2,10},{6,14},... | collective-permute-start | bytes 196616 | tf_op jit(solution)/shard_map/ppermute | solution.py:363
  8.2 2.5 %collective-permute-start.4 = (bf16[8,4096]{1,0:T(8,128)(2,1)}, bf16[8,4096]{1,0:T(8,128)(2,1)S(1)}, u32[]{:S(2)}, u32[]{:S(2)}) collective-permute-start(bf16[8,4096]{1,0:T(8,128)(2,1)} %refs_2_.4), channel_id=1, source_target_pairs={{0,4},{4,0},{8,12},{12,8},{1,5},{5,1},{9,13},{13,9},{2,6},{6,2},{1... | collective-permute-start | bytes 196616 | tf_op jit(solution)/shard_map/ppermute | solution.py:363
  10.7 0.0 collective-permute-done.1.refs_4_
  10.7 3.6 %collective-permute-start.6 = (bf16[8,4096]{1,0:T(8,128)(2,1)}, bf16[8,4096]{1,0:T(8,128)(2,1)S(1)}, u32[]{:S(2)}, u32[]{:S(2)}) collective-permute-start(bf16[8,4096]{1,0:T(8,128)(2,1)} %refs_2_.4), channel_id=1, source_target_pairs={{0,12},{4,8},{8,4},{12,0},{1,13},{5,9},{9,5},{13,1},{2,14},{6,10},... | collective-permute-start | bytes 196616 | tf_op jit(solution)/shard_map/ppermute | solution.py:363
  14.3 0.0 collective-permute-done.refs_3_
  14.3 0.0 collective-permute-done.2.refs_5_
  14.3 10.1 %shard_map.119 = (bf16[2,28,32,128]{3,2,1,0:T(8,128)(2,1)S(1)}, bf16[32,32,128]{2,1,0:T(8,128)(2,1)S(1)}) custom-call(s32[1,1,384]{2,1,0:T(1,128)} %refs_0_.9, s32[1,1,384]{2,1,0:T(1,128)} %refs_1_.5, bf16[8,4096]{1,0:T(8,128)(2,1)} %refs_2_.3, bf16[8,4096]{1,0:T(8,128)(2,1)S(1)} %collective-permute-done.refs_3_, ...), custom_call_target="tpu_custom_call" | custom-call | flops 16106127360 | bytes 26151936 | tf_op jit(solution)/shard_map/pallas_call | solution.py:133
  24.5 1.7 %collective-permute-start.3 = (bf16[2,28,32,128]{3,2,1,0:T(8,128)(2,1)S(1)}, bf16[2,28,32,128]{3,2,1,0:T(8,128)(2,1)S(1)}, u32[]{:S(2)}, u32[]{:S(2)}) collective-permute-start(bf16[2,28,32,128]{3,2,1,0:T(8,128)(2,1)S(1)} %get-tuple-element.35.refs_1_.refs_0_), channel_id=1, source_target_pairs={{0,16},{16,0},{1,17},{17,1},{2,18},{18,2},{3,19},{19,3},{4,20},{20... | collective-permute-start | bytes 1376264 | tf_op jit(solution)/shard_map/ppermute | solution.py:363
  26.1 0.0 collective-permute-done.5.refs_4_
  26.1 0.0 collective-permute-done.4.refs_3_
  26.1 0.0 collective-permute-done.6.refs_5_
  26.1 6.9 %shard_map.120 = (bf16[28,32,128]{2,1,0:T(8,128)(2,1)S(1)}, bf16[64,32,128]{2,1,0:T(8,128)(2,1)S(1)}) custom-call(s32[1,1,384]{2,1,0:T(1,128)} %refs_2_.5, bf16[32,32,128]{2,1,0:T(8,128)(2,1)S(1)} %get-tuple-element.33.refs_1_, bf16[8,4096]{1,0:T(8,128)(2,1)S(1)} %copy-done, bf16[8,4096]{1,0:T(8,128)(2,1)S(1)} %collective-permute-done.4.refs_3_, ...), custom_call_target="tpu_custom_call" | custom-call | flops 8053063680 | bytes 13862400 | tf_op jit(solution)/shard_map/pallas_call | solution.py:133
  33.0 1.6 %collective-permute-start.8 = (bf16[64,32,128]{2,1,0:T(8,128)(2,1)S(1)}, bf16[64,32,128]{2,1,0:T(8,128)(2,1)S(1)}, u32[]{:S(2)}, u32[]{:S(2)}) collective-permute-start(bf16[64,32,128]{2,1,0:T(8,128)(2,1)S(1)} %get-tuple-element.41.refs_3_), channel_id=1, source_target_pairs={{0,2},{1,3},{2,0},{3,1},{4,6},{5,7},{6,4},{7,5},{8,10},{9,11},{10,... | collective-permute-start | bytes 1572872 | tf_op jit(solution)/shard_map/ppermute | solution.py:363
  34.6 2.2 %collective-permute-start.7 = (bf16[28,32,128]{2,1,0:T(8,128)(2,1)S(1)}, bf16[28,32,128]{2,1,0:T(8,128)(2,1)S(1)}, u32[]{:S(2)}, u32[]{:S(2)}) collective-permute-start(bf16[28,32,128]{2,1,0:T(8,128)(2,1)S(1)} %get-tuple-element.38.refs_2_), channel_id=1, source_target_pairs={{0,16},{16,0},{1,17},{17,1},{2,18},{18,2},{3,19},{19,3},{4,20},{20... | collective-permute-start | bytes 688136 | tf_op jit(solution)/shard_map/ppermute | solution.py:363
  36.8 6.3 %shard_map.121.refs_5_ = bf16[32,4096]{1,0:T(8,128)(2,1)S(1)} custom-call(s32[1,1,384]{2,1,0:T(1,128)} %refs_2_.5, bf16[2,28,32,128]{3,2,1,0:T(8,128)(2,1)S(1)} %get-tuple-element.35.refs_1_.refs_0_, bf16[2,28,32,128]{3,2,1,0:T(8,128)(2,1)S(1)} %collective-permute-done.3.refs_2_.refs_1_, bf16[1,1,384,128,128]{4,3,2,1,0:T(8,128)(2,1)} %refs_3_.2), custom_call_target="tpu_custom_call" | custom-call | flops 8053063680 | bytes 13764096 | tf_op jit(solution)/shard_map/pallas_call | solution.py:133
  43.1 0.3 shard_map.122.refs_2_.refs_7_
  43.4 0.1 collective-permute-start.15
  43.5 1.6 %collective-permute-start.14 = (bf16[84,32,128]{2,1,0:T(8,128)(2,1)S(1)}, bf16[84,32,128]{2,1,0:T(8,128)(2,1)S(1)}, u32[]{:S(2)}, u32[]{:S(2)}) collective-permute-start(bf16[84,32,128]{2,1,0:T(8,128)(2,1)S(1)} %shard_map.122.refs_2_.refs_7_), channel_id=1, source_target_pairs={{0,2},{1,3},{2,0},{3,1},{4,6},{5,7},{6,4},{7,5},{8,10},{9,11},{10,... | collective-permute-start | bytes 2064392 | tf_op jit(solution)/shard_map/ppermute | solution.py:363
  45.1 10.7 %shard_map.123 = (bf16[16,4096]{1,0:T(8,128)(2,1)S(1)}, bf16[16,4096]{1,0:T(8,128)(2,1)S(1)}, bf16[16,4096]{1,0:T(8,128)(2,1)S(1)}, bf16[16,4096]{1,0:T(8,128)(2,1)S(1)}) custom-call(s32[1,1,384]{2,1,0:T(1,128)} %refs_0_.9, s32[1,1,384]{2,1,0:T(1,128)} %refs_1_.5, bf16[84,32,128]{2,1,0:T(8,128)(2,1)S(1)} %shard_map.122.refs_2_.refs_7_, ...), custom_call_target="tpu_custom_call" | custom-call | flops 16106127360 | bytes 26643456 | tf_op jit(solution)/shard_map/pallas_call | solution.py:133
  55.8 5.6 %collective-permute-done.14.refs_8_ = bf16[84,32,128]{2,1,0:T(8,128)(2,1)S(1)} collective-permute-done((bf16[84,32,128]{2,1,0:T(8,128)(2,1)S(1)}, bf16[84,32,128]{2,1,0:T(8,128)(2,1)S(1)}, u32[]{:S(2)}, u32[]{:S(2)}) %collective-permute-start.14) | collective-permute-done | bytes 688160 | tf_op jit(solution)/shard_map/ppermute | solution.py:363
  61.4 0.5 collective-permute-start.12
  61.9 0.0 collective-permute-start.13
  61.9 0.5 collective-permute-start.9
  62.3 1.9 %collective-permute-done.12.refs_5_ = bf16[64,32,128]{2,1,0:T(8,128)(2,1)S(1)} collective-permute-done((bf16[64,32,128]{2,1,0:T(8,128)(2,1)S(1)}, bf16[64,32,128]{2,1,0:T(8,128)(2,1)S(1)}, u32[]{:S(2)}, u32[]{:S(2)}) %collective-permute-start.12) | collective-permute-done | bytes 524320 | tf_op jit(solution)/shard_map/ppermute | solution.py:363
  64.3 1.7 %collective-permute-start.10 = (bf16[16,4096]{1,0:T(8,128)(2,1)S(1)}, bf16[16,4096]{1,0:T(8,128)(2,1)S(1)}, u32[]{:S(2)}, u32[]{:S(2)}) collective-permute-start(bf16[16,4096]{1,0:T(8,128)(2,1)S(1)} %get-tuple-element.45), channel_id=1, source_target_pairs={{0,8},{4,12},{8,0},{12,4},{1,9},{5,13},{9,1},{13,5},{2,10},{6,14},... | collective-permute-start | bytes 393224 | tf_op jit(solution)/shard_map/ppermute | solution.py:363
  66.0 1.1 %collective-permute-start.11 = (bf16[16,4096]{1,0:T(8,128)(2,1)S(1)}, bf16[16,4096]{1,0:T(8,128)(2,1)S(1)}, u32[]{:S(2)}, u32[]{:S(2)}) collective-permute-start(bf16[16,4096]{1,0:T(8,128)(2,1)S(1)} %get-tuple-element.46), channel_id=1, source_target_pairs={{0,12},{4,8},{8,4},{12,0},{1,13},{5,9},{9,5},{13,1},{2,14},{6,10},... | collective-permute-start | bytes 393224 | tf_op jit(solution)/shard_map/ppermute | solution.py:363
  67.1 0.0 collective-permute-done.15.refs_9_
  67.1 14.8 %shard_map.124 = (bf16[1,1,384,128,128]{4,3,2,1,0:T(8,128)(2,1)}, bf16[1,1,384,128,128]{4,3,2,1,0:T(8,128)(2,1)}, bf16[1,1,384,128,128]{4,3,2,1,0:T(8,128)(2,1)}) custom-call(s32[1,1,384]{2,1,0:T(1,128)} %refs_0_.9, s32[1,1,384]{2,1,0:T(1,128)} %refs_1_.5, s32[1,1,384]{2,1,0:T(1,128)} %refs_2_.5, bf16[64,32,128]{2,1,0:T(8,128)(2,1)S(1)} %get-tuple-element.41.refs_3_, ...), custom_call_target="tpu_custom_call" | custom-call | flops 96636764160 | bytes 42603008 | tf_op jit(solution)/shard_map/pallas_call | solution.py:133
  81.9 0.1 add_convert_fusion
  82.0 0.7 fusion
  (12 shorter events, 0.0 us)
Async XLA Ops:
  0.6 25.5 %copy-start = (bf16[8,4096]{1,0:T(8,128)(2,1)S(1)}, bf16[8,4096]{1,0:T(8,128)(2,1)}, u32[]{:S(2)}) copy-start(bf16[8,4096]{1,0:T(8,128)(2,1)} %refs_2_.4) | copy-start | bytes 196612
  0.6 10.1 %collective-permute-start.1 = (bf16[8,4096]{1,0:T(8,128)(2,1)}, bf16[8,4096]{1,0:T(8,128)(2,1)S(1)}, u32[]{:S(2)}, u32[]{:S(2)}) collective-permute-start(bf16[8,4096]{1,0:T(8,128)(2,1)} %refs_2_.3), channel_id=1, source_target_pairs={{0,8},{4,12},{8,0},{12,4},{1,9},{5,13},{9,1},{13,5},{2,10},{6,14},... | collective-permute-start | bytes 196616 | tf_op jit(solution)/shard_map/ppermute | solution.py:363
  4.7 9.6 %collective-permute-start = (bf16[8,4096]{1,0:T(8,128)(2,1)}, bf16[8,4096]{1,0:T(8,128)(2,1)S(1)}, u32[]{:S(2)}, u32[]{:S(2)}) collective-permute-start(bf16[8,4096]{1,0:T(8,128)(2,1)} %refs_2_.3), channel_id=1, source_target_pairs={{0,4},{4,0},{8,12},{12,8},{1,5},{5,1},{9,13},{13,9},{2,6},{6,2},{1... | collective-permute-start | bytes 196616 | tf_op jit(solution)/shard_map/ppermute | solution.py:363
  6.3 8.0 %collective-permute-start.2 = (bf16[8,4096]{1,0:T(8,128)(2,1)}, bf16[8,4096]{1,0:T(8,128)(2,1)S(1)}, u32[]{:S(2)}, u32[]{:S(2)}) collective-permute-start(bf16[8,4096]{1,0:T(8,128)(2,1)} %refs_2_.3), channel_id=1, source_target_pairs={{0,12},{4,8},{8,4},{12,0},{1,13},{5,9},{9,5},{13,1},{2,14},{6,10},... | collective-permute-start | bytes 196616 | tf_op jit(solution)/shard_map/ppermute | solution.py:363
  6.3 19.8 %collective-permute-start.5 = (bf16[8,4096]{1,0:T(8,128)(2,1)}, bf16[8,4096]{1,0:T(8,128)(2,1)S(1)}, u32[]{:S(2)}, u32[]{:S(2)}) collective-permute-start(bf16[8,4096]{1,0:T(8,128)(2,1)} %refs_2_.4), channel_id=1, source_target_pairs={{0,8},{4,12},{8,0},{12,4},{1,9},{5,13},{9,1},{13,5},{2,10},{6,14},... | collective-permute-start | bytes 196616 | tf_op jit(solution)/shard_map/ppermute | solution.py:363
  8.2 17.9 %collective-permute-start.4 = (bf16[8,4096]{1,0:T(8,128)(2,1)}, bf16[8,4096]{1,0:T(8,128)(2,1)S(1)}, u32[]{:S(2)}, u32[]{:S(2)}) collective-permute-start(bf16[8,4096]{1,0:T(8,128)(2,1)} %refs_2_.4), channel_id=1, source_target_pairs={{0,4},{4,0},{8,12},{12,8},{1,5},{5,1},{9,13},{13,9},{2,6},{6,2},{1... | collective-permute-start | bytes 196616 | tf_op jit(solution)/shard_map/ppermute | solution.py:363
  10.7 15.4 %collective-permute-start.6 = (bf16[8,4096]{1,0:T(8,128)(2,1)}, bf16[8,4096]{1,0:T(8,128)(2,1)S(1)}, u32[]{:S(2)}, u32[]{:S(2)}) collective-permute-start(bf16[8,4096]{1,0:T(8,128)(2,1)} %refs_2_.4), channel_id=1, source_target_pairs={{0,12},{4,8},{8,4},{12,0},{1,13},{5,9},{9,5},{13,1},{2,14},{6,10},... | collective-permute-start | bytes 196616 | tf_op jit(solution)/shard_map/ppermute | solution.py:363
  24.5 10.2 %collective-permute-start.3 = (bf16[2,28,32,128]{3,2,1,0:T(8,128)(2,1)S(1)}, bf16[2,28,32,128]{3,2,1,0:T(8,128)(2,1)S(1)}, u32[]{:S(2)}, u32[]{:S(2)}) collective-permute-start(bf16[2,28,32,128]{3,2,1,0:T(8,128)(2,1)S(1)} %get-tuple-element.35.refs_1_.refs_0_), channel_id=1, source_target_pairs={{0,16},{16,0},{1,17},{17,1},{2,18},{18,2},{3,19},{19,3},{4,20},{20... | collective-permute-start | bytes 1376264 | tf_op jit(solution)/shard_map/ppermute | solution.py:363
  33.0 12.0 %collective-permute-start.8 = (bf16[64,32,128]{2,1,0:T(8,128)(2,1)S(1)}, bf16[64,32,128]{2,1,0:T(8,128)(2,1)S(1)}, u32[]{:S(2)}, u32[]{:S(2)}) collective-permute-start(bf16[64,32,128]{2,1,0:T(8,128)(2,1)S(1)} %get-tuple-element.41.refs_3_), channel_id=1, source_target_pairs={{0,2},{1,3},{2,0},{3,1},{4,6},{5,7},{6,4},{7,5},{8,10},{9,11},{10,... | collective-permute-start | bytes 1572872 | tf_op jit(solution)/shard_map/ppermute | solution.py:363
  34.6 8.5 %collective-permute-start.7 = (bf16[28,32,128]{2,1,0:T(8,128)(2,1)S(1)}, bf16[28,32,128]{2,1,0:T(8,128)(2,1)S(1)}, u32[]{:S(2)}, u32[]{:S(2)}) collective-permute-start(bf16[28,32,128]{2,1,0:T(8,128)(2,1)S(1)} %get-tuple-element.38.refs_2_), channel_id=1, source_target_pairs={{0,16},{16,0},{1,17},{17,1},{2,18},{18,2},{3,19},{19,3},{4,20},{20... | collective-permute-start | bytes 688136 | tf_op jit(solution)/shard_map/ppermute | solution.py:363
  43.4 23.7 %collective-permute-start.15 = (bf16[84,32,128]{2,1,0:T(8,128)(2,1)S(1)}, bf16[84,32,128]{2,1,0:T(8,128)(2,1)S(1)}, u32[]{:S(2)}, u32[]{:S(2)}) collective-permute-start(bf16[84,32,128]{2,1,0:T(8,128)(2,1)S(1)} %shard_map.122.refs_2_.refs_7_), channel_id=1, source_target_pairs={{0,1},{1,0},{2,3},{3,2},{4,5},{5,4},{6,7},{7,6},{8,9},{9,8},{10,11... | collective-permute-start | bytes 2064392 | tf_op jit(solution)/shard_map/ppermute | solution.py:363
  43.5 17.9 %collective-permute-start.14 = (bf16[84,32,128]{2,1,0:T(8,128)(2,1)S(1)}, bf16[84,32,128]{2,1,0:T(8,128)(2,1)S(1)}, u32[]{:S(2)}, u32[]{:S(2)}) collective-permute-start(bf16[84,32,128]{2,1,0:T(8,128)(2,1)S(1)} %shard_map.122.refs_2_.refs_7_), channel_id=1, source_target_pairs={{0,2},{1,3},{2,0},{3,1},{4,6},{5,7},{6,4},{7,5},{8,10},{9,11},{10,... | collective-permute-start | bytes 2064392 | tf_op jit(solution)/shard_map/ppermute | solution.py:363
  61.4 5.7 %collective-permute-start.16 = (bf16[84,32,128]{2,1,0:T(8,128)(2,1)S(1)}, bf16[84,32,128]{2,1,0:T(8,128)(2,1)S(1)}, u32[]{:S(2)}, u32[]{:S(2)}) collective-permute-start(bf16[84,32,128]{2,1,0:T(8,128)(2,1)S(1)} %collective-permute-done.14.refs_8_), channel_id=1, source_target_pairs={{0,1},{1,0},{2,3},{3,2},{4,5},{5,4},{6,7},{7,6},{8,9},{9,8},{10,11... | collective-permute-start | bytes 2064392 | tf_op jit(solution)/shard_map/ppermute | solution.py:363
  61.4 2.9 %collective-permute-start.12 = (bf16[64,32,128]{2,1,0:T(8,128)(2,1)S(1)}, bf16[64,32,128]{2,1,0:T(8,128)(2,1)S(1)}, u32[]{:S(2)}, u32[]{:S(2)}) collective-permute-start(bf16[64,32,128]{2,1,0:T(8,128)(2,1)S(1)} %get-tuple-element.41.refs_3_), channel_id=1, source_target_pairs={{0,1},{1,0},{2,3},{3,2},{4,5},{5,4},{6,7},{7,6},{8,9},{9,8},{10,11... | collective-permute-start | bytes 1572872 | tf_op jit(solution)/shard_map/ppermute | solution.py:363
  61.9 4.1 %collective-permute-start.13 = (bf16[64,32,128]{2,1,0:T(8,128)(2,1)S(1)}, bf16[64,32,128]{2,1,0:T(8,128)(2,1)S(1)}, u32[]{:S(2)}, u32[]{:S(2)}) collective-permute-start(bf16[64,32,128]{2,1,0:T(8,128)(2,1)S(1)} %collective-permute-done.8.refs_4_), channel_id=1, source_target_pairs={{0,1},{1,0},{2,3},{3,2},{4,5},{5,4},{6,7},{7,6},{8,9},{9,8},{10,11... | collective-permute-start | bytes 1572872 | tf_op jit(solution)/shard_map/ppermute | solution.py:363
  61.9 20.0 %collective-permute-start.9 = (bf16[16,4096]{1,0:T(8,128)(2,1)S(1)}, bf16[16,4096]{1,0:T(8,128)(2,1)S(1)}, u32[]{:S(2)}, u32[]{:S(2)}) collective-permute-start(bf16[16,4096]{1,0:T(8,128)(2,1)S(1)} %get-tuple-element.44), channel_id=1, source_target_pairs={{0,4},{4,0},{8,12},{12,8},{1,5},{5,1},{9,13},{13,9},{2,6},{6,2},{1... | collective-permute-start | bytes 393224 | tf_op jit(solution)/shard_map/ppermute | solution.py:363
  64.3 17.6 %collective-permute-start.10 = (bf16[16,4096]{1,0:T(8,128)(2,1)S(1)}, bf16[16,4096]{1,0:T(8,128)(2,1)S(1)}, u32[]{:S(2)}, u32[]{:S(2)}) collective-permute-start(bf16[16,4096]{1,0:T(8,128)(2,1)S(1)} %get-tuple-element.45), channel_id=1, source_target_pairs={{0,8},{4,12},{8,0},{12,4},{1,9},{5,13},{9,1},{13,5},{2,10},{6,14},... | collective-permute-start | bytes 393224 | tf_op jit(solution)/shard_map/ppermute | solution.py:363
  66.0 15.9 %collective-permute-start.11 = (bf16[16,4096]{1,0:T(8,128)(2,1)S(1)}, bf16[16,4096]{1,0:T(8,128)(2,1)S(1)}, u32[]{:S(2)}, u32[]{:S(2)}) collective-permute-start(bf16[16,4096]{1,0:T(8,128)(2,1)S(1)} %get-tuple-element.46), channel_id=1, source_target_pairs={{0,12},{4,8},{8,4},{12,0},{1,13},{5,9},{9,5},{13,1},{2,14},{6,10},... | collective-permute-start | bytes 393224 | tf_op jit(solution)/shard_map/ppermute | solution.py:363

commit v5 on v4

--- a/solution.py
+++ b/solution.py
@@ -161,8 +161,8 @@
 
 def gate_up_kernel(grid, arrive, gate_ids, up_ids, *refs):
     row_count, col_count = grid
-    parts = refs[:-10]
-    gate, up, out, rows, source, gate_sum, up_sum, gate_held, up_held, sems = refs[-10:]
+    parts = refs[:-9]
+    gate, up, out, source, gate_sum, up_sum, gate_held, up_held, sems = refs[-9:]
     copies = streams((gate, up), (gate_held, up_held), sems)
     start_all(copies, sems.shape[1])
     zero(source.at[row_count])
@@ -171,7 +171,6 @@
     arrive()
     for row in range(row_count):
         source[row] = block_of(parts, row)
-        rows[row] = source[row]
 
     def body(slot):
         for ids, held, total in ((gate_ids, gate_held, gate_sum), (up_ids, up_held, up_sum)):
@@ -183,74 +182,32 @@
     out[1] = up_sum[...].astype(out.dtype)
 
 
-def back_kernel(grid, arrive, ids, token_rows, *refs):
+def rows_kernel(row_count, *refs):
+    *parts, out = refs
+    half = len(parts) // 2
+    for row in range(row_count):
+        out[row] = block_of(parts[:half], row)
+        out[row_count + row] = block_of(parts[half:], row)
+    zero(out.at[2 * row_count])
+
+
+def back_kernel(grid, arrive, ids, rows, down, out, total, near, far, held, sems):
     row_count, col_count = grid
-    parts = refs[:-9]
-    down, out, rows, source, total, near, far, held, sems = refs[-9:]
     copies = streams((down,), (held,), sems)
     start_all(copies, sems.shape[1])
-    rows[:row_count] = token_rows[...]
-    for row in range(row_count):
-        source[row] = block_of(parts, row)
-        rows[row_count + row] = source[row]
-    zero(source.at[row_count])
     zero(total)
+    arrive()
 
     def body(slot, turned):
         row, col = place(ids[0, 0, slot], *grid)
-        total[col] += product(source[row], turned[0][...])
-
-    arrive()
+        total[col] += product(rows[row_count + row], turned[0][...])
+
     over_turned_slots((held,), ((near, far),), sems.shape[1], copies, body)
     out[...] = total[...].astype(out.dtype)
 
 
-def run_back(grid, down_ids, token_rows, grad_parts, down_blocks, flops):
-    (row_count, col_count), block = grid, down_blocks.shape[-1]
-    group = token_rows.shape[1]
-    shape = jax.ShapeDtypeStruct
-    return call(
-        functools.partial(back_kernel, grid),
-        [
-            shape((col_count, group, block), jnp.bfloat16),
-            shape((2 * row_count, group, block), jnp.bfloat16),
-        ],
-        [down_ids, token_rows, *grad_parts, down_blocks],
-        1,
-        [
-            pltpu.VMEM((row_count + 1, group, block), jnp.bfloat16),
-            pltpu.VMEM((col_count, group, block), jnp.float32),
-            *turned_scratch(down_blocks, 1),
-            *stream_scratch(down_blocks, 1, 2),
-        ],
-        48,
-        flops,
-    )
-
-
 def gate_and_up(parts, col):
     return [sum(part[which, col].astype(jnp.float32) for part in parts) for which in (0, 1)]
-
-
-def down_kernel(grid, arrive, ids, *refs):
-    row_count, col_count = grid
-    parts = refs[:-6]
-    down, out, hidden, total, held, sems = refs[-6:]
-    copies = streams((down,), (held,), sems)
-    start_all(copies, sems.shape[1])
-    for col in range(col_count):
-        gate_sum, up_sum = gate_and_up(parts, col)
-        hidden[col] = (gate_sum * jax.nn.sigmoid(gate_sum) * up_sum).astype(hidden.dtype)
-    zero(total)
-
-    def body(slot):
-        row, col = place(ids[0, 0, slot], *grid)
-        total[row] += product(hidden[col], held[slot])
-
-    arrive()
-    over_slots(down.shape[2], sems.shape[1], copies, body)
-    for row in range(row_count):
-        out[:, row * 128 : (row + 1) * 128] = total[row].astype(out.dtype)
 
 
 def hidden_kernel(col_count, *refs):
@@ -268,45 +225,32 @@
         out[2 * col_count + col] = (grad * silu_gate).astype(out.dtype)
 
 
-def input_kernel(grid, arrive, gate_ids, up_ids, acts, gate, up, partial, *refs):
+def model_kernel(grid, arrive, gate_ids, up_ids, down_ids, acts, gate, up, down, *refs):
     row_count, col_count = grid
-    *outs, total, gate_near, gate_far, up_near, up_far, gate_held, up_held, sems = refs
-    copies = streams((gate, up), (gate_held, up_held), sems)
+    *outs, y_sum, x_sum, gate_near, gate_far, up_near, up_far = refs[:-4]
+    gate_held, up_held, down_held, sems = refs[-4:]
+    copies = streams((gate, up, down), (gate_held, up_held, down_held), sems)
     start_all(copies, sems.shape[1])
-    zero(total)
+    zero(y_sum)
+    zero(x_sum)
+    arrive()
 
     def body(slot, turned):
         for ids, blocks, which in ((gate_ids, turned[0], 1), (up_ids, turned[1], 2)):
             row, col = place(ids[0, 0, slot], *grid)
-            total[row] += product(acts[which * col_count + col], blocks[...])
+            x_sum[row] += product(acts[which * col_count + col], blocks[...])
+        row, col = place(down_ids[0, 0, slot], *grid)
+        y_sum[row] += product(acts[col], down_held[slot])
 
     halves = ((gate_near, gate_far), (up_near, up_far))
-    arrive()
     over_turned_slots((gate_held, up_held), halves, sems.shape[1], copies, body)
     height = outs[0].shape[0] // 2
     for piece, out in enumerate(outs):
         tokens = slice(piece * height, (piece + 1) * height)
-        out[:height] = partial[tokens]
         for row in range(row_count):
-            out[height:, row * 128 : (row + 1) * 128] = total[row, tokens].astype(out.dtype)
-
-
-def run_input(grid, gate_ids, up_ids, acts, gate_blocks, up_blocks, partial, tile, flops):
-    (row_count, _), block = grid, gate_blocks.shape[-1]
-    group = partial.shape[0]
-    return call(
-        functools.partial(input_kernel, grid),
-        [jax.ShapeDtypeStruct((2 * group // tile, row_count * block), jnp.bfloat16)] * tile,
-        [gate_ids, up_ids, acts, gate_blocks, up_blocks, partial],
-        2,
-        [
-            pltpu.VMEM((row_count + 1, group, block), jnp.float32),
-            *turned_scratch(gate_blocks, 2),
-            *stream_scratch(gate_blocks, 2, 2),
-        ],
-        48,
-        flops,
-    )
+            columns = slice(row * 128, (row + 1) * 128)
+            out[:height, columns] = y_sum[row, tokens].astype(out.dtype)
+            out[height:, columns] = x_sum[row, tokens].astype(out.dtype)
 
 
 def grads_kernel(grid, groups, arrive, gate_ids, up_ids, down_ids, *refs):
@@ -406,9 +350,9 @@
     step_flops = 2 * slot_count * group * block * block
 
     token_parts, grad_parts = gathered(tokens, "tile"), gathered(out_grad, "tile")
-    gate_up, token_rows = call(
+    gate_up = call(
         functools.partial(gate_up_kernel, grid),
-        [shape((2, col_count, group, block), bf16), shape((row_count, group, block), bf16)],
+        shape((2, col_count, group, block), bf16),
         [gate_ids, up_ids, *token_parts, gate_blocks, up_blocks],
         2,
         [pltpu.VMEM((row_count + 1, group, block), bf16)]
@@ -418,25 +362,34 @@
         2 * step_flops,
         fetched=1,
     )
-    back, rows = run_back(grid, down_ids, token_rows, grad_parts, down_blocks, step_flops)
+    _, grad_parts = lax.optimization_barrier((gate_up, grad_parts))
+    rows = call(
+        functools.partial(rows_kernel, row_count),
+        shape((2 * row_count + 1, group, block), bf16),
+        [*token_parts, *grad_parts],
+        0,
+        [],
+        8,
+        1,
+    )
     first_doubling, *later_doublings = doublings("replica")
     all_rows = first_doubling([rows])
-    gate_up_parts = gathered(gate_up, "dp")
-    gate_up_parts, back = lax.optimization_barrier((gate_up_parts, back))
-    partial = call(
-        functools.partial(down_kernel, grid),
-        shape((group, row_count * block), bf16),
-        [down_ids, *gate_up_parts, down_blocks],
+    back = call(
+        functools.partial(back_kernel, grid),
+        shape((col_count, group, block), bf16),
+        [down_ids, rows, down_blocks],
         1,
         [
-            pltpu.VMEM((col_count, group, block), bf16),
-            pltpu.VMEM((row_count + 1, group, block), f32),
-            *stream_scratch(down_blocks, 1),
+            pltpu.VMEM((col_count, group, block), f32),
+            *turned_scratch(down_blocks, 1),
+            *stream_scratch(down_blocks, 1, 2),
         ],
         48,
         step_flops,
     )
-    back_parts, partial = lax.optimization_barrier((gathered(back, "dp"), partial))
+    gate_up_parts = gathered(gate_up, "dp")
+    gate_up_parts, back = lax.optimization_barrier((gate_up_parts, back))
+    back_parts, all_rows[1:] = lax.optimization_barrier((gathered(back, "dp"), all_rows[1:]))
     acts = call(
         functools.partial(hidden_kernel, col_count),
         shape((3 * col_count, group, block), bf16),
@@ -447,11 +400,17 @@
         1,
     )
     all_acts = first_doubling([acts])
-    partial, all_rows[1:] = lax.optimization_barrier((partial, all_rows[1:]))
     for doubling in later_doublings:
         all_rows = doubling(all_rows)
-    pieces = run_input(
-        grid, gate_ids, up_ids, acts, gate_blocks, up_blocks, partial, tile, 2 * step_flops
+    pieces = call(
+        functools.partial(model_kernel, grid),
+        [shape((2 * height, row_count * block), bf16)] * tile,
+        [gate_ids, up_ids, down_ids, acts, gate_blocks, up_blocks, down_blocks],
+        3,
+        [pltpu.VMEM((row_count + 1, group, block), f32)] * 2
+        + [*turned_scratch(gate_blocks, 2), *stream_scratch(gate_blocks, 3, 2)],
+        48,
+        3 * step_flops,
     )
     _, all_acts[1:] = lax.optimization_barrier((pieces, all_acts[1:]))
     for doubling in later_doublings:

time: 83.1 us -> 80 us (0.963)
  Pallas kernels: 49.1 us -> 46.5 us
  starting transfers between devices: 24.5 us -> 22.6 us
  waiting for transfers between devices: 7.57 us -> 9.35 us
    pallas_call x6, Pallas kernels: 49.1 us -> 46.5 us  [call(): pl.pallas_call(kernel, out_shape=out_shape, in_specs=[pl.BlockSpec(memory...]
    ppermute x17, starting transfers between devices: 24.5 us -> 22.6 us  [sent(): lax.ppermute(value, axis, [(i, target(i, size)) for i in range(size)])]
    ppermute x17, waiting for transfers between devices: 7.57 us -> 9.35 us  [sent(): lax.ppermute(value, axis, [(i, target(i, size)) for i in range(size)])]
  transfers between devices with their start and end apart: 17 -> 17, of which waited for: 2 -> 5; matrix products, arithmetic and copies ran while one was open for 0% -> 0% of each run, Pallas kernels for 59% -> 58%
where the time goes in v5:
time: 80 us
  Pallas kernels  46.5 us (58%)
  starting transfers between devices  22.6 us (28%)
  waiting for transfers between devices  9.35 us (12%)
    pallas_call x6, Pallas kernels, call(): pl.pallas_call(kernel, out_shape=out_shape, in_specs=[pl.BlockSpec(memory...  46.5 us
    ppermute x17, starting transfers between devices, sent(): lax.ppermute(value, axis, [(i, target(i, size)) for i in range(size)])  22.6 us
    ppermute x17, waiting for transfers between devices, sent(): lax.ppermute(value, axis, [(i, target(i, size)) for i in range(size)])  9.35 us
  transfers between devices with their start and end apart: 17, of which 5 were waited for; matrix products, arithmetic and copies ran while one was open for 0% of the time, Pallas kernels for 58%

profile of v5, /device:TPU:0, one launch (start us, length us, event | category | flops | bytes accessed | tf_op | source)
XLA Modules:
  0.0 80.0 jit_solution(3606424257156471567)
XLA Ops:
  0.7 5.1 %collective-permute-start.2 = (bf16[8,4096]{1,0:T(8,128)(2,1)}, bf16[8,4096]{1,0:T(8,128)(2,1)S(1)}, u32[]{:S(2)}, u32[]{:S(2)}) collective-permute-start(bf16[8,4096]{1,0:T(8,128)(2,1)} %refs_0_.6), channel_id=1, source_target_pairs={{0,12},{4,8},{8,4},{12,0},{1,13},{5,9},{9,5},{13,1},{2,14},{6,10},... | collective-permute-start | bytes 196616 | tf_op jit(solution)/shard_map/ppermute | solution.py:307
  5.8 0.0 collective-permute-start.1
  5.8 0.6 collective-permute-start
  6.4 2.3 %collective-permute-start.5 = (bf16[8,4096]{1,0:T(8,128)(2,1)}, bf16[8,4096]{1,0:T(8,128)(2,1)S(1)}, u32[]{:S(2)}, u32[]{:S(2)}) collective-permute-start(bf16[8,4096]{1,0:T(8,128)(2,1)} %refs_4_.1), channel_id=1, source_target_pairs={{0,8},{4,12},{8,0},{12,4},{1,9},{5,13},{9,1},{13,5},{2,10},{6,14},... | collective-permute-start | bytes 196616 | tf_op jit(solution)/shard_map/ppermute | solution.py:307
  8.7 2.0 %collective-permute-start.4 = (bf16[8,4096]{1,0:T(8,128)(2,1)}, bf16[8,4096]{1,0:T(8,128)(2,1)S(1)}, u32[]{:S(2)}, u32[]{:S(2)}) collective-permute-start(bf16[8,4096]{1,0:T(8,128)(2,1)} %refs_4_.1), channel_id=1, source_target_pairs={{0,4},{4,0},{8,12},{12,8},{1,5},{5,1},{9,13},{13,9},{2,6},{6,2},{1... | collective-permute-start | bytes 196616 | tf_op jit(solution)/shard_map/ppermute | solution.py:307
  10.7 2.0 %collective-permute-start.6 = (bf16[8,4096]{1,0:T(8,128)(2,1)}, bf16[8,4096]{1,0:T(8,128)(2,1)S(1)}, u32[]{:S(2)}, u32[]{:S(2)}) collective-permute-start(bf16[8,4096]{1,0:T(8,128)(2,1)} %refs_4_.1), channel_id=1, source_target_pairs={{0,12},{4,8},{8,4},{12,0},{1,13},{5,9},{9,5},{13,1},{2,14},{6,10},... | collective-permute-start | bytes 196616 | tf_op jit(solution)/shard_map/ppermute | solution.py:307
  12.8 0.0 collective-permute-done.1.refs_4_.refs_2_
  12.8 0.0 collective-permute-done.refs_3_.refs_1_
  12.8 10.0 %shard_map.119.refs_0_ = bf16[2,28,32,128]{3,2,1,0:T(8,128)(2,1)S(1)} custom-call(s32[1,1,384]{2,1,0:T(1,128)} %refs_0_.9, s32[1,1,384]{2,1,0:T(1,128)} %refs_1_.5, bf16[8,4096]{1,0:T(8,128)(2,1)} %refs_0_.6, bf16[8,4096]{1,0:T(8,128)(2,1)S(1)} %collective-permute-done.refs_3_.refs_1_, bf16[8,4096]{1,0:T(8,128)(2,1)S(1)} %collective-permute-done.1.refs_4_.refs_2_, ...), custom_call_target="tpu_custom_call" | custom-call | flops 16106127360 | bytes 25889792 | tf_op jit(solution)/shard_map/pallas_call | solution.py:133
  22.7 1.8 %collective-permute-start.3 = (bf16[2,28,32,128]{3,2,1,0:T(8,128)(2,1)S(1)}, bf16[2,28,32,128]{3,2,1,0:T(8,128)(2,1)S(1)}, u32[]{:S(2)}, u32[]{:S(2)}) collective-permute-start(bf16[2,28,32,128]{3,2,1,0:T(8,128)(2,1)S(1)} %shard_map.119.refs_0_), channel_id=1, source_target_pairs={{0,16},{16,0},{1,17},{17,1},{2,18},{18,2},{3,19},{19,3},{4,20},{20... | collective-permute-start | bytes 1376264 | tf_op jit(solution)/shard_map/ppermute | solution.py:307
  24.6 0.1 shard_map.120.refs_1_.refs_3_
  24.7 1.6 %collective-permute-start.8 = (bf16[65,32,128]{2,1,0:T(8,128)(2,1)S(1)}, bf16[65,32,128]{2,1,0:T(8,128)(2,1)S(1)}, u32[]{:S(2)}, u32[]{:S(2)}) collective-permute-start(bf16[65,32,128]{2,1,0:T(8,128)(2,1)S(1)} %shard_map.120.refs_1_.refs_3_), channel_id=1, source_target_pairs={{0,2},{1,3},{2,0},{3,1},{4,6},{5,7},{6,4},{7,5},{8,10},{9,11},{10,... | collective-permute-start | bytes 1597448 | tf_op jit(solution)/shard_map/ppermute | solution.py:307
  26.3 6.6 %shard_map.121.refs_2_ = bf16[28,32,128]{2,1,0:T(8,128)(2,1)S(1)} custom-call(s32[1,1,384]{2,1,0:T(1,128)} %refs_2_.7, bf16[65,32,128]{2,1,0:T(8,128)(2,1)S(1)} %shard_map.120.refs_1_.refs_3_, bf16[1,1,384,128,128]{4,3,2,1,0:T(8,128)(2,1)} %refs_6_.3), custom_call_target="tpu_custom_call" | custom-call | flops 8053063680 | bytes 13346304 | tf_op jit(solution)/shard_map/pallas_call | solution.py:133
  32.9 1.7 %collective-permute-done.3.refs_1_ = bf16[2,28,32,128]{3,2,1,0:T(8,128)(2,1)S(1)} collective-permute-done((bf16[2,28,32,128]{3,2,1,0:T(8,128)(2,1)S(1)}, bf16[2,28,32,128]{3,2,1,0:T(8,128)(2,1)S(1)}, u32[]{:S(2)}, u32[]{:S(2)}) %collective-permute-start.3) | collective-permute-done | bytes 458784 | tf_op jit(solution)/shard_map/ppermute | solution.py:307
  34.6 1.7 %collective-permute-start.7 = (bf16[28,32,128]{2,1,0:T(8,128)(2,1)S(1)}, bf16[28,32,128]{2,1,0:T(8,128)(2,1)S(1)}, u32[]{:S(2)}, u32[]{:S(2)}) collective-permute-start(bf16[28,32,128]{2,1,0:T(8,128)(2,1)S(1)} %shard_map.121.refs_2_), channel_id=1, source_target_pairs={{0,16},{16,0},{1,17},{17,1},{2,18},{18,2},{3,19},{19,3},{4,20},{20... | collective-permute-start | bytes 688136 | tf_op jit(solution)/shard_map/ppermute | solution.py:307
  36.4 1.5 %collective-permute-done.8.refs_4_ = bf16[65,32,128]{2,1,0:T(8,128)(2,1)S(1)} collective-permute-done((bf16[65,32,128]{2,1,0:T(8,128)(2,1)S(1)}, bf16[65,32,128]{2,1,0:T(8,128)(2,1)S(1)}, u32[]{:S(2)}, u32[]{:S(2)}) %collective-permute-start.8) | collective-permute-done | bytes 532512 | tf_op jit(solution)/shard_map/ppermute | solution.py:307
  37.9 2.8 %collective-permute-done.7.refs_3_ = bf16[28,32,128]{2,1,0:T(8,128)(2,1)S(1)} collective-permute-done((bf16[28,32,128]{2,1,0:T(8,128)(2,1)S(1)}, bf16[28,32,128]{2,1,0:T(8,128)(2,1)S(1)}, u32[]{:S(2)}, u32[]{:S(2)}) %collective-permute-start.7) | collective-permute-done | bytes 229408 | tf_op jit(solution)/shard_map/ppermute | solution.py:307
  40.6 0.3 shard_map.122.refs_3_.refs_7_
  41.0 1.6 %collective-permute-start.14 = (bf16[84,32,128]{2,1,0:T(8,128)(2,1)S(1)}, bf16[84,32,128]{2,1,0:T(8,128)(2,1)S(1)}, u32[]{:S(2)}, u32[]{:S(2)}) collective-permute-start(bf16[84,32,128]{2,1,0:T(8,128)(2,1)S(1)} %shard_map.122.refs_3_.refs_7_), channel_id=1, source_target_pairs={{0,2},{1,3},{2,0},{3,1},{4,6},{5,7},{6,4},{7,5},{8,10},{9,11},{10,... | collective-permute-start | bytes 2064392 | tf_op jit(solution)/shard_map/ppermute | solution.py:307
  42.5 14.7 %shard_map.123 = (bf16[16,4096]{1,0:T(8,128)(2,1)S(1)}, bf16[16,4096]{1,0:T(8,128)(2,1)S(1)}, bf16[16,4096]{1,0:T(8,128)(2,1)S(1)}, bf16[16,4096]{1,0:T(8,128)(2,1)S(1)}) custom-call(s32[1,1,384]{2,1,0:T(1,128)} %refs_0_.9, s32[1,1,384]{2,1,0:T(1,128)} %refs_1_.5, s32[1,1,384]{2,1,0:T(1,128)} %refs_2_.7, ...), custom_call_target="tpu_custom_call" | custom-call | flops 24159191040 | bytes 38965760 | tf_op jit(solution)/shard_map/pallas_call | solution.py:133
  57.3 0.1 collective-permute-start.15
  57.4 0.5 collective-permute-start.16
  57.9 0.1 collective-permute-start.12
  57.9 0.4 collective-permute-start.13
  58.4 0.1 collective-permute-start.9
  58.5 2.8 %collective-permute-done.12.refs_5_ = bf16[65,32,128]{2,1,0:T(8,128)(2,1)S(1)} collective-permute-done((bf16[65,32,128]{2,1,0:T(8,128)(2,1)S(1)}, bf16[65,32,128]{2,1,0:T(8,128)(2,1)S(1)}, u32[]{:S(2)}, u32[]{:S(2)}) %collective-permute-start.12) | collective-permute-done | bytes 532512 | tf_op jit(solution)/shard_map/ppermute | solution.py:307
  61.2 0.2 collective-permute-start.10
  61.5 0.5 collective-permute-done.13.refs_6_
  62.0 2.4 %collective-permute-start.11 = (bf16[16,4096]{1,0:T(8,128)(2,1)S(1)}, bf16[16,4096]{1,0:T(8,128)(2,1)S(1)}, u32[]{:S(2)}, u32[]{:S(2)}) collective-permute-start(bf16[16,4096]{1,0:T(8,128)(2,1)S(1)} %get-tuple-element.42), channel_id=1, source_target_pairs={{0,12},{4,8},{8,4},{12,0},{1,13},{5,9},{9,5},{13,1},{2,14},{6,10},... | collective-permute-start | bytes 393224 | tf_op jit(solution)/shard_map/ppermute | solution.py:307
  64.4 14.8 %shard_map.124 = (bf16[1,1,384,128,128]{4,3,2,1,0:T(8,128)(2,1)}, bf16[1,1,384,128,128]{4,3,2,1,0:T(8,128)(2,1)}, bf16[1,1,384,128,128]{4,3,2,1,0:T(8,128)(2,1)}) custom-call(s32[1,1,384]{2,1,0:T(1,128)} %refs_0_.9, s32[1,1,384]{2,1,0:T(1,128)} %refs_1_.5, s32[1,1,384]{2,1,0:T(1,128)} %refs_2_.7, bf16[65,32,128]{2,1,0:T(8,128)(2,1)S(1)} %shard_map.120.refs_1_.refs_3_, ...), custom_call_target="tpu_custom_call" | custom-call | flops 96636764160 | bytes 42635776 | tf_op jit(solution)/shard_map/pallas_call | solution.py:133
  79.2 0.1 add_convert_fusion
  79.3 0.7 fusion
  (14 shorter events, 0.0 us)
Async XLA Ops:
  0.6 23.9 %copy-start = (bf16[8,4096]{1,0:T(8,128)(2,1)S(1)}, bf16[8,4096]{1,0:T(8,128)(2,1)}, u32[]{:S(2)}) copy-start(bf16[8,4096]{1,0:T(8,128)(2,1)} %refs_0_.6) | copy-start | bytes 196612
  0.6 23.9 %copy-start.1 = (bf16[8,4096]{1,0:T(8,128)(2,1)S(1)}, bf16[8,4096]{1,0:T(8,128)(2,1)}, u32[]{:S(2)}) copy-start(bf16[8,4096]{1,0:T(8,128)(2,1)} %refs_4_.1) | copy-start | bytes 196612
  0.7 10.1 %collective-permute-start.2 = (bf16[8,4096]{1,0:T(8,128)(2,1)}, bf16[8,4096]{1,0:T(8,128)(2,1)S(1)}, u32[]{:S(2)}, u32[]{:S(2)}) collective-permute-start(bf16[8,4096]{1,0:T(8,128)(2,1)} %refs_0_.6), channel_id=1, source_target_pairs={{0,12},{4,8},{8,4},{12,0},{1,13},{5,9},{9,5},{13,1},{2,14},{6,10},... | collective-permute-start | bytes 196616 | tf_op jit(solution)/shard_map/ppermute | solution.py:307
  5.8 7.0 %collective-permute-start.1 = (bf16[8,4096]{1,0:T(8,128)(2,1)}, bf16[8,4096]{1,0:T(8,128)(2,1)S(1)}, u32[]{:S(2)}, u32[]{:S(2)}) collective-permute-start(bf16[8,4096]{1,0:T(8,128)(2,1)} %refs_0_.6), channel_id=1, source_target_pairs={{0,8},{4,12},{8,0},{12,4},{1,9},{5,13},{9,1},{13,5},{2,10},{6,14},... | collective-permute-start | bytes 196616 | tf_op jit(solution)/shard_map/ppermute | solution.py:307
  5.8 7.0 %collective-permute-start = (bf16[8,4096]{1,0:T(8,128)(2,1)}, bf16[8,4096]{1,0:T(8,128)(2,1)S(1)}, u32[]{:S(2)}, u32[]{:S(2)}) collective-permute-start(bf16[8,4096]{1,0:T(8,128)(2,1)} %refs_0_.6), channel_id=1, source_target_pairs={{0,4},{4,0},{8,12},{12,8},{1,5},{5,1},{9,13},{13,9},{2,6},{6,2},{1... | collective-permute-start | bytes 196616 | tf_op jit(solution)/shard_map/ppermute | solution.py:307
  6.4 18.2 %collective-permute-start.5 = (bf16[8,4096]{1,0:T(8,128)(2,1)}, bf16[8,4096]{1,0:T(8,128)(2,1)S(1)}, u32[]{:S(2)}, u32[]{:S(2)}) collective-permute-start(bf16[8,4096]{1,0:T(8,128)(2,1)} %refs_4_.1), channel_id=1, source_target_pairs={{0,8},{4,12},{8,0},{12,4},{1,9},{5,13},{9,1},{13,5},{2,10},{6,14},... | collective-permute-start | bytes 196616 | tf_op jit(solution)/shard_map/ppermute | solution.py:307
  8.7 15.9 %collective-permute-start.4 = (bf16[8,4096]{1,0:T(8,128)(2,1)}, bf16[8,4096]{1,0:T(8,128)(2,1)S(1)}, u32[]{:S(2)}, u32[]{:S(2)}) collective-permute-start(bf16[8,4096]{1,0:T(8,128)(2,1)} %refs_4_.1), channel_id=1, source_target_pairs={{0,4},{4,0},{8,12},{12,8},{1,5},{5,1},{9,13},{13,9},{2,6},{6,2},{1... | collective-permute-start | bytes 196616 | tf_op jit(solution)/shard_map/ppermute | solution.py:307
  10.7 13.9 %collective-permute-start.6 = (bf16[8,4096]{1,0:T(8,128)(2,1)}, bf16[8,4096]{1,0:T(8,128)(2,1)S(1)}, u32[]{:S(2)}, u32[]{:S(2)}) collective-permute-start(bf16[8,4096]{1,0:T(8,128)(2,1)} %refs_4_.1), channel_id=1, source_target_pairs={{0,12},{4,8},{8,4},{12,0},{1,13},{5,9},{9,5},{13,1},{2,14},{6,10},... | collective-permute-start | bytes 196616 | tf_op jit(solution)/shard_map/ppermute | solution.py:307
  22.7 11.9 %collective-permute-start.3 = (bf16[2,28,32,128]{3,2,1,0:T(8,128)(2,1)S(1)}, bf16[2,28,32,128]{3,2,1,0:T(8,128)(2,1)S(1)}, u32[]{:S(2)}, u32[]{:S(2)}) collective-permute-start(bf16[2,28,32,128]{3,2,1,0:T(8,128)(2,1)S(1)} %shard_map.119.refs_0_), channel_id=1, source_target_pairs={{0,16},{16,0},{1,17},{17,1},{2,18},{18,2},{3,19},{19,3},{4,20},{20... | collective-permute-start | bytes 1376264 | tf_op jit(solution)/shard_map/ppermute | solution.py:307
  24.7 13.2 %collective-permute-start.8 = (bf16[65,32,128]{2,1,0:T(8,128)(2,1)S(1)}, bf16[65,32,128]{2,1,0:T(8,128)(2,1)S(1)}, u32[]{:S(2)}, u32[]{:S(2)}) collective-permute-start(bf16[65,32,128]{2,1,0:T(8,128)(2,1)S(1)} %shard_map.120.refs_1_.refs_3_), channel_id=1, source_target_pairs={{0,2},{1,3},{2,0},{3,1},{4,6},{5,7},{6,4},{7,5},{8,10},{9,11},{10,... | collective-permute-start | bytes 1597448 | tf_op jit(solution)/shard_map/ppermute | solution.py:307
  34.6 6.0 %collective-permute-start.7 = (bf16[28,32,128]{2,1,0:T(8,128)(2,1)S(1)}, bf16[28,32,128]{2,1,0:T(8,128)(2,1)S(1)}, u32[]{:S(2)}, u32[]{:S(2)}) collective-permute-start(bf16[28,32,128]{2,1,0:T(8,128)(2,1)S(1)} %shard_map.121.refs_2_), channel_id=1, source_target_pairs={{0,16},{16,0},{1,17},{17,1},{2,18},{18,2},{3,19},{19,3},{4,20},{20... | collective-permute-start | bytes 688136 | tf_op jit(solution)/shard_map/ppermute | solution.py:307
  41.0 16.4 %collective-permute-start.14 = (bf16[84,32,128]{2,1,0:T(8,128)(2,1)S(1)}, bf16[84,32,128]{2,1,0:T(8,128)(2,1)S(1)}, u32[]{:S(2)}, u32[]{:S(2)}) collective-permute-start(bf16[84,32,128]{2,1,0:T(8,128)(2,1)S(1)} %shard_map.122.refs_3_.refs_7_), channel_id=1, source_target_pairs={{0,2},{1,3},{2,0},{3,1},{4,6},{5,7},{6,4},{7,5},{8,10},{9,11},{10,... | collective-permute-start | bytes 2064392 | tf_op jit(solution)/shard_map/ppermute | solution.py:307
  57.3 7.1 %collective-permute-start.15 = (bf16[84,32,128]{2,1,0:T(8,128)(2,1)S(1)}, bf16[84,32,128]{2,1,0:T(8,128)(2,1)S(1)}, u32[]{:S(2)}, u32[]{:S(2)}) collective-permute-start(bf16[84,32,128]{2,1,0:T(8,128)(2,1)S(1)} %shard_map.122.refs_3_.refs_7_), channel_id=1, source_target_pairs={{0,1},{1,0},{2,3},{3,2},{4,5},{5,4},{6,7},{7,6},{8,9},{9,8},{10,11... | collective-permute-start | bytes 2064392 | tf_op jit(solution)/shard_map/ppermute | solution.py:307
  57.4 7.0 %collective-permute-start.16 = (bf16[84,32,128]{2,1,0:T(8,128)(2,1)S(1)}, bf16[84,32,128]{2,1,0:T(8,128)(2,1)S(1)}, u32[]{:S(2)}, u32[]{:S(2)}) collective-permute-start(bf16[84,32,128]{2,1,0:T(8,128)(2,1)S(1)} %collective-permute-done.14.refs_8_), channel_id=1, source_target_pairs={{0,1},{1,0},{2,3},{3,2},{4,5},{5,4},{6,7},{7,6},{8,9},{9,8},{10,11... | collective-permute-start | bytes 2064392 | tf_op jit(solution)/shard_map/ppermute | solution.py:307
  57.9 3.4 %collective-permute-start.12 = (bf16[65,32,128]{2,1,0:T(8,128)(2,1)S(1)}, bf16[65,32,128]{2,1,0:T(8,128)(2,1)S(1)}, u32[]{:S(2)}, u32[]{:S(2)}) collective-permute-start(bf16[65,32,128]{2,1,0:T(8,128)(2,1)S(1)} %shard_map.120.refs_1_.refs_3_), channel_id=1, source_target_pairs={{0,1},{1,0},{2,3},{3,2},{4,5},{5,4},{6,7},{7,6},{8,9},{9,8},{10,11... | collective-permute-start | bytes 1597448 | tf_op jit(solution)/shard_map/ppermute | solution.py:307
  57.9 4.1 %collective-permute-start.13 = (bf16[65,32,128]{2,1,0:T(8,128)(2,1)S(1)}, bf16[65,32,128]{2,1,0:T(8,128)(2,1)S(1)}, u32[]{:S(2)}, u32[]{:S(2)}) collective-permute-start(bf16[65,32,128]{2,1,0:T(8,128)(2,1)S(1)} %collective-permute-done.8.refs_4_), channel_id=1, source_target_pairs={{0,1},{1,0},{2,3},{3,2},{4,5},{5,4},{6,7},{7,6},{8,9},{9,8},{10,11... | collective-permute-start | bytes 1597448 | tf_op jit(solution)/shard_map/ppermute | solution.py:307
  58.4 20.8 %collective-permute-start.9 = (bf16[16,4096]{1,0:T(8,128)(2,1)S(1)}, bf16[16,4096]{1,0:T(8,128)(2,1)S(1)}, u32[]{:S(2)}, u32[]{:S(2)}) collective-permute-start(bf16[16,4096]{1,0:T(8,128)(2,1)S(1)} %get-tuple-element.40), channel_id=1, source_target_pairs={{0,4},{4,0},{8,12},{12,8},{1,5},{5,1},{9,13},{13,9},{2,6},{6,2},{1... | collective-permute-start | bytes 393224 | tf_op jit(solution)/shard_map/ppermute | solution.py:307
  61.2 18.0 %collective-permute-start.10 = (bf16[16,4096]{1,0:T(8,128)(2,1)S(1)}, bf16[16,4096]{1,0:T(8,128)(2,1)S(1)}, u32[]{:S(2)}, u32[]{:S(2)}) collective-permute-start(bf16[16,4096]{1,0:T(8,128)(2,1)S(1)} %get-tuple-element.41), channel_id=1, source_target_pairs={{0,8},{4,12},{8,0},{12,4},{1,9},{5,13},{9,1},{13,5},{2,10},{6,14},... | collective-permute-start | bytes 393224 | tf_op jit(solution)/shard_map/ppermute | solution.py:307
  62.0 17.2 %collective-permute-start.11 = (bf16[16,4096]{1,0:T(8,128)(2,1)S(1)}, bf16[16,4096]{1,0:T(8,128)(2,1)S(1)}, u32[]{:S(2)}, u32[]{:S(2)}) collective-permute-start(bf16[16,4096]{1,0:T(8,128)(2,1)S(1)} %get-tuple-element.42), channel_id=1, source_target_pairs={{0,12},{4,8},{8,4},{12,0},{1,13},{5,9},{9,5},{13,1},{2,14},{6,10},... | collective-permute-start | bytes 393224 | tf_op jit(solution)/shard_map/ppermute | solution.py:307

commit v6 on v5

--- a/solution.py
+++ b/solution.py
@@ -88,9 +88,9 @@
                 turn(later, slot, 1 - half)
 
 
-def stream_scratch(blocks, count, halves=1):
+def stream_scratch(blocks, count, halves=1, limit=SLOTS_PER_STEP):
     slot_count, block = blocks.shape[2], blocks.shape[-1]
-    steps = halves * (slot_count // halves // divisor_up_to(slot_count // halves, SLOTS_PER_STEP))
+    steps = halves * (slot_count // halves // divisor_up_to(slot_count // halves, limit))
     return [pltpu.VMEM((slot_count, block, block), blocks.dtype)] * count + [
         pltpu.SemaphoreType.DMA((count, steps))
     ]
@@ -210,19 +210,24 @@
     return [sum(part[which, col].astype(jnp.float32) for part in parts) for which in (0, 1)]
 
 
-def hidden_kernel(col_count, *refs):
-    half = len(refs) // 2
-    parts, backs, out = refs[:half], refs[half:-1], refs[-1]
+def hidden_kernel(col_count, summands, row_arrays, row_blocks, *refs):
+    parts, backs = refs[:summands], refs[summands : 2 * summands]
+    rows = refs[2 * summands : 2 * summands + row_arrays]
+    acts, *packs = refs[2 * summands + row_arrays :]
     for col in range(col_count):
         gate_sum, up_sum = gate_and_up(parts, col)
         grad = sum(back[col].astype(jnp.float32) for back in backs)
         sigmoid = jax.nn.sigmoid(gate_sum)
         silu_gate = gate_sum * sigmoid
-        out[col] = (silu_gate * up_sum).astype(out.dtype)
-        out[col_count + col] = (
+        acts[col] = (silu_gate * up_sum).astype(acts.dtype)
+        acts[col_count + col] = (
             grad * up_sum * sigmoid * (1.0 + gate_sum * (1.0 - sigmoid))
-        ).astype(out.dtype)
-        out[2 * col_count + col] = (grad * silu_gate).astype(out.dtype)
+        ).astype(acts.dtype)
+        acts[2 * col_count + col] = (grad * silu_gate).astype(acts.dtype)
+    for pack in packs:
+        for place_of, held in enumerate(rows):
+            pack[place_of * row_blocks : (place_of + 1) * row_blocks] = held[:row_blocks]
+        pack[len(rows) * row_blocks :] = acts[...]
 
 
 def model_kernel(grid, arrive, gate_ids, up_ids, down_ids, acts, gate, up, down, *refs):
@@ -253,14 +258,13 @@
             out[height:, columns] = x_sum[row, tokens].astype(out.dtype)
 
 
-def grads_kernel(grid, groups, arrive, gate_ids, up_ids, down_ids, *refs):
+def grads_kernel(grid, rows, acts, arrive, gate_ids, up_ids, down_ids, *refs):
     row_count, col_count = grid
-    rows, acts = refs[:groups], refs[groups : 2 * groups]
-    gate_out, up_out, down_out = refs[2 * groups : 2 * groups + 3]
-    x, g, hidden, gate_act, up_act, gate_buf, up_buf, down_buf, sems = refs[2 * groups + 3 :]
-
-    def joined(parts, index):
-        return jnp.concatenate([part[index] for part in parts], axis=0)
+    gate_out, up_out, down_out, x, g, hidden, gate_act, up_act = refs[-12:-4]
+    gate_buf, up_buf, down_buf, sems = refs[-4:]
+
+    def joined(groups, index):
+        return jnp.concatenate([refs[array][first + index] for array, first in groups], axis=0)
 
     for row in range(row_count):
         x[row] = joined(rows, row).T
@@ -318,15 +322,8 @@
     ]
 
 
-def doublings(axis):
-    size = lax.axis_size(axis)
-    if size & (size - 1):
-        return [lambda pieces: gathered(pieces[0], axis)]
-    return [
-        lambda pieces, d=1 << bit: pieces
-        + [sent(piece, axis, lambda i, n: i ^ d) for piece in pieces]
-        for bit in reversed(range(size.bit_length() - 1))
-    ]
+def across(value, distance):
+    return sent(value, "replica", lambda i, n: i ^ distance)
 
 
 def scattered(pieces, axis):
@@ -357,7 +354,7 @@
         2,
         [pltpu.VMEM((row_count + 1, group, block), bf16)]
         + [pltpu.VMEM((col_count, group, block), f32)] * 2
-        + stream_scratch(gate_blocks, 2),
+        + stream_scratch(gate_blocks, 2, limit=48),
         48,
         2 * step_flops,
         fetched=1,
@@ -372,8 +369,8 @@
         8,
         1,
     )
-    first_doubling, *later_doublings = doublings("replica")
-    all_rows = first_doubling([rows])
+    packed = groups == 4
+    far_rows = across(rows, 2) if packed else None
     back = call(
         functools.partial(back_kernel, grid),
         shape((col_count, group, block), bf16),
@@ -388,20 +385,21 @@
         step_flops,
     )
     gate_up_parts = gathered(gate_up, "dp")
-    gate_up_parts, back = lax.optimization_barrier((gate_up_parts, back))
-    back_parts, all_rows[1:] = lax.optimization_barrier((gathered(back, "dp"), all_rows[1:]))
-    acts = call(
-        functools.partial(hidden_kernel, col_count),
-        shape((3 * col_count, group, block), bf16),
-        [*gate_up_parts, *back_parts],
+    gate_up_parts, _ = lax.optimization_barrier((gate_up_parts, back))
+    back_parts, far_rows = lax.optimization_barrier((gathered(back, "dp"), far_rows))
+    acts_shape = shape((3 * col_count, group, block), bf16)
+    row_blocks = 2 * row_count
+    pack_shape = shape((2 * row_blocks + 3 * col_count, group, block), bf16)
+    acts, *pack = call(
+        functools.partial(hidden_kernel, col_count, len(back_parts), 2 * packed, row_blocks),
+        [acts_shape, pack_shape] if packed else [acts_shape],
+        [*gate_up_parts, *back_parts, *([rows, far_rows] if packed else [])],
         0,
         [],
         8,
         1,
     )
-    all_acts = first_doubling([acts])
-    for doubling in later_doublings:
-        all_rows = doubling(all_rows)
+    far_acts = across(acts, 2) if packed else None
     pieces = call(
         functools.partial(model_kernel, grid),
         [shape((2 * height, row_count * block), bf16)] * tile,
@@ -412,15 +410,21 @@
         48,
         3 * step_flops,
     )
-    _, all_acts[1:] = lax.optimization_barrier((pieces, all_acts[1:]))
-    for doubling in later_doublings:
-        all_acts = doubling(all_acts)
+    if packed:
+        _, far_acts = lax.optimization_barrier((pieces, far_acts))
+        arrays = [rows, far_rows, across(pack[0], 1), acts, far_acts, across(far_acts, 1)]
+        rows_at = ((0, 0), (1, 0), (2, 0), (2, row_blocks))
+        acts_at = ((3, 0), (4, 0), (2, 2 * row_blocks), (5, 0))
+    else:
+        arrays = gathered(rows, "replica") + gathered(acts, "replica")
+        rows_at = tuple((i, 0) for i in range(groups))
+        acts_at = tuple((groups + i, 0) for i in range(groups))
     total = group * groups
     slots = divisor_up_to(slot_count, SLOTS_PER_STEP)
     grads = call(
-        functools.partial(grads_kernel, grid, groups),
+        functools.partial(grads_kernel, grid, rows_at, acts_at),
         [shape(gate_blocks.shape, bf16)] * 3,
-        [gate_ids, up_ids, down_ids, *all_rows, *all_acts],
+        [gate_ids, up_ids, down_ids, *arrays],
         3,
         [
             pltpu.VMEM((row_count + 1, block, total), bf16),
@@ -436,8 +440,11 @@
         out_hbm=True,
     )
     pieces, grads = lax.optimization_barrier((scattered(pieces, "tile"), grads))
-    summed = sum(piece.astype(f32) for piece in pieces).astype(bf16)
-    return (summed[:height], summed[height:], *grads)
+    output, input_grad = (
+        sum(piece[half].astype(f32) for piece in pieces).astype(bf16)
+        for half in (slice(height), slice(height, None))
+    )
+    return (output, input_grad, *grads)
 
 
 def solution(mesh):

time: 80 us -> 77.1 us (0.964)
  waiting for transfers between devices: 9.35 us -> 6.13 us
    ppermute x17 -> x15, waiting for transfers between devices: 9.35 us -> 6.13 us  [sent(): lax.ppermute(value, axis, [(i, target(i, size)) for i in range(size)])]
    ppermute x17 -> x15, starting transfers between devices: 22.6 us -> 22.4 us  [sent(): lax.ppermute(value, axis, [(i, target(i, size)) for i in range(size)])]
  transfers between devices with their start and end apart: 17 -> 15, of which waited for: 5 -> 2; matrix products, arithmetic and copies ran while one was open for 0% -> 0% of each run, Pallas kernels for 58% -> 60%
where the time goes in v6:
time: 77.1 us; the launch traced here: 76.9 us
  Pallas kernels  46.9 us (61%)
  starting transfers between devices  22.4 us (29%)
  waiting for transfers between devices  6.13 us (8%)
    pallas_call x6, Pallas kernels, call(): pl.pallas_call(kernel, out_shape=out_shape, in_specs=[pl.BlockSpec(memory...  46.9 us
    ppermute x15, starting transfers between devices, sent(): lax.ppermute(value, axis, [(i, target(i, size)) for i in range(size)])  22.4 us
    ppermute x15, waiting for transfers between devices, sent(): lax.ppermute(value, axis, [(i, target(i, size)) for i in range(size)])  6.13 us
  transfers between devices with their start and end apart: 15, of which 2 were waited for; matrix products, arithmetic and copies ran while one was open for 0% of the time, Pallas kernels for 60%

profile of v6, /device:TPU:0, one launch (start us, length us, event | category | flops | bytes accessed | tf_op | source)
XLA Modules:
  0.0 76.9 jit_solution(15169294130014359978)
XLA Ops:
  0.7 5.1 %collective-permute-start.2 = (bf16[8,4096]{1,0:T(8,128)(2,1)}, bf16[8,4096]{1,0:T(8,128)(2,1)S(1)}, u32[]{:S(2)}, u32[]{:S(2)}) collective-permute-start(bf16[8,4096]{1,0:T(8,128)(2,1)} %refs_0_.6), channel_id=1, source_target_pairs={{0,12},{4,8},{8,4},{12,0},{1,13},{5,9},{9,5},{13,1},{2,14},{6,10},... | collective-permute-start | bytes 196616 | tf_op jit(solution)/shard_map/ppermute | solution.py:311
  5.8 0.0 collective-permute-start.1
  5.8 0.6 collective-permute-start
  6.4 2.3 %collective-permute-start.5 = (bf16[8,4096]{1,0:T(8,128)(2,1)}, bf16[8,4096]{1,0:T(8,128)(2,1)S(1)}, u32[]{:S(2)}, u32[]{:S(2)}) collective-permute-start(bf16[8,4096]{1,0:T(8,128)(2,1)} %refs_4_.1), channel_id=1, source_target_pairs={{0,8},{4,12},{8,0},{12,4},{1,9},{5,13},{9,1},{13,5},{2,10},{6,14},... | collective-permute-start | bytes 196616 | tf_op jit(solution)/shard_map/ppermute | solution.py:311
  8.7 2.0 %collective-permute-start.4 = (bf16[8,4096]{1,0:T(8,128)(2,1)}, bf16[8,4096]{1,0:T(8,128)(2,1)S(1)}, u32[]{:S(2)}, u32[]{:S(2)}) collective-permute-start(bf16[8,4096]{1,0:T(8,128)(2,1)} %refs_4_.1), channel_id=1, source_target_pairs={{0,4},{4,0},{8,12},{12,8},{1,5},{5,1},{9,13},{13,9},{2,6},{6,2},{1... | collective-permute-start | bytes 196616 | tf_op jit(solution)/shard_map/ppermute | solution.py:311
  10.7 0.0 collective-permute-done.2.refs_5_.refs_3_
  10.7 2.0 %collective-permute-start.6 = (bf16[8,4096]{1,0:T(8,128)(2,1)}, bf16[8,4096]{1,0:T(8,128)(2,1)S(1)}, u32[]{:S(2)}, u32[]{:S(2)}) collective-permute-start(bf16[8,4096]{1,0:T(8,128)(2,1)} %refs_4_.1), channel_id=1, source_target_pairs={{0,12},{4,8},{8,4},{12,0},{1,13},{5,9},{9,5},{13,1},{2,14},{6,10},... | collective-permute-start | bytes 196616 | tf_op jit(solution)/shard_map/ppermute | solution.py:311
  12.8 0.0 collective-permute-done.refs_3_.refs_1_
  12.8 10.0 %shard_map.119.refs_0_ = bf16[2,28,32,128]{3,2,1,0:T(8,128)(2,1)S(1)} custom-call(s32[1,1,384]{2,1,0:T(1,128)} %refs_0_.9, s32[1,1,384]{2,1,0:T(1,128)} %refs_1_.5, bf16[8,4096]{1,0:T(8,128)(2,1)} %refs_0_.6, bf16[8,4096]{1,0:T(8,128)(2,1)S(1)} %collective-permute-done.refs_3_.refs_1_, bf16[8,4096]{1,0:T(8,128)(2,1)S(1)} %collective-permute-done.1.refs_4_.refs_2_, ...), custom_call_target="tpu_custom_call" | custom-call | flops 16106127360 | bytes 25889792 | tf_op jit(solution)/shard_map/pallas_call | solution.py:133
  22.8 1.4 %collective-permute-start.3 = (bf16[2,28,32,128]{3,2,1,0:T(8,128)(2,1)S(1)}, bf16[2,28,32,128]{3,2,1,0:T(8,128)(2,1)S(1)}, u32[]{:S(2)}, u32[]{:S(2)}) collective-permute-start(bf16[2,28,32,128]{3,2,1,0:T(8,128)(2,1)S(1)} %shard_map.119.refs_0_), channel_id=1, source_target_pairs={{0,16},{16,0},{1,17},{17,1},{2,18},{18,2},{3,19},{19,3},{4,20},{20... | collective-permute-start | bytes 1376264 | tf_op jit(solution)/shard_map/ppermute | solution.py:311
  24.2 0.0 collective-permute-done.5.refs_6_
  24.2 0.0 collective-permute-done.4.refs_5_
  24.2 0.0 collective-permute-done.6.refs_7_
  24.2 0.1 shard_map.120.refs_1_.refs_4_.refs_3_
  24.3 1.6 %collective-permute-start.8 = (bf16[65,32,128]{2,1,0:T(8,128)(2,1)S(1)}, bf16[65,32,128]{2,1,0:T(8,128)(2,1)S(1)}, u32[]{:S(2)}, u32[]{:S(2)}) collective-permute-start(bf16[65,32,128]{2,1,0:T(8,128)(2,1)S(1)} %shard_map.120.refs_1_.refs_4_.refs_3_), channel_id=1, source_target_pairs={{0,2},{1,3},{2,0},{3,1},{4,6},{5,7},{6,4},{7,5},{8,10},{9,11},{10,... | collective-permute-start | bytes 1597448 | tf_op jit(solution)/shard_map/ppermute | solution.py:311
  25.9 6.8 %shard_map.121.refs_2_ = bf16[28,32,128]{2,1,0:T(8,128)(2,1)S(1)} custom-call(s32[1,1,384]{2,1,0:T(1,128)} %refs_2_.7, bf16[65,32,128]{2,1,0:T(8,128)(2,1)S(1)} %shard_map.120.refs_1_.refs_4_.refs_3_, bf16[1,1,384,128,128]{4,3,2,1,0:T(8,128)(2,1)} %refs_6_.3), custom_call_target="tpu_custom_call" | custom-call | flops 8053063680 | bytes 13346304 | tf_op jit(solution)/shard_map/pallas_call | solution.py:133
  32.6 0.6 collective-permute-start.7
  33.3 1.5 %collective-permute-done.3.refs_1_ = bf16[2,28,32,128]{3,2,1,0:T(8,128)(2,1)S(1)} collective-permute-done((bf16[2,28,32,128]{3,2,1,0:T(8,128)(2,1)S(1)}, bf16[2,28,32,128]{3,2,1,0:T(8,128)(2,1)S(1)}, u32[]{:S(2)}, u32[]{:S(2)}) %collective-permute-start.3) | collective-permute-done | bytes 458784 | tf_op jit(solution)/shard_map/ppermute | solution.py:311
  34.7 4.6 %collective-permute-done.7.refs_3_ = bf16[28,32,128]{2,1,0:T(8,128)(2,1)S(1)} collective-permute-done((bf16[28,32,128]{2,1,0:T(8,128)(2,1)S(1)}, bf16[28,32,128]{2,1,0:T(8,128)(2,1)S(1)}, u32[]{:S(2)}, u32[]{:S(2)}) %collective-permute-start.7) | collective-permute-done | bytes 229408 | tf_op jit(solution)/shard_map/ppermute | solution.py:311
  39.4 0.4 shard_map.122
  39.8 1.7 %collective-permute-start.13 = (bf16[84,32,128]{2,1,0:T(8,128)(2,1)S(1)}, bf16[84,32,128]{2,1,0:T(8,128)(2,1)S(1)}, u32[]{:S(2)}, u32[]{:S(2)}) collective-permute-start(bf16[84,32,128]{2,1,0:T(8,128)(2,1)S(1)} %get-tuple-element.40.refs_3_.refs_6_), channel_id=1, source_target_pairs={{0,2},{1,3},{2,0},{3,1},{4,6},{5,7},{6,4},{7,5},{8,10},{9,11},{10,... | collective-permute-start | bytes 2064392 | tf_op jit(solution)/shard_map/ppermute | solution.py:311
  41.5 14.8 %shard_map.123 = (bf16[16,4096]{1,0:T(8,128)(2,1)S(1)}, bf16[16,4096]{1,0:T(8,128)(2,1)S(1)}, bf16[16,4096]{1,0:T(8,128)(2,1)S(1)}, bf16[16,4096]{1,0:T(8,128)(2,1)S(1)}) custom-call(s32[1,1,384]{2,1,0:T(1,128)} %refs_0_.9, s32[1,1,384]{2,1,0:T(1,128)} %refs_1_.5, s32[1,1,384]{2,1,0:T(1,128)} %refs_2_.7, ...), custom_call_target="tpu_custom_call" | custom-call | flops 24159191040 | bytes 38965760 | tf_op jit(solution)/shard_map/pallas_call | solution.py:133
  56.3 0.0 collective-permute-done.13.refs_7_
  56.3 0.6 collective-permute-start.14
  56.9 0.0 collective-permute-start.9
  56.9 2.3 %collective-permute-start.10 = (bf16[16,4096]{1,0:T(8,128)(2,1)S(1)}, bf16[16,4096]{1,0:T(8,128)(2,1)S(1)}, u32[]{:S(2)}, u32[]{:S(2)}) collective-permute-start(bf16[16,4096]{1,0:T(8,128)(2,1)S(1)} %get-tuple-element.43), channel_id=1, source_target_pairs={{0,8},{4,12},{8,0},{12,4},{1,9},{5,13},{9,1},{13,5},{2,10},{6,14},... | collective-permute-start | bytes 393224 | tf_op jit(solution)/shard_map/ppermute | solution.py:311
  59.2 2.1 %collective-permute-start.11 = (bf16[16,4096]{1,0:T(8,128)(2,1)S(1)}, bf16[16,4096]{1,0:T(8,128)(2,1)S(1)}, u32[]{:S(2)}, u32[]{:S(2)}) collective-permute-start(bf16[16,4096]{1,0:T(8,128)(2,1)S(1)} %get-tuple-element.44), channel_id=1, source_target_pairs={{0,12},{4,8},{8,4},{12,0},{1,13},{5,9},{9,5},{13,1},{2,14},{6,10},... | collective-permute-start | bytes 393224 | tf_op jit(solution)/shard_map/ppermute | solution.py:311
  61.3 0.0 collective-permute-done.14.refs_8_
  61.3 0.0 collective-permute-done.12.refs_5_
  61.3 14.8 %shard_map.124 = (bf16[1,1,384,128,128]{4,3,2,1,0:T(8,128)(2,1)}, bf16[1,1,384,128,128]{4,3,2,1,0:T(8,128)(2,1)}, bf16[1,1,384,128,128]{4,3,2,1,0:T(8,128)(2,1)}) custom-call(s32[1,1,384]{2,1,0:T(1,128)} %refs_0_.9, s32[1,1,384]{2,1,0:T(1,128)} %refs_1_.5, s32[1,1,384]{2,1,0:T(1,128)} %refs_2_.7, ...), custom_call_target="tpu_custom_call" | custom-call | flops 96636764160 | bytes 42619392 | tf_op jit(solution)/shard_map/pallas_call | solution.py:133
  76.1 0.0 collective-permute-done.9
  76.1 0.7 add_convert_fusion
  (9 shorter events, 0.0 us)
Async XLA Ops:
  0.6 23.6 %copy-start = (bf16[8,4096]{1,0:T(8,128)(2,1)S(1)}, bf16[8,4096]{1,0:T(8,128)(2,1)}, u32[]{:S(2)}) copy-start(bf16[8,4096]{1,0:T(8,128)(2,1)} %refs_0_.6) | copy-start | bytes 196612
  0.6 23.6 %copy-start.1 = (bf16[8,4096]{1,0:T(8,128)(2,1)S(1)}, bf16[8,4096]{1,0:T(8,128)(2,1)}, u32[]{:S(2)}) copy-start(bf16[8,4096]{1,0:T(8,128)(2,1)} %refs_4_.1) | copy-start | bytes 196612
  0.7 10.1 %collective-permute-start.2 = (bf16[8,4096]{1,0:T(8,128)(2,1)}, bf16[8,4096]{1,0:T(8,128)(2,1)S(1)}, u32[]{:S(2)}, u32[]{:S(2)}) collective-permute-start(bf16[8,4096]{1,0:T(8,128)(2,1)} %refs_0_.6), channel_id=1, source_target_pairs={{0,12},{4,8},{8,4},{12,0},{1,13},{5,9},{9,5},{13,1},{2,14},{6,10},... | collective-permute-start | bytes 196616 | tf_op jit(solution)/shard_map/ppermute | solution.py:311
  5.8 7.0 %collective-permute-start.1 = (bf16[8,4096]{1,0:T(8,128)(2,1)}, bf16[8,4096]{1,0:T(8,128)(2,1)S(1)}, u32[]{:S(2)}, u32[]{:S(2)}) collective-permute-start(bf16[8,4096]{1,0:T(8,128)(2,1)} %refs_0_.6), channel_id=1, source_target_pairs={{0,8},{4,12},{8,0},{12,4},{1,9},{5,13},{9,1},{13,5},{2,10},{6,14},... | collective-permute-start | bytes 196616 | tf_op jit(solution)/shard_map/ppermute | solution.py:311
  5.8 7.0 %collective-permute-start = (bf16[8,4096]{1,0:T(8,128)(2,1)}, bf16[8,4096]{1,0:T(8,128)(2,1)S(1)}, u32[]{:S(2)}, u32[]{:S(2)}) collective-permute-start(bf16[8,4096]{1,0:T(8,128)(2,1)} %refs_0_.6), channel_id=1, source_target_pairs={{0,4},{4,0},{8,12},{12,8},{1,5},{5,1},{9,13},{13,9},{2,6},{6,2},{1... | collective-permute-start | bytes 196616 | tf_op jit(solution)/shard_map/ppermute | solution.py:311
  6.4 17.8 %collective-permute-start.5 = (bf16[8,4096]{1,0:T(8,128)(2,1)}, bf16[8,4096]{1,0:T(8,128)(2,1)S(1)}, u32[]{:S(2)}, u32[]{:S(2)}) collective-permute-start(bf16[8,4096]{1,0:T(8,128)(2,1)} %refs_4_.1), channel_id=1, source_target_pairs={{0,8},{4,12},{8,0},{12,4},{1,9},{5,13},{9,1},{13,5},{2,10},{6,14},... | collective-permute-start | bytes 196616 | tf_op jit(solution)/shard_map/ppermute | solution.py:311
  8.7 15.5 %collective-permute-start.4 = (bf16[8,4096]{1,0:T(8,128)(2,1)}, bf16[8,4096]{1,0:T(8,128)(2,1)S(1)}, u32[]{:S(2)}, u32[]{:S(2)}) collective-permute-start(bf16[8,4096]{1,0:T(8,128)(2,1)} %refs_4_.1), channel_id=1, source_target_pairs={{0,4},{4,0},{8,12},{12,8},{1,5},{5,1},{9,13},{13,9},{2,6},{6,2},{1... | collective-permute-start | bytes 196616 | tf_op jit(solution)/shard_map/ppermute | solution.py:311
  10.7 13.5 %collective-permute-start.6 = (bf16[8,4096]{1,0:T(8,128)(2,1)}, bf16[8,4096]{1,0:T(8,128)(2,1)S(1)}, u32[]{:S(2)}, u32[]{:S(2)}) collective-permute-start(bf16[8,4096]{1,0:T(8,128)(2,1)} %refs_4_.1), channel_id=1, source_target_pairs={{0,12},{4,8},{8,4},{12,0},{1,13},{5,9},{9,5},{13,1},{2,14},{6,10},... | collective-permute-start | bytes 196616 | tf_op jit(solution)/shard_map/ppermute | solution.py:311
  22.8 12.0 %collective-permute-start.3 = (bf16[2,28,32,128]{3,2,1,0:T(8,128)(2,1)S(1)}, bf16[2,28,32,128]{3,2,1,0:T(8,128)(2,1)S(1)}, u32[]{:S(2)}, u32[]{:S(2)}) collective-permute-start(bf16[2,28,32,128]{3,2,1,0:T(8,128)(2,1)S(1)} %shard_map.119.refs_0_), channel_id=1, source_target_pairs={{0,16},{16,0},{1,17},{17,1},{2,18},{18,2},{3,19},{19,3},{4,20},{20... | collective-permute-start | bytes 1376264 | tf_op jit(solution)/shard_map/ppermute | solution.py:311
  24.3 15.1 %collective-permute-start.8 = (bf16[65,32,128]{2,1,0:T(8,128)(2,1)S(1)}, bf16[65,32,128]{2,1,0:T(8,128)(2,1)S(1)}, u32[]{:S(2)}, u32[]{:S(2)}) collective-permute-start(bf16[65,32,128]{2,1,0:T(8,128)(2,1)S(1)} %shard_map.120.refs_1_.refs_4_.refs_3_), channel_id=1, source_target_pairs={{0,2},{1,3},{2,0},{3,1},{4,6},{5,7},{6,4},{7,5},{8,10},{9,11},{10,... | collective-permute-start | bytes 1597448 | tf_op jit(solution)/shard_map/ppermute | solution.py:311
  32.6 6.7 %collective-permute-start.7 = (bf16[28,32,128]{2,1,0:T(8,128)(2,1)S(1)}, bf16[28,32,128]{2,1,0:T(8,128)(2,1)S(1)}, u32[]{:S(2)}, u32[]{:S(2)}) collective-permute-start(bf16[28,32,128]{2,1,0:T(8,128)(2,1)S(1)} %shard_map.121.refs_2_), channel_id=1, source_target_pairs={{0,16},{16,0},{1,17},{17,1},{2,18},{18,2},{3,19},{19,3},{4,20},{20... | collective-permute-start | bytes 688136 | tf_op jit(solution)/shard_map/ppermute | solution.py:311
  39.8 16.6 %collective-permute-start.13 = (bf16[84,32,128]{2,1,0:T(8,128)(2,1)S(1)}, bf16[84,32,128]{2,1,0:T(8,128)(2,1)S(1)}, u32[]{:S(2)}, u32[]{:S(2)}) collective-permute-start(bf16[84,32,128]{2,1,0:T(8,128)(2,1)S(1)} %get-tuple-element.40.refs_3_.refs_6_), channel_id=1, source_target_pairs={{0,2},{1,3},{2,0},{3,1},{4,6},{5,7},{6,4},{7,5},{8,10},{9,11},{10,... | collective-permute-start | bytes 2064392 | tf_op jit(solution)/shard_map/ppermute | solution.py:311
  41.5 19.8 %collective-permute-start.12 = (bf16[212,32,128]{2,1,0:T(8,128)(2,1)S(1)}, bf16[212,32,128]{2,1,0:T(8,128)(2,1)S(1)}, u32[]{:S(2)}, u32[]{:S(2)}) collective-permute-start(bf16[212,32,128]{2,1,0:T(8,128)(2,1)S(1)} %get-tuple-element.45), channel_id=1, source_target_pairs={{0,1},{1,0},{2,3},{3,2},{4,5},{5,4},{6,7},{7,6},{8,9},{9,8},{10,11... | collective-permute-start | bytes 5210120 | tf_op jit(solution)/shard_map/ppermute | solution.py:311
  56.3 5.0 %collective-permute-start.14 = (bf16[84,32,128]{2,1,0:T(8,128)(2,1)S(1)}, bf16[84,32,128]{2,1,0:T(8,128)(2,1)S(1)}, u32[]{:S(2)}, u32[]{:S(2)}) collective-permute-start(bf16[84,32,128]{2,1,0:T(8,128)(2,1)S(1)} %collective-permute-done.13.refs_7_), channel_id=1, source_target_pairs={{0,1},{1,0},{2,3},{3,2},{4,5},{5,4},{6,7},{7,6},{8,9},{9,8},{10,11... | collective-permute-start | bytes 2064392 | tf_op jit(solution)/shard_map/ppermute | solution.py:311
  56.9 19.2 %collective-permute-start.9 = (bf16[16,4096]{1,0:T(8,128)(2,1)S(1)}, bf16[16,4096]{1,0:T(8,128)(2,1)S(1)}, u32[]{:S(2)}, u32[]{:S(2)}) collective-permute-start(bf16[16,4096]{1,0:T(8,128)(2,1)S(1)} %get-tuple-element.42), channel_id=1, source_target_pairs={{0,4},{4,0},{8,12},{12,8},{1,5},{5,1},{9,13},{13,9},{2,6},{6,2},{1... | collective-permute-start | bytes 393224 | tf_op jit(solution)/shard_map/ppermute | solution.py:311
  56.9 19.2 %collective-permute-start.10 = (bf16[16,4096]{1,0:T(8,128)(2,1)S(1)}, bf16[16,4096]{1,0:T(8,128)(2,1)S(1)}, u32[]{:S(2)}, u32[]{:S(2)}) collective-permute-start(bf16[16,4096]{1,0:T(8,128)(2,1)S(1)} %get-tuple-element.43), channel_id=1, source_target_pairs={{0,8},{4,12},{8,0},{12,4},{1,9},{5,13},{9,1},{13,5},{2,10},{6,14},... | collective-permute-start | bytes 393224 | tf_op jit(solution)/shard_map/ppermute | solution.py:311
  59.2 16.9 %collective-permute-start.11 = (bf16[16,4096]{1,0:T(8,128)(2,1)S(1)}, bf16[16,4096]{1,0:T(8,128)(2,1)S(1)}, u32[]{:S(2)}, u32[]{:S(2)}) collective-permute-start(bf16[16,4096]{1,0:T(8,128)(2,1)S(1)} %get-tuple-element.44), channel_id=1, source_target_pairs={{0,12},{4,8},{8,4},{12,0},{1,13},{5,9},{9,5},{13,1},{2,14},{6,10},... | collective-permute-start | bytes 393224 | tf_op jit(solution)/shard_map/ppermute | solution.py:311

commit v7 on v6

--- a/solution.py
+++ b/solution.py
@@ -86,6 +86,18 @@
             for slot in range(slots):
                 body(step * slots + slot, [targets[half].at[slot] for targets in turned])
                 turn(later, slot, 1 - half)
+
+
+def filled_steps(ids, grid, steps, least=0):
+    slot_count = ids.shape[-1]
+    ends = lax.broadcasted_iota(jnp.int32, ids.shape, 2) + 1
+    last = jnp.max(jnp.where(ids[...] < grid[0] * grid[1], ends, 0).astype(jnp.float32))
+    slots = slot_count // steps
+    return jnp.clip(lax.div(last.astype(jnp.int32) + (slots - 1), slots), least, steps)
+
+
+def each(start, stop, body):
+    lax.fori_loop(start, stop, lambda step, carry: (body(step), carry)[1], 0)
 
 
 def stream_scratch(blocks, count, halves=1, limit=SLOTS_PER_STEP):
@@ -159,25 +171,42 @@
     return jnp.concatenate([part[:, row * 128 : (row + 1) * 128] for part in parts], axis=0)
 
 
-def gate_up_kernel(grid, arrive, gate_ids, up_ids, *refs):
+def gate_up_kernel(grid, arrive, gate_ids, up_ids, gate_list, up_list, *refs):
     row_count, col_count = grid
     parts = refs[:-9]
     gate, up, out, source, gate_sum, up_sum, gate_held, up_held, sems = refs[-9:]
     copies = streams((gate, up), (gate_held, up_held), sems)
-    start_all(copies, sems.shape[1])
+    steps = sems.shape[1]
+    slots = gate_held.shape[0] // steps
+    ahead = min(2, steps)
+    for step in range(ahead):
+        for copy in copies(step):
+            copy.start()
     zero(source.at[row_count])
     zero(gate_sum)
     zero(up_sum)
     arrive()
+    filled = [filled_steps(ids, grid, steps, ahead) for ids in (gate_list, up_list)]
+    both = jnp.minimum(*filled)
+    each(ahead, both, lambda step: [copy.start() for copy in copies(step)])
+    for which in (0, 1):
+        each(jnp.maximum(both, ahead), filled[which], lambda step, i=which: copies(step)[i].start())
     for row in range(row_count):
         source[row] = block_of(parts, row)
-
-    def body(slot):
-        for ids, held, total in ((gate_ids, gate_held, gate_sum), (up_ids, up_held, up_sum)):
-            row, col = place(ids[0, 0, slot], *grid)
-            total[col] += product(source[row], held[slot])
-
-    over_slots(gate.shape[2], sems.shape[1], copies, body)
+    matrices = ((gate_ids, gate_held, gate_sum), (up_ids, up_held, up_sum))
+
+    def run(step, chosen):
+        for which in chosen:
+            copies(step)[which].wait()
+        for index in range(slots):
+            slot = step * slots + index
+            for ids, held, total in (matrices[which] for which in chosen):
+                row, col = place(ids[0, 0, slot], *grid)
+                total[col] += product(source[row], held[slot])
+
+    each(0, both, lambda step: run(step, (0, 1)))
+    for which in (0, 1):
+        each(both, filled[which], lambda step, i=which: run(step, (i,)))
     out[0] = gate_sum[...].astype(out.dtype)
     out[1] = up_sum[...].astype(out.dtype)
 
@@ -259,13 +288,30 @@
 
 
 def grads_kernel(grid, rows, acts, arrive, gate_ids, up_ids, down_ids, *refs):
+    lists, refs = refs[:3], refs[3:]
     row_count, col_count = grid
-    gate_out, up_out, down_out, x, g, hidden, gate_act, up_act = refs[-12:-4]
-    gate_buf, up_buf, down_buf, sems = refs[-4:]
+    gate_out, up_out, down_out, x, g, hidden, gate_act, up_act = refs[-13:-5]
+    gate_buf, up_buf, down_buf, nothing, sems = refs[-5:]
 
     def joined(groups, index):
         return jnp.concatenate([refs[array][first + index] for array, first in groups], axis=0)
 
+    slot_count = gate_buf.shape[0]
+    slots = divisor_up_to(slot_count, SLOTS_PER_STEP)
+    steps = slot_count // slots
+    pairs = ((gate_buf, gate_out), (up_buf, up_out), (down_buf, down_out))
+
+    def copy(which, step, empty=False):
+        buf, out = pairs[which]
+        chunk = pl.ds(step * slots, slots)
+        source = nothing if empty else buf.at[chunk]
+        return pltpu.make_async_copy(source, out.at[0, 0, chunk], sems.at[which, step])
+
+    zero(nothing)
+    arrive()
+    filled = [filled_steps(ids, grid, steps) for ids in lists]
+    for which in range(3):
+        each(filled[which], steps, lambda step, i=which: copy(i, step, True).start())
     for row in range(row_count):
         x[row] = joined(rows, row).T
         g[row] = joined(rows, row_count + row)
@@ -275,35 +321,29 @@
         hidden[col] = joined(acts, col).T
         gate_act[col] = joined(acts, col_count + col)
         up_act[col] = joined(acts, 2 * col_count + col)
-    slot_count = gate_buf.shape[0]
-    slots = divisor_up_to(slot_count, SLOTS_PER_STEP)
-    pairs = ((gate_buf, gate_out), (up_buf, up_out), (down_buf, down_out))
-
-    def copies(step):
-        chunk = pl.ds(step * slots, slots)
-        return [
-            pltpu.make_async_copy(buf.at[chunk], out.at[0, 0, chunk], sems.at[i, step])
-            for i, (buf, out) in enumerate(pairs)
-        ]
-
-    arrive()
-
-    @pl.loop(0, slot_count // slots)
-    def _(step):
-        for index in range(slots):
-            slot = step * slots + index
-            for ids, act, buf in ((gate_ids, gate_act, gate_buf), (up_ids, up_act, up_buf)):
+    matrices = (
+        (gate_ids, x, gate_act, gate_buf),
+        (up_ids, x, up_act, up_buf),
+        (down_ids, g, hidden, down_buf),
+    )
+
+    def run(step, chosen):
+        for which in chosen:
+            ids, model, act, buf = matrices[which]
+            for index in range(slots):
+                slot = step * slots + index
                 row, col = place(ids[0, 0, slot], *grid)
-                buf[slot] = product(x[row], act[col]).astype(buf.dtype)
-            row, col = place(down_ids[0, 0, slot], *grid)
-            down_buf[slot] = product(hidden[col], g[row]).astype(down_buf.dtype)
-        for copy in copies(step):
-            copy.start()
-
-    @pl.loop(0, slot_count // slots)
-    def _(step):
-        for copy in copies(step):
-            copy.wait()
+                left, right = (act[col], model[row]) if which == 2 else (model[row], act[col])
+                buf[slot] = product(left, right).astype(buf.dtype)
+        for which in chosen:
+            copy(which, step).start()
+
+    every = jnp.minimum(jnp.minimum(*filled[:2]), filled[2])
+    each(0, every, lambda step: run(step, (0, 1, 2)))
+    for which in range(3):
+        each(every, filled[which], lambda step, i=which: run(step, (i,)))
+    for which in range(3):
+        each(0, steps, lambda step, i=which: copy(i, step).wait())
 
 
 def sent(value, axis, target):
@@ -350,14 +390,14 @@
     gate_up = call(
         functools.partial(gate_up_kernel, grid),
         shape((2, col_count, group, block), bf16),
-        [gate_ids, up_ids, *token_parts, gate_blocks, up_blocks],
+        [gate_ids, up_ids, gate_ids, up_ids, *token_parts, gate_blocks, up_blocks],
         2,
         [pltpu.VMEM((row_count + 1, group, block), bf16)]
         + [pltpu.VMEM((col_count, group, block), f32)] * 2
         + stream_scratch(gate_blocks, 2, limit=48),
         48,
         2 * step_flops,
-        fetched=1,
+        fetched=3,
     )
     _, grad_parts = lax.optimization_barrier((gate_up, grad_parts))
     rows = call(
@@ -424,7 +464,7 @@
     grads = call(
         functools.partial(grads_kernel, grid, rows_at, acts_at),
         [shape(gate_blocks.shape, bf16)] * 3,
-        [gate_ids, up_ids, down_ids, *arrays],
+        [gate_ids, up_ids, down_ids, gate_ids, up_ids, down_ids, *arrays],
         3,
         [
             pltpu.VMEM((row_count + 1, block, total), bf16),
@@ -434,10 +474,14 @@
             pltpu.VMEM((col_count, total, block), bf16),
         ]
         + [pltpu.VMEM((slot_count, block, block), bf16)] * 3
-        + [pltpu.SemaphoreType.DMA((3, slot_count // slots))],
-        44,
+        + [
+            pltpu.VMEM((slots, block, block), bf16),
+            pltpu.SemaphoreType.DMA((3, slot_count // slots)),
+        ],
+        46,
         3 * step_flops * groups,
         out_hbm=True,
+        fetched=3,
     )
     pieces, grads = lax.optimization_barrier((scattered(pieces, "tile"), grads))
     output, input_grad = (

time: 77.1 us -> 73.9 us (0.958)
  Pallas kernels: 46.9 us -> 43.9 us
    pallas_call x6, Pallas kernels: 46.9 us -> 43.9 us  [call(): pl.pallas_call(kernel, out_shape=out_shape, in_specs=[pl.BlockSpec(memory...]
  transfers between devices with their start and end apart: 15 -> 15, of which waited for: 2 -> 2; matrix products, arithmetic and copies ran while one was open for 0% -> 0% of each run, Pallas kernels for 60% -> 59%
where the time goes in v7:
time: 73.9 us; the launch traced here: 74 us
  Pallas kernels  43.9 us (59%)
  starting transfers between devices  22.5 us (30%)
  waiting for transfers between devices  6.11 us (8%)
  between operations  0.78 us (1%)
    pallas_call x6, Pallas kernels, call(): pl.pallas_call(kernel, out_shape=out_shape, in_specs=[pl.BlockSpec(memory...  43.9 us
    ppermute x15, starting transfers between devices, sent(): lax.ppermute(value, axis, [(i, target(i, size)) for i in range(size)])  22.5 us
    ppermute x15, waiting for transfers between devices, sent(): lax.ppermute(value, axis, [(i, target(i, size)) for i in range(size)])  6.11 us
  transfers between devices with their start and end apart: 15, of which 2 were waited for; matrix products, arithmetic and copies ran while one was open for 0% of the time, Pallas kernels for 59%

profile of v7, /device:TPU:0, one launch (start us, length us, event | category | flops | bytes accessed | tf_op | source)
XLA Modules:
  0.0 74.0 jit_solution(961798218843881987)
XLA Ops:
  0.7 5.1 %collective-permute-start.2 = (bf16[8,4096]{1,0:T(8,128)(2,1)}, bf16[8,4096]{1,0:T(8,128)(2,1)S(1)}, u32[]{:S(2)}, u32[]{:S(2)}) collective-permute-start(bf16[8,4096]{1,0:T(8,128)(2,1)} %refs_0_.6), channel_id=1, source_target_pairs={{0,12},{4,8},{8,4},{12,0},{1,13},{5,9},{9,5},{13,1},{2,14},{6,10},... | collective-permute-start | bytes 196616 | tf_op jit(solution)/shard_map/ppermute | solution.py:351
  5.8 0.0 collective-permute-start.1
  5.8 0.6 collective-permute-start
  6.4 2.3 %collective-permute-start.5 = (bf16[8,4096]{1,0:T(8,128)(2,1)}, bf16[8,4096]{1,0:T(8,128)(2,1)S(1)}, u32[]{:S(2)}, u32[]{:S(2)}) collective-permute-start(bf16[8,4096]{1,0:T(8,128)(2,1)} %refs_4_.4), channel_id=1, source_target_pairs={{0,8},{4,12},{8,0},{12,4},{1,9},{5,13},{9,1},{13,5},{2,10},{6,14},... | collective-permute-start | bytes 196616 | tf_op jit(solution)/shard_map/ppermute | solution.py:351
  8.7 2.0 %collective-permute-start.4 = (bf16[8,4096]{1,0:T(8,128)(2,1)}, bf16[8,4096]{1,0:T(8,128)(2,1)S(1)}, u32[]{:S(2)}, u32[]{:S(2)}) collective-permute-start(bf16[8,4096]{1,0:T(8,128)(2,1)} %refs_4_.4), channel_id=1, source_target_pairs={{0,4},{4,0},{8,12},{12,8},{1,5},{5,1},{9,13},{13,9},{2,6},{6,2},{1... | collective-permute-start | bytes 196616 | tf_op jit(solution)/shard_map/ppermute | solution.py:351
  10.7 0.0 collective-permute-done.2.refs_7_.refs_3_
  10.7 2.0 %collective-permute-start.6 = (bf16[8,4096]{1,0:T(8,128)(2,1)}, bf16[8,4096]{1,0:T(8,128)(2,1)S(1)}, u32[]{:S(2)}, u32[]{:S(2)}) collective-permute-start(bf16[8,4096]{1,0:T(8,128)(2,1)} %refs_4_.4), channel_id=1, source_target_pairs={{0,12},{4,8},{8,4},{12,0},{1,13},{5,9},{9,5},{13,1},{2,14},{6,10},... | collective-permute-start | bytes 196616 | tf_op jit(solution)/shard_map/ppermute | solution.py:351
  12.8 0.0 collective-permute-done.1.refs_6_.refs_2_
  12.8 0.0 collective-permute-done.refs_5_.refs_1_
  12.8 8.7 %shard_map.119.refs_0_ = bf16[2,28,32,128]{3,2,1,0:T(8,128)(2,1)S(1)} custom-call(s32[1,1,384]{2,1,0:T(1,128)} %refs_3_.3, s32[1,1,384]{2,1,0:T(1,128)} %refs_4_.6, s32[1,1,384]{2,1,0:T(1,128)} %refs_3_.3, s32[1,1,384]{2,1,0:T(1,128)} %refs_4_.6, bf16[8,4096]{1,0:T(8,128)(2,1)} %refs_0_.6, bf16[8,4096]{1,0:T(8,128)(2,1)S(1)} %collective-permute-done.refs_5_.refs_1_, ...), custom_call_target="tpu_custom_call" | custom-call | flops 16106127360 | bytes 25892864 | tf_op jit(solution)/shard_map/pallas_call | solution.py:145
  21.5 0.1 collective-permute-start.3
  21.6 0.0 collective-permute-done.4.refs_5_
  21.6 0.0 collective-permute-done.6.refs_7_
  21.6 0.1 shard_map.120.refs_1_.refs_4_.refs_6_
  21.7 1.6 %collective-permute-start.8 = (bf16[65,32,128]{2,1,0:T(8,128)(2,1)S(1)}, bf16[65,32,128]{2,1,0:T(8,128)(2,1)S(1)}, u32[]{:S(2)}, u32[]{:S(2)}) collective-permute-start(bf16[65,32,128]{2,1,0:T(8,128)(2,1)S(1)} %shard_map.120.refs_1_.refs_4_.refs_6_), channel_id=1, source_target_pairs={{0,2},{1,3},{2,0},{3,1},{4,6},{5,7},{6,4},{7,5},{8,10},{9,11},{10,... | collective-permute-start | bytes 1597448 | tf_op jit(solution)/shard_map/ppermute | solution.py:351
  23.3 6.7 %shard_map.121.refs_2_ = bf16[28,32,128]{2,1,0:T(8,128)(2,1)S(1)} custom-call(s32[1,1,384]{2,1,0:T(1,128)} %refs_5_.3, bf16[65,32,128]{2,1,0:T(8,128)(2,1)S(1)} %shard_map.120.refs_1_.refs_4_.refs_6_, bf16[1,1,384,128,128]{4,3,2,1,0:T(8,128)(2,1)} %refs_6_.1), custom_call_target="tpu_custom_call" | custom-call | flops 8053063680 | bytes 13346304 | tf_op jit(solution)/shard_map/pallas_call | solution.py:145
  29.9 2.1 %collective-permute-start.7 = (bf16[28,32,128]{2,1,0:T(8,128)(2,1)S(1)}, bf16[28,32,128]{2,1,0:T(8,128)(2,1)S(1)}, u32[]{:S(2)}, u32[]{:S(2)}) collective-permute-start(bf16[28,32,128]{2,1,0:T(8,128)(2,1)S(1)} %shard_map.121.refs_2_), channel_id=1, source_target_pairs={{0,16},{16,0},{1,17},{17,1},{2,18},{18,2},{3,19},{19,3},{4,20},{20... | collective-permute-start | bytes 688136 | tf_op jit(solution)/shard_map/ppermute | solution.py:351
  32.0 2.6 %collective-permute-done.3.refs_1_ = bf16[2,28,32,128]{3,2,1,0:T(8,128)(2,1)S(1)} collective-permute-done((bf16[2,28,32,128]{3,2,1,0:T(8,128)(2,1)S(1)}, bf16[2,28,32,128]{3,2,1,0:T(8,128)(2,1)S(1)}, u32[]{:S(2)}, u32[]{:S(2)}) %collective-permute-start.3) | collective-permute-done | bytes 458784 | tf_op jit(solution)/shard_map/ppermute | solution.py:351
  34.6 3.5 %collective-permute-done.7.refs_3_ = bf16[28,32,128]{2,1,0:T(8,128)(2,1)S(1)} collective-permute-done((bf16[28,32,128]{2,1,0:T(8,128)(2,1)S(1)}, bf16[28,32,128]{2,1,0:T(8,128)(2,1)S(1)}, u32[]{:S(2)}, u32[]{:S(2)}) %collective-permute-start.7) | collective-permute-done | bytes 229408 | tf_op jit(solution)/shard_map/ppermute | solution.py:351
  38.1 0.0 collective-permute-done.8.refs_5_.refs_7_
  38.1 0.4 shard_map.122
  38.5 1.7 %collective-permute-start.13 = (bf16[84,32,128]{2,1,0:T(8,128)(2,1)S(1)}, bf16[84,32,128]{2,1,0:T(8,128)(2,1)S(1)}, u32[]{:S(2)}, u32[]{:S(2)}) collective-permute-start(bf16[84,32,128]{2,1,0:T(8,128)(2,1)S(1)} %get-tuple-element.40.refs_3_.refs_9_), channel_id=1, source_target_pairs={{0,2},{1,3},{2,0},{3,1},{4,6},{5,7},{6,4},{7,5},{8,10},{9,11},{10,... | collective-permute-start | bytes 2064392 | tf_op jit(solution)/shard_map/ppermute | solution.py:351
  40.2 14.7 %shard_map.123 = (bf16[16,4096]{1,0:T(8,128)(2,1)S(1)}, bf16[16,4096]{1,0:T(8,128)(2,1)S(1)}, bf16[16,4096]{1,0:T(8,128)(2,1)S(1)}, bf16[16,4096]{1,0:T(8,128)(2,1)S(1)}) custom-call(s32[1,1,384]{2,1,0:T(1,128)} %refs_3_.3, s32[1,1,384]{2,1,0:T(1,128)} %refs_4_.6, s32[1,1,384]{2,1,0:T(1,128)} %refs_5_.3, ...), custom_call_target="tpu_custom_call" | custom-call | flops 24159191040 | bytes 38965760 | tf_op jit(solution)/shard_map/pallas_call | solution.py:145
  54.9 0.0 collective-permute-done.13.refs_10_
  54.9 0.6 collective-permute-start.14
  55.5 0.3 collective-permute-start.9
  55.8 0.2 collective-permute-start.10
  56.0 3.9 %collective-permute-start.11 = (bf16[16,4096]{1,0:T(8,128)(2,1)S(1)}, bf16[16,4096]{1,0:T(8,128)(2,1)S(1)}, u32[]{:S(2)}, u32[]{:S(2)}) collective-permute-start(bf16[16,4096]{1,0:T(8,128)(2,1)S(1)} %get-tuple-element.44), channel_id=1, source_target_pairs={{0,12},{4,8},{8,4},{12,0},{1,13},{5,9},{9,5},{13,1},{2,14},{6,10},... | collective-permute-start | bytes 393224 | tf_op jit(solution)/shard_map/ppermute | solution.py:351
  59.9 0.0 collective-permute-done.14.refs_11_
  59.9 13.4 %shard_map.124 = (bf16[1,1,384,128,128]{4,3,2,1,0:T(8,128)(2,1)}, bf16[1,1,384,128,128]{4,3,2,1,0:T(8,128)(2,1)}, bf16[1,1,384,128,128]{4,3,2,1,0:T(8,128)(2,1)}) custom-call(s32[1,1,384]{2,1,0:T(1,128)} %refs_3_.3, s32[1,1,384]{2,1,0:T(1,128)} %refs_4_.6, s32[1,1,384]{2,1,0:T(1,128)} %refs_5_.3, s32[1,1,384]{2,1,0:T(1,128)} %refs_3_.3, ...), custom_call_target="tpu_custom_call" | custom-call | flops 96636764160 | bytes 42624000 | tf_op jit(solution)/shard_map/pallas_call | solution.py:145
  73.3 0.0 collective-permute-done.9
  73.3 0.7 add_convert_fusion
  (9 shorter events, 0.0 us)
Async XLA Ops:
  0.6 21.0 %copy-start = (bf16[8,4096]{1,0:T(8,128)(2,1)S(1)}, bf16[8,4096]{1,0:T(8,128)(2,1)}, u32[]{:S(2)}) copy-start(bf16[8,4096]{1,0:T(8,128)(2,1)} %refs_0_.6) | copy-start | bytes 196612
  0.6 21.0 %copy-start.1 = (bf16[8,4096]{1,0:T(8,128)(2,1)S(1)}, bf16[8,4096]{1,0:T(8,128)(2,1)}, u32[]{:S(2)}) copy-start(bf16[8,4096]{1,0:T(8,128)(2,1)} %refs_4_.4) | copy-start | bytes 196612
  0.7 10.1 %collective-permute-start.2 = (bf16[8,4096]{1,0:T(8,128)(2,1)}, bf16[8,4096]{1,0:T(8,128)(2,1)S(1)}, u32[]{:S(2)}, u32[]{:S(2)}) collective-permute-start(bf16[8,4096]{1,0:T(8,128)(2,1)} %refs_0_.6), channel_id=1, source_target_pairs={{0,12},{4,8},{8,4},{12,0},{1,13},{5,9},{9,5},{13,1},{2,14},{6,10},... | collective-permute-start | bytes 196616 | tf_op jit(solution)/shard_map/ppermute | solution.py:351
  5.8 7.0 %collective-permute-start.1 = (bf16[8,4096]{1,0:T(8,128)(2,1)}, bf16[8,4096]{1,0:T(8,128)(2,1)S(1)}, u32[]{:S(2)}, u32[]{:S(2)}) collective-permute-start(bf16[8,4096]{1,0:T(8,128)(2,1)} %refs_0_.6), channel_id=1, source_target_pairs={{0,8},{4,12},{8,0},{12,4},{1,9},{5,13},{9,1},{13,5},{2,10},{6,14},... | collective-permute-start | bytes 196616 | tf_op jit(solution)/shard_map/ppermute | solution.py:351
  5.8 7.0 %collective-permute-start = (bf16[8,4096]{1,0:T(8,128)(2,1)}, bf16[8,4096]{1,0:T(8,128)(2,1)S(1)}, u32[]{:S(2)}, u32[]{:S(2)}) collective-permute-start(bf16[8,4096]{1,0:T(8,128)(2,1)} %refs_0_.6), channel_id=1, source_target_pairs={{0,4},{4,0},{8,12},{12,8},{1,5},{5,1},{9,13},{13,9},{2,6},{6,2},{1... | collective-permute-start | bytes 196616 | tf_op jit(solution)/shard_map/ppermute | solution.py:351
  6.4 15.2 %collective-permute-start.5 = (bf16[8,4096]{1,0:T(8,128)(2,1)}, bf16[8,4096]{1,0:T(8,128)(2,1)S(1)}, u32[]{:S(2)}, u32[]{:S(2)}) collective-permute-start(bf16[8,4096]{1,0:T(8,128)(2,1)} %refs_4_.4), channel_id=1, source_target_pairs={{0,8},{4,12},{8,0},{12,4},{1,9},{5,13},{9,1},{13,5},{2,10},{6,14},... | collective-permute-start | bytes 196616 | tf_op jit(solution)/shard_map/ppermute | solution.py:351
  8.7 12.9 %collective-permute-start.4 = (bf16[8,4096]{1,0:T(8,128)(2,1)}, bf16[8,4096]{1,0:T(8,128)(2,1)S(1)}, u32[]{:S(2)}, u32[]{:S(2)}) collective-permute-start(bf16[8,4096]{1,0:T(8,128)(2,1)} %refs_4_.4), channel_id=1, source_target_pairs={{0,4},{4,0},{8,12},{12,8},{1,5},{5,1},{9,13},{13,9},{2,6},{6,2},{1... | collective-permute-start | bytes 196616 | tf_op jit(solution)/shard_map/ppermute | solution.py:351
  10.7 10.9 %collective-permute-start.6 = (bf16[8,4096]{1,0:T(8,128)(2,1)}, bf16[8,4096]{1,0:T(8,128)(2,1)S(1)}, u32[]{:S(2)}, u32[]{:S(2)}) collective-permute-start(bf16[8,4096]{1,0:T(8,128)(2,1)} %refs_4_.4), channel_id=1, source_target_pairs={{0,12},{4,8},{8,4},{12,0},{1,13},{5,9},{9,5},{13,1},{2,14},{6,10},... | collective-permute-start | bytes 196616 | tf_op jit(solution)/shard_map/ppermute | solution.py:351
  21.5 13.1 %collective-permute-start.3 = (bf16[2,28,32,128]{3,2,1,0:T(8,128)(2,1)S(1)}, bf16[2,28,32,128]{3,2,1,0:T(8,128)(2,1)S(1)}, u32[]{:S(2)}, u32[]{:S(2)}) collective-permute-start(bf16[2,28,32,128]{3,2,1,0:T(8,128)(2,1)S(1)} %shard_map.119.refs_0_), channel_id=1, source_target_pairs={{0,16},{16,0},{1,17},{17,1},{2,18},{18,2},{3,19},{19,3},{4,20},{20... | collective-permute-start | bytes 1376264 | tf_op jit(solution)/shard_map/ppermute | solution.py:351
  21.7 16.4 %collective-permute-start.8 = (bf16[65,32,128]{2,1,0:T(8,128)(2,1)S(1)}, bf16[65,32,128]{2,1,0:T(8,128)(2,1)S(1)}, u32[]{:S(2)}, u32[]{:S(2)}) collective-permute-start(bf16[65,32,128]{2,1,0:T(8,128)(2,1)S(1)} %shard_map.120.refs_1_.refs_4_.refs_6_), channel_id=1, source_target_pairs={{0,2},{1,3},{2,0},{3,1},{4,6},{5,7},{6,4},{7,5},{8,10},{9,11},{10,... | collective-permute-start | bytes 1597448 | tf_op jit(solution)/shard_map/ppermute | solution.py:351
  29.9 8.1 %collective-permute-start.7 = (bf16[28,32,128]{2,1,0:T(8,128)(2,1)S(1)}, bf16[28,32,128]{2,1,0:T(8,128)(2,1)S(1)}, u32[]{:S(2)}, u32[]{:S(2)}) collective-permute-start(bf16[28,32,128]{2,1,0:T(8,128)(2,1)S(1)} %shard_map.121.refs_2_), channel_id=1, source_target_pairs={{0,16},{16,0},{1,17},{17,1},{2,18},{18,2},{3,19},{19,3},{4,20},{20... | collective-permute-start | bytes 688136 | tf_op jit(solution)/shard_map/ppermute | solution.py:351
  38.5 16.4 %collective-permute-start.13 = (bf16[84,32,128]{2,1,0:T(8,128)(2,1)S(1)}, bf16[84,32,128]{2,1,0:T(8,128)(2,1)S(1)}, u32[]{:S(2)}, u32[]{:S(2)}) collective-permute-start(bf16[84,32,128]{2,1,0:T(8,128)(2,1)S(1)} %get-tuple-element.40.refs_3_.refs_9_), channel_id=1, source_target_pairs={{0,2},{1,3},{2,0},{3,1},{4,6},{5,7},{6,4},{7,5},{8,10},{9,11},{10,... | collective-permute-start | bytes 2064392 | tf_op jit(solution)/shard_map/ppermute | solution.py:351
  40.2 19.7 %collective-permute-start.12 = (bf16[212,32,128]{2,1,0:T(8,128)(2,1)S(1)}, bf16[212,32,128]{2,1,0:T(8,128)(2,1)S(1)}, u32[]{:S(2)}, u32[]{:S(2)}) collective-permute-start(bf16[212,32,128]{2,1,0:T(8,128)(2,1)S(1)} %get-tuple-element.45), channel_id=1, source_target_pairs={{0,1},{1,0},{2,3},{3,2},{4,5},{5,4},{6,7},{7,6},{8,9},{9,8},{10,11... | collective-permute-start | bytes 5210120 | tf_op jit(solution)/shard_map/ppermute | solution.py:351
  54.9 5.0 %collective-permute-start.14 = (bf16[84,32,128]{2,1,0:T(8,128)(2,1)S(1)}, bf16[84,32,128]{2,1,0:T(8,128)(2,1)S(1)}, u32[]{:S(2)}, u32[]{:S(2)}) collective-permute-start(bf16[84,32,128]{2,1,0:T(8,128)(2,1)S(1)} %collective-permute-done.13.refs_10_), channel_id=1, source_target_pairs={{0,1},{1,0},{2,3},{3,2},{4,5},{5,4},{6,7},{7,6},{8,9},{9,8},{10,11... | collective-permute-start | bytes 2064392 | tf_op jit(solution)/shard_map/ppermute | solution.py:351
  55.5 17.8 %collective-permute-start.9 = (bf16[16,4096]{1,0:T(8,128)(2,1)S(1)}, bf16[16,4096]{1,0:T(8,128)(2,1)S(1)}, u32[]{:S(2)}, u32[]{:S(2)}) collective-permute-start(bf16[16,4096]{1,0:T(8,128)(2,1)S(1)} %get-tuple-element.42), channel_id=1, source_target_pairs={{0,4},{4,0},{8,12},{12,8},{1,5},{5,1},{9,13},{13,9},{2,6},{6,2},{1... | collective-permute-start | bytes 393224 | tf_op jit(solution)/shard_map/ppermute | solution.py:351
  55.8 17.5 %collective-permute-start.10 = (bf16[16,4096]{1,0:T(8,128)(2,1)S(1)}, bf16[16,4096]{1,0:T(8,128)(2,1)S(1)}, u32[]{:S(2)}, u32[]{:S(2)}) collective-permute-start(bf16[16,4096]{1,0:T(8,128)(2,1)S(1)} %get-tuple-element.43), channel_id=1, source_target_pairs={{0,8},{4,12},{8,0},{12,4},{1,9},{5,13},{9,1},{13,5},{2,10},{6,14},... | collective-permute-start | bytes 393224 | tf_op jit(solution)/shard_map/ppermute | solution.py:351
  56.0 17.3 %collective-permute-start.11 = (bf16[16,4096]{1,0:T(8,128)(2,1)S(1)}, bf16[16,4096]{1,0:T(8,128)(2,1)S(1)}, u32[]{:S(2)}, u32[]{:S(2)}) collective-permute-start(bf16[16,4096]{1,0:T(8,128)(2,1)S(1)} %get-tuple-element.44), channel_id=1, source_target_pairs={{0,12},{4,8},{8,4},{12,0},{1,13},{5,9},{9,5},{13,1},{2,14},{6,10},... | collective-permute-start | bytes 393224 | tf_op jit(solution)/shard_map/ppermute | solution.py:351

commit v8 on v7

--- a/solution.py
+++ b/solution.py
@@ -59,7 +59,7 @@
             body(step * slots + slot)
 
 
-def over_turned_slots(held, turned, steps, copies, body):
+def over_turned_slots(held, turned, steps, copies, body, filled=None):
     assert steps % 2 == 0
     slots = held[0].shape[0] // steps
 
@@ -78,10 +78,8 @@
             step = 2 * pair + half
             later = jnp.minimum(step + 1, steps - 1)
 
-            @pl.when(step + 1 < steps)
-            def _():
-                for copy in copies(later):
-                    copy.wait()
+            for copy, stop in zip(copies(later), filled or [steps] * len(held)):
+                pl.when(step + 1 < stop)(copy.wait)
 
             for slot in range(slots):
                 body(step * slots + slot, [targets[half].at[slot] for targets in turned])
@@ -239,45 +237,64 @@
     return [sum(part[which, col].astype(jnp.float32) for part in parts) for which in (0, 1)]
 
 
-def hidden_kernel(col_count, summands, row_arrays, row_blocks, *refs):
+def hidden_kernel(col_count, *refs):
+    *parts, out = refs
+    for col in range(col_count):
+        gate_sum, up_sum = gate_and_up(parts, col)
+        out[col] = (gate_sum * jax.nn.sigmoid(gate_sum) * up_sum).astype(out.dtype)
+
+
+def act_grads_kernel(col_count, summands, row_arrays, row_blocks, *refs):
     parts, backs = refs[:summands], refs[summands : 2 * summands]
-    rows = refs[2 * summands : 2 * summands + row_arrays]
-    acts, *packs = refs[2 * summands + row_arrays :]
+    hidden = refs[2 * summands]
+    rows = refs[2 * summands + 1 : 2 * summands + 1 + row_arrays]
+    acts, *packs = refs[2 * summands + 1 + row_arrays :]
     for col in range(col_count):
         gate_sum, up_sum = gate_and_up(parts, col)
         grad = sum(back[col].astype(jnp.float32) for back in backs)
         sigmoid = jax.nn.sigmoid(gate_sum)
         silu_gate = gate_sum * sigmoid
-        acts[col] = (silu_gate * up_sum).astype(acts.dtype)
-        acts[col_count + col] = (
-            grad * up_sum * sigmoid * (1.0 + gate_sum * (1.0 - sigmoid))
-        ).astype(acts.dtype)
-        acts[2 * col_count + col] = (grad * silu_gate).astype(acts.dtype)
+        acts[col] = (grad * up_sum * sigmoid * (1.0 + gate_sum * (1.0 - sigmoid))).astype(
+            acts.dtype
+        )
+        acts[col_count + col] = (grad * silu_gate).astype(acts.dtype)
     for pack in packs:
+        first = len(rows) * row_blocks
         for place_of, held in enumerate(rows):
             pack[place_of * row_blocks : (place_of + 1) * row_blocks] = held[:row_blocks]
-        pack[len(rows) * row_blocks :] = acts[...]
-
-
-def model_kernel(grid, arrive, gate_ids, up_ids, down_ids, acts, gate, up, down, *refs):
+        pack[first : first + col_count] = hidden[...]
+        pack[first + col_count :] = acts[...]
+
+
+def model_kernel(grid, arrive, gate_ids, up_ids, down_ids, *refs):
     row_count, col_count = grid
+    lists, (hidden, acts, gate, up, down) = refs[:3], refs[3:8]
+    refs = refs[8:]
     *outs, y_sum, x_sum, gate_near, gate_far, up_near, up_far = refs[:-4]
     gate_held, up_held, down_held, sems = refs[-4:]
     copies = streams((gate, up, down), (gate_held, up_held, down_held), sems)
-    start_all(copies, sems.shape[1])
+    steps = sems.shape[1]
+    for copy in copies(0):
+        copy.start()
     zero(y_sum)
     zero(x_sum)
     arrive()
+    filled = [filled_steps(ids, grid, steps, 1) for ids in lists]
+
+    @pl.loop(1, steps)
+    def _(step):
+        for copy, stop in zip(copies(step), filled):
+            pl.when(step < stop)(copy.start)
 
     def body(slot, turned):
-        for ids, blocks, which in ((gate_ids, turned[0], 1), (up_ids, turned[1], 2)):
+        for ids, blocks, which in ((gate_ids, turned[0], 0), (up_ids, turned[1], 1)):
             row, col = place(ids[0, 0, slot], *grid)
             x_sum[row] += product(acts[which * col_count + col], blocks[...])
         row, col = place(down_ids[0, 0, slot], *grid)
-        y_sum[row] += product(acts[col], down_held[slot])
+        y_sum[row] += product(hidden[col], down_held[slot])
 
     halves = ((gate_near, gate_far), (up_near, up_far))
-    over_turned_slots((gate_held, up_held), halves, sems.shape[1], copies, body)
+    over_turned_slots((gate_held, up_held), halves, steps, copies, body, filled)
     height = outs[0].shape[0] // 2
     for piece, out in enumerate(outs):
         tokens = slice(piece * height, (piece + 1) * height)
@@ -287,7 +304,7 @@
             out[height:, columns] = x_sum[row, tokens].astype(out.dtype)
 
 
-def grads_kernel(grid, rows, acts, arrive, gate_ids, up_ids, down_ids, *refs):
+def grads_kernel(grid, rows, hiddens, acts, arrive, gate_ids, up_ids, down_ids, *refs):
     lists, refs = refs[:3], refs[3:]
     row_count, col_count = grid
     gate_out, up_out, down_out, x, g, hidden, gate_act, up_act = refs[-13:-5]
@@ -318,9 +335,9 @@
     zero(x.at[row_count])
     zero(g.at[row_count])
     for col in range(col_count):
-        hidden[col] = joined(acts, col).T
-        gate_act[col] = joined(acts, col_count + col)
-        up_act[col] = joined(acts, 2 * col_count + col)
+        hidden[col] = joined(hiddens, col).T
+        gate_act[col] = joined(acts, col)
+        up_act[col] = joined(acts, col_count + col)
     matrices = (
         (gate_ids, x, gate_act, gate_buf),
         (up_ids, x, up_act, up_buf),
@@ -426,43 +443,66 @@
     )
     gate_up_parts = gathered(gate_up, "dp")
     gate_up_parts, _ = lax.optimization_barrier((gate_up_parts, back))
-    back_parts, far_rows = lax.optimization_barrier((gathered(back, "dp"), far_rows))
-    acts_shape = shape((3 * col_count, group, block), bf16)
-    row_blocks = 2 * row_count
-    pack_shape = shape((2 * row_blocks + 3 * col_count, group, block), bf16)
-    acts, *pack = call(
-        functools.partial(hidden_kernel, col_count, len(back_parts), 2 * packed, row_blocks),
-        [acts_shape, pack_shape] if packed else [acts_shape],
-        [*gate_up_parts, *back_parts, *([rows, far_rows] if packed else [])],
+    hidden = call(
+        functools.partial(hidden_kernel, col_count),
+        shape((col_count, group, block), bf16),
+        gate_up_parts,
         0,
         [],
         8,
         1,
     )
+    far_hidden = across(hidden, 2) if packed else None
+    back_parts, far_rows, hidden = lax.optimization_barrier(
+        (gathered(back, "dp"), far_rows, hidden)
+    )
+    acts_shape = shape((2 * col_count, group, block), bf16)
+    row_blocks = 2 * row_count
+    pack_shape = shape((2 * row_blocks + 3 * col_count, group, block), bf16)
+    acts, *pack = call(
+        functools.partial(act_grads_kernel, col_count, len(back_parts), 2 * packed, row_blocks),
+        [acts_shape, pack_shape] if packed else [acts_shape],
+        [*gate_up_parts, *back_parts, hidden, *([rows, far_rows] if packed else [])],
+        0,
+        [],
+        8,
+        1,
+    )
     far_acts = across(acts, 2) if packed else None
     pieces = call(
         functools.partial(model_kernel, grid),
         [shape((2 * height, row_count * block), bf16)] * tile,
-        [gate_ids, up_ids, down_ids, acts, gate_blocks, up_blocks, down_blocks],
+        [
+            *[gate_ids, up_ids, down_ids] * 2,
+            hidden,
+            acts,
+            gate_blocks,
+            up_blocks,
+            down_blocks,
+        ],
         3,
         [pltpu.VMEM((row_count + 1, group, block), f32)] * 2
         + [*turned_scratch(gate_blocks, 2), *stream_scratch(gate_blocks, 3, 2)],
         48,
         3 * step_flops,
+        fetched=3,
     )
     if packed:
-        _, far_acts = lax.optimization_barrier((pieces, far_acts))
-        arrays = [rows, far_rows, across(pack[0], 1), acts, far_acts, across(far_acts, 1)]
+        _, far_hidden, far_acts = lax.optimization_barrier((pieces, far_hidden, far_acts))
+        arrays = [rows, far_rows, across(pack[0], 1), hidden, far_hidden, across(far_hidden, 1)]
+        arrays += [acts, far_acts, across(far_acts, 1)]
         rows_at = ((0, 0), (1, 0), (2, 0), (2, row_blocks))
-        acts_at = ((3, 0), (4, 0), (2, 2 * row_blocks), (5, 0))
+        hidden_at = ((3, 0), (4, 0), (2, 2 * row_blocks), (5, 0))
+        acts_at = ((6, 0), (7, 0), (2, 2 * row_blocks + col_count), (8, 0))
     else:
-        arrays = gathered(rows, "replica") + gathered(acts, "replica")
-        rows_at = tuple((i, 0) for i in range(groups))
-        acts_at = tuple((groups + i, 0) for i in range(groups))
+        arrays = [piece for whole in (rows, hidden, acts) for piece in gathered(whole, "replica")]
+        rows_at, hidden_at, acts_at = (
+            tuple((first * groups + i, 0) for i in range(groups)) for first in range(3)
+        )
     total = group * groups
     slots = divisor_up_to(slot_count, SLOTS_PER_STEP)
     grads = call(
-        functools.partial(grads_kernel, grid, rows_at, acts_at),
+        functools.partial(grads_kernel, grid, rows_at, hidden_at, acts_at),
         [shape(gate_blocks.shape, bf16)] * 3,
         [gate_ids, up_ids, down_ids, gate_ids, up_ids, down_ids, *arrays],
         3,

time: 73.9 us -> 76.3 us (1.032)
  starting transfers between devices: 22.5 us -> 25.3 us
    ppermute x15 -> x17, starting transfers between devices: 22.5 us -> 25.3 us  [sent(): lax.ppermute(value, axis, [(i, target(i, size)) for i in range(size)])]
    pallas_call x6 -> x7, Pallas kernels: 43.9 us -> 43.4 us  [call(): pl.pallas_call(kernel, out_shape=out_shape, in_specs=[pl.BlockSpec(memory...]
    ppermute x15 -> x17, waiting for transfers between devices: 6.11 us -> 6.09 us  [sent(): lax.ppermute(value, axis, [(i, target(i, size)) for i in range(size)])]
  transfers between devices with their start and end apart: 15 -> 17, of which waited for: 2 -> 3; matrix products, arithmetic and copies ran while one was open for 0% -> 0% of each run, Pallas kernels for 59% -> 57%
where the time goes in v8:
time: 76.3 us; the launch traced here: 76.2 us
  Pallas kernels  43.4 us (57%)
  starting transfers between devices  25.3 us (33%)
  waiting for transfers between devices  6.09 us (8%)
  between operations  0.77 us (1%)
    pallas_call x7, Pallas kernels, call(): pl.pallas_call(kernel, out_shape=out_shape, in_specs=[pl.BlockSpec(memory...  43.4 us
    ppermute x17, starting transfers between devices, sent(): lax.ppermute(value, axis, [(i, target(i, size)) for i in range(size)])  25.3 us
    ppermute x17, waiting for transfers between devices, sent(): lax.ppermute(value, axis, [(i, target(i, size)) for i in range(size)])  6.09 us
  transfers between devices with their start and end apart: 17, of which 3 were waited for; matrix products, arithmetic and copies ran while one was open for 0% of the time, Pallas kernels for 57%

profile of v8, /device:TPU:0, one launch (start us, length us, event | category | flops | bytes accessed | tf_op | source)
XLA Modules:
  0.0 76.2 jit_solution(9163842469690647425)
XLA Ops:
  0.7 5.1 %collective-permute-start.2 = (bf16[8,4096]{1,0:T(8,128)(2,1)}, bf16[8,4096]{1,0:T(8,128)(2,1)S(1)}, u32[]{:S(2)}, u32[]{:S(2)}) collective-permute-start(bf16[8,4096]{1,0:T(8,128)(2,1)} %refs_0_.6), channel_id=1, source_target_pairs={{0,12},{4,8},{8,4},{12,0},{1,13},{5,9},{9,5},{13,1},{2,14},{6,10},... | collective-permute-start | bytes 196616 | tf_op jit(solution)/shard_map/ppermute | solution.py:368
  5.8 0.6 collective-permute-start
  6.4 2.3 %collective-permute-start.4 = (bf16[8,4096]{1,0:T(8,128)(2,1)}, bf16[8,4096]{1,0:T(8,128)(2,1)S(1)}, u32[]{:S(2)}, u32[]{:S(2)}) collective-permute-start(bf16[8,4096]{1,0:T(8,128)(2,1)} %refs_4_.4), channel_id=1, source_target_pairs={{0,8},{4,12},{8,0},{12,4},{1,9},{5,13},{9,1},{13,5},{2,10},{6,14},... | collective-permute-start | bytes 196616 | tf_op jit(solution)/shard_map/ppermute | solution.py:368
  8.7 2.0 %collective-permute-start.3 = (bf16[8,4096]{1,0:T(8,128)(2,1)}, bf16[8,4096]{1,0:T(8,128)(2,1)S(1)}, u32[]{:S(2)}, u32[]{:S(2)}) collective-permute-start(bf16[8,4096]{1,0:T(8,128)(2,1)} %refs_4_.4), channel_id=1, source_target_pairs={{0,4},{4,0},{8,12},{12,8},{1,5},{5,1},{9,13},{13,9},{2,6},{6,2},{1... | collective-permute-start | bytes 196616 | tf_op jit(solution)/shard_map/ppermute | solution.py:368
  10.7 0.0 collective-permute-done.2.refs_7_.refs_3_
  10.7 2.0 %collective-permute-start.5 = (bf16[8,4096]{1,0:T(8,128)(2,1)}, bf16[8,4096]{1,0:T(8,128)(2,1)S(1)}, u32[]{:S(2)}, u32[]{:S(2)}) collective-permute-start(bf16[8,4096]{1,0:T(8,128)(2,1)} %refs_4_.4), channel_id=1, source_target_pairs={{0,12},{4,8},{8,4},{12,0},{1,13},{5,9},{9,5},{13,1},{2,14},{6,10},... | collective-permute-start | bytes 196616 | tf_op jit(solution)/shard_map/ppermute | solution.py:368
  12.8 0.0 collective-permute-done.1.refs_6_.refs_2_
  12.8 6.7 %shard_map.119.refs_0_ = bf16[2,28,32,128]{3,2,1,0:T(8,128)(2,1)S(1)} custom-call(s32[1,1,384]{2,1,0:T(1,128)} %refs_3_.5, s32[1,1,384]{2,1,0:T(1,128)} %refs_4_.6, s32[1,1,384]{2,1,0:T(1,128)} %refs_3_.5, s32[1,1,384]{2,1,0:T(1,128)} %refs_4_.6, bf16[8,4096]{1,0:T(8,128)(2,1)} %refs_0_.6, bf16[8,4096]{1,0:T(8,128)(2,1)S(1)} %collective-permute-done.refs_5_.refs_1_, ...), custom_call_target="tpu_custom_call" | custom-call | flops 16106127360 | bytes 25892864 | tf_op jit(solution)/shard_map/pallas_call | solution.py:143
  19.5 4.8 %collective-permute-start.8 = (bf16[2,28,32,128]{3,2,1,0:T(8,128)(2,1)S(1)}, bf16[2,28,32,128]{3,2,1,0:T(8,128)(2,1)S(1)}, u32[]{:S(2)}, u32[]{:S(2)}) collective-permute-start(bf16[2,28,32,128]{3,2,1,0:T(8,128)(2,1)S(1)} %shard_map.119.refs_0_), channel_id=1, source_target_pairs={{0,16},{16,0},{1,17},{17,1},{2,18},{18,2},{3,19},{19,3},{4,20},{20... | collective-permute-start | bytes 1376264 | tf_op jit(solution)/shard_map/ppermute | solution.py:368
  24.3 0.0 collective-permute-done.4.refs_6_
  24.3 0.0 collective-permute-done.3.refs_5_
  24.3 0.1 shard_map.120.refs_1_.refs_5_.refs_6_
  24.4 1.6 %collective-permute-start.7 = (bf16[65,32,128]{2,1,0:T(8,128)(2,1)S(1)}, bf16[65,32,128]{2,1,0:T(8,128)(2,1)S(1)}, u32[]{:S(2)}, u32[]{:S(2)}) collective-permute-start(bf16[65,32,128]{2,1,0:T(8,128)(2,1)S(1)} %shard_map.120.refs_1_.refs_5_.refs_6_), channel_id=1, source_target_pairs={{0,2},{1,3},{2,0},{3,1},{4,6},{5,7},{6,4},{7,5},{8,10},{9,11},{10,... | collective-permute-start | bytes 1597448 | tf_op jit(solution)/shard_map/ppermute | solution.py:368
  26.0 6.8 %shard_map.121.refs_2_ = bf16[28,32,128]{2,1,0:T(8,128)(2,1)S(1)} custom-call(s32[1,1,384]{2,1,0:T(1,128)} %refs_5_.3, bf16[65,32,128]{2,1,0:T(8,128)(2,1)S(1)} %shard_map.120.refs_1_.refs_5_.refs_6_, bf16[1,1,384,128,128]{4,3,2,1,0:T(8,128)(2,1)} %refs_10_.1), custom_call_target="tpu_custom_call" | custom-call | flops 8053063680 | bytes 13346304 | tf_op jit(solution)/shard_map/pallas_call | solution.py:143
  32.9 0.1 collective-permute-start.6
  32.9 2.1 %collective-permute-done.8.refs_1_ = bf16[2,28,32,128]{3,2,1,0:T(8,128)(2,1)S(1)} collective-permute-done((bf16[2,28,32,128]{3,2,1,0:T(8,128)(2,1)S(1)}, bf16[2,28,32,128]{3,2,1,0:T(8,128)(2,1)S(1)}, u32[]{:S(2)}, u32[]{:S(2)}) %collective-permute-start.8) | collective-permute-done | bytes 458784 | tf_op jit(solution)/shard_map/ppermute | solution.py:368
  35.1 0.2 shard_map.122.refs_4_.refs_6_.refs_9_
  35.2 1.8 %collective-permute-start.13 = (bf16[28,32,128]{2,1,0:T(8,128)(2,1)S(1)}, bf16[28,32,128]{2,1,0:T(8,128)(2,1)S(1)}, u32[]{:S(2)}, u32[]{:S(2)}) collective-permute-start(bf16[28,32,128]{2,1,0:T(8,128)(2,1)S(1)} %shard_map.122.refs_4_.refs_6_.refs_9_), channel_id=1, source_target_pairs={{0,2},{1,3},{2,0},{3,1},{4,6},{5,7},{6,4},{7,5},{8,10},{9,11},{10,... | collective-permute-start | bytes 688136 | tf_op jit(solution)/shard_map/ppermute | solution.py:368
  37.0 2.2 %collective-permute-done.6.refs_3_ = bf16[28,32,128]{2,1,0:T(8,128)(2,1)S(1)} collective-permute-done((bf16[28,32,128]{2,1,0:T(8,128)(2,1)S(1)}, bf16[28,32,128]{2,1,0:T(8,128)(2,1)S(1)}, u32[]{:S(2)}, u32[]{:S(2)}) %collective-permute-start.6) | collective-permute-done | bytes 229408 | tf_op jit(solution)/shard_map/ppermute | solution.py:368
  39.3 0.4 shard_map.123
  39.7 1.6 %collective-permute-start.14 = (bf16[56,32,128]{2,1,0:T(8,128)(2,1)S(1)}, bf16[56,32,128]{2,1,0:T(8,128)(2,1)S(1)}, u32[]{:S(2)}, u32[]{:S(2)}) collective-permute-start(bf16[56,32,128]{2,1,0:T(8,128)(2,1)S(1)} %get-tuple-element.43.refs_7_.refs_12_), channel_id=1, source_target_pairs={{0,2},{1,3},{2,0},{3,1},{4,6},{5,7},{6,4},{7,5},{8,10},{9,11},{10,... | collective-permute-start | bytes 1376264 | tf_op jit(solution)/shard_map/ppermute | solution.py:368
  41.2 0.0 collective-permute-start.12
  41.2 15.7 %shard_map.124 = (bf16[16,4096]{1,0:T(8,128)(2,1)S(1)}, bf16[16,4096]{1,0:T(8,128)(2,1)S(1)}, bf16[16,4096]{1,0:T(8,128)(2,1)S(1)}, bf16[16,4096]{1,0:T(8,128)(2,1)S(1)}) custom-call(s32[1,1,384]{2,1,0:T(1,128)} %refs_3_.5, s32[1,1,384]{2,1,0:T(1,128)} %refs_4_.6, s32[1,1,384]{2,1,0:T(1,128)} %refs_5_.3, s32[1,1,384]{2,1,0:T(1,128)} %refs_3_.5, ...), custom_call_target="tpu_custom_call" | custom-call | flops 24159191040 | bytes 38970368 | tf_op jit(solution)/shard_map/pallas_call | solution.py:143
  57.0 0.0 collective-permute-done.13.refs_10_
  57.0 0.0 collective-permute-done.14.refs_13_
  57.0 0.6 collective-permute-start.16
  57.5 0.1 collective-permute-start.15
  57.6 1.7 %collective-permute-done.15.refs_11_ = bf16[28,32,128]{2,1,0:T(8,128)(2,1)S(1)} collective-permute-done((bf16[28,32,128]{2,1,0:T(8,128)(2,1)S(1)}, bf16[28,32,128]{2,1,0:T(8,128)(2,1)S(1)}, u32[]{:S(2)}, u32[]{:S(2)}) %collective-permute-start.15) | collective-permute-done | bytes 229408 | tf_op jit(solution)/shard_map/ppermute | solution.py:368
  59.3 2.7 %collective-permute-start.11 = (bf16[16,4096]{1,0:T(8,128)(2,1)S(1)}, bf16[16,4096]{1,0:T(8,128)(2,1)S(1)}, u32[]{:S(2)}, u32[]{:S(2)}) collective-permute-start(bf16[16,4096]{1,0:T(8,128)(2,1)S(1)} %get-tuple-element.47), channel_id=1, source_target_pairs={{0,12},{4,8},{8,4},{12,0},{1,13},{5,9},{9,5},{13,1},{2,14},{6,10},... | collective-permute-start | bytes 393224 | tf_op jit(solution)/shard_map/ppermute | solution.py:368
  62.0 13.5 %shard_map.125 = (bf16[1,1,384,128,128]{4,3,2,1,0:T(8,128)(2,1)}, bf16[1,1,384,128,128]{4,3,2,1,0:T(8,128)(2,1)}, bf16[1,1,384,128,128]{4,3,2,1,0:T(8,128)(2,1)}) custom-call(s32[1,1,384]{2,1,0:T(1,128)} %refs_3_.5, s32[1,1,384]{2,1,0:T(1,128)} %refs_4_.6, s32[1,1,384]{2,1,0:T(1,128)} %refs_5_.3, s32[1,1,384]{2,1,0:T(1,128)} %refs_3_.5, ...), custom_call_target="tpu_custom_call" | custom-call | flops 96636764160 | bytes 42624000 | tf_op jit(solution)/shard_map/pallas_call | solution.py:143
  75.5 0.0 collective-permute-done.10
  75.5 0.7 add_convert_fusion
  (14 shorter events, 0.0 us)
Async XLA Ops:
  0.6 23.7 %copy-start = (bf16[8,4096]{1,0:T(8,128)(2,1)S(1)}, bf16[8,4096]{1,0:T(8,128)(2,1)}, u32[]{:S(2)}) copy-start(bf16[8,4096]{1,0:T(8,128)(2,1)} %refs_0_.6) | copy-start | bytes 196612
  0.6 23.7 %copy-start.1 = (bf16[8,4096]{1,0:T(8,128)(2,1)S(1)}, bf16[8,4096]{1,0:T(8,128)(2,1)}, u32[]{:S(2)}) copy-start(bf16[8,4096]{1,0:T(8,128)(2,1)} %refs_4_.4) | copy-start | bytes 196612
  0.7 10.1 %collective-permute-start.2 = (bf16[8,4096]{1,0:T(8,128)(2,1)}, bf16[8,4096]{1,0:T(8,128)(2,1)S(1)}, u32[]{:S(2)}, u32[]{:S(2)}) collective-permute-start(bf16[8,4096]{1,0:T(8,128)(2,1)} %refs_0_.6), channel_id=1, source_target_pairs={{0,12},{4,8},{8,4},{12,0},{1,13},{5,9},{9,5},{13,1},{2,14},{6,10},... | collective-permute-start | bytes 196616 | tf_op jit(solution)/shard_map/ppermute | solution.py:368
  5.8 7.0 %collective-permute-start.1 = (bf16[8,4096]{1,0:T(8,128)(2,1)}, bf16[8,4096]{1,0:T(8,128)(2,1)S(1)}, u32[]{:S(2)}, u32[]{:S(2)}) collective-permute-start(bf16[8,4096]{1,0:T(8,128)(2,1)} %refs_0_.6), channel_id=1, source_target_pairs={{0,8},{4,12},{8,0},{12,4},{1,9},{5,13},{9,1},{13,5},{2,10},{6,14},... | collective-permute-start | bytes 196616 | tf_op jit(solution)/shard_map/ppermute | solution.py:368
  5.8 7.0 %collective-permute-start = (bf16[8,4096]{1,0:T(8,128)(2,1)}, bf16[8,4096]{1,0:T(8,128)(2,1)S(1)}, u32[]{:S(2)}, u32[]{:S(2)}) collective-permute-start(bf16[8,4096]{1,0:T(8,128)(2,1)} %refs_0_.6), channel_id=1, source_target_pairs={{0,4},{4,0},{8,12},{12,8},{1,5},{5,1},{9,13},{13,9},{2,6},{6,2},{1... | collective-permute-start | bytes 196616 | tf_op jit(solution)/shard_map/ppermute | solution.py:368
  6.4 17.9 %collective-permute-start.4 = (bf16[8,4096]{1,0:T(8,128)(2,1)}, bf16[8,4096]{1,0:T(8,128)(2,1)S(1)}, u32[]{:S(2)}, u32[]{:S(2)}) collective-permute-start(bf16[8,4096]{1,0:T(8,128)(2,1)} %refs_4_.4), channel_id=1, source_target_pairs={{0,8},{4,12},{8,0},{12,4},{1,9},{5,13},{9,1},{13,5},{2,10},{6,14},... | collective-permute-start | bytes 196616 | tf_op jit(solution)/shard_map/ppermute | solution.py:368
  8.7 15.6 %collective-permute-start.3 = (bf16[8,4096]{1,0:T(8,128)(2,1)}, bf16[8,4096]{1,0:T(8,128)(2,1)S(1)}, u32[]{:S(2)}, u32[]{:S(2)}) collective-permute-start(bf16[8,4096]{1,0:T(8,128)(2,1)} %refs_4_.4), channel_id=1, source_target_pairs={{0,4},{4,0},{8,12},{12,8},{1,5},{5,1},{9,13},{13,9},{2,6},{6,2},{1... | collective-permute-start | bytes 196616 | tf_op jit(solution)/shard_map/ppermute | solution.py:368
  10.7 13.6 %collective-permute-start.5 = (bf16[8,4096]{1,0:T(8,128)(2,1)}, bf16[8,4096]{1,0:T(8,128)(2,1)S(1)}, u32[]{:S(2)}, u32[]{:S(2)}) collective-permute-start(bf16[8,4096]{1,0:T(8,128)(2,1)} %refs_4_.4), channel_id=1, source_target_pairs={{0,12},{4,8},{8,4},{12,0},{1,13},{5,9},{9,5},{13,1},{2,14},{6,10},... | collective-permute-start | bytes 196616 | tf_op jit(solution)/shard_map/ppermute | solution.py:368
  19.5 15.6 %collective-permute-start.8 = (bf16[2,28,32,128]{3,2,1,0:T(8,128)(2,1)S(1)}, bf16[2,28,32,128]{3,2,1,0:T(8,128)(2,1)S(1)}, u32[]{:S(2)}, u32[]{:S(2)}) collective-permute-start(bf16[2,28,32,128]{3,2,1,0:T(8,128)(2,1)S(1)} %shard_map.119.refs_0_), channel_id=1, source_target_pairs={{0,16},{16,0},{1,17},{17,1},{2,18},{18,2},{3,19},{19,3},{4,20},{20... | collective-permute-start | bytes 1376264 | tf_op jit(solution)/shard_map/ppermute | solution.py:368
  24.4 14.8 %collective-permute-start.7 = (bf16[65,32,128]{2,1,0:T(8,128)(2,1)S(1)}, bf16[65,32,128]{2,1,0:T(8,128)(2,1)S(1)}, u32[]{:S(2)}, u32[]{:S(2)}) collective-permute-start(bf16[65,32,128]{2,1,0:T(8,128)(2,1)S(1)} %shard_map.120.refs_1_.refs_5_.refs_6_), channel_id=1, source_target_pairs={{0,2},{1,3},{2,0},{3,1},{4,6},{5,7},{6,4},{7,5},{8,10},{9,11},{10,... | collective-permute-start | bytes 1597448 | tf_op jit(solution)/shard_map/ppermute | solution.py:368
  32.9 6.4 %collective-permute-start.6 = (bf16[28,32,128]{2,1,0:T(8,128)(2,1)S(1)}, bf16[28,32,128]{2,1,0:T(8,128)(2,1)S(1)}, u32[]{:S(2)}, u32[]{:S(2)}) collective-permute-start(bf16[28,32,128]{2,1,0:T(8,128)(2,1)S(1)} %shard_map.121.refs_2_), channel_id=1, source_target_pairs={{0,16},{16,0},{1,17},{17,1},{2,18},{18,2},{3,19},{19,3},{4,20},{20... | collective-permute-start | bytes 688136 | tf_op jit(solution)/shard_map/ppermute | solution.py:368
  35.2 21.7 %collective-permute-start.13 = (bf16[28,32,128]{2,1,0:T(8,128)(2,1)S(1)}, bf16[28,32,128]{2,1,0:T(8,128)(2,1)S(1)}, u32[]{:S(2)}, u32[]{:S(2)}) collective-permute-start(bf16[28,32,128]{2,1,0:T(8,128)(2,1)S(1)} %shard_map.122.refs_4_.refs_6_.refs_9_), channel_id=1, source_target_pairs={{0,2},{1,3},{2,0},{3,1},{4,6},{5,7},{6,4},{7,5},{8,10},{9,11},{10,... | collective-permute-start | bytes 688136 | tf_op jit(solution)/shard_map/ppermute | solution.py:368
  39.7 17.3 %collective-permute-start.14 = (bf16[56,32,128]{2,1,0:T(8,128)(2,1)S(1)}, bf16[56,32,128]{2,1,0:T(8,128)(2,1)S(1)}, u32[]{:S(2)}, u32[]{:S(2)}) collective-permute-start(bf16[56,32,128]{2,1,0:T(8,128)(2,1)S(1)} %get-tuple-element.43.refs_7_.refs_12_), channel_id=1, source_target_pairs={{0,2},{1,3},{2,0},{3,1},{4,6},{5,7},{6,4},{7,5},{8,10},{9,11},{10,... | collective-permute-start | bytes 1376264 | tf_op jit(solution)/shard_map/ppermute | solution.py:368
  41.2 20.8 %collective-permute-start.12 = (bf16[212,32,128]{2,1,0:T(8,128)(2,1)S(1)}, bf16[212,32,128]{2,1,0:T(8,128)(2,1)S(1)}, u32[]{:S(2)}, u32[]{:S(2)}) collective-permute-start(bf16[212,32,128]{2,1,0:T(8,128)(2,1)S(1)} %get-tuple-element.48), channel_id=1, source_target_pairs={{0,1},{1,0},{2,3},{3,2},{4,5},{5,4},{6,7},{7,6},{8,9},{9,8},{10,11... | collective-permute-start | bytes 5210120 | tf_op jit(solution)/shard_map/ppermute | solution.py:368
  57.0 5.0 %collective-permute-start.16 = (bf16[56,32,128]{2,1,0:T(8,128)(2,1)S(1)}, bf16[56,32,128]{2,1,0:T(8,128)(2,1)S(1)}, u32[]{:S(2)}, u32[]{:S(2)}) collective-permute-start(bf16[56,32,128]{2,1,0:T(8,128)(2,1)S(1)} %collective-permute-done.14.refs_13_), channel_id=1, source_target_pairs={{0,1},{1,0},{2,3},{3,2},{4,5},{5,4},{6,7},{7,6},{8,9},{9,8},{10,11... | collective-permute-start | bytes 1376264 | tf_op jit(solution)/shard_map/ppermute | solution.py:368
  57.5 1.8 %collective-permute-start.15 = (bf16[28,32,128]{2,1,0:T(8,128)(2,1)S(1)}, bf16[28,32,128]{2,1,0:T(8,128)(2,1)S(1)}, u32[]{:S(2)}, u32[]{:S(2)}) collective-permute-start(bf16[28,32,128]{2,1,0:T(8,128)(2,1)S(1)} %collective-permute-done.13.refs_10_), channel_id=1, source_target_pairs={{0,1},{1,0},{2,3},{3,2},{4,5},{5,4},{6,7},{7,6},{8,9},{9,8},{10,11... | collective-permute-start | bytes 688136 | tf_op jit(solution)/shard_map/ppermute | solution.py:368
  57.6 17.9 %collective-permute-start.9 = (bf16[16,4096]{1,0:T(8,128)(2,1)S(1)}, bf16[16,4096]{1,0:T(8,128)(2,1)S(1)}, u32[]{:S(2)}, u32[]{:S(2)}) collective-permute-start(bf16[16,4096]{1,0:T(8,128)(2,1)S(1)} %get-tuple-element.45), channel_id=1, source_target_pairs={{0,4},{4,0},{8,12},{12,8},{1,5},{5,1},{9,13},{13,9},{2,6},{6,2},{1... | collective-permute-start | bytes 393224 | tf_op jit(solution)/shard_map/ppermute | solution.py:368
  57.6 17.9 %collective-permute-start.10 = (bf16[16,4096]{1,0:T(8,128)(2,1)S(1)}, bf16[16,4096]{1,0:T(8,128)(2,1)S(1)}, u32[]{:S(2)}, u32[]{:S(2)}) collective-permute-start(bf16[16,4096]{1,0:T(8,128)(2,1)S(1)} %get-tuple-element.46), channel_id=1, source_target_pairs={{0,8},{4,12},{8,0},{12,4},{1,9},{5,13},{9,1},{13,5},{2,10},{6,14},... | collective-permute-start | bytes 393224 | tf_op jit(solution)/shard_map/ppermute | solution.py:368
  59.3 16.2 %collective-permute-start.11 = (bf16[16,4096]{1,0:T(8,128)(2,1)S(1)}, bf16[16,4096]{1,0:T(8,128)(2,1)S(1)}, u32[]{:S(2)}, u32[]{:S(2)}) collective-permute-start(bf16[16,4096]{1,0:T(8,128)(2,1)S(1)} %get-tuple-element.47), channel_id=1, source_target_pairs={{0,12},{4,8},{8,4},{12,0},{1,13},{5,9},{9,5},{13,1},{2,14},{6,10},... | collective-permute-start | bytes 393224 | tf_op jit(solution)/shard_map/ppermute | solution.py:368
